TPU v7x, 32 devices: a whole 2x2x4 slice. The times are simulated.
32 devices in a mesh: dp: 8 (over z, x), shard: 4 (over y, core).
Axes of the slice: x: 2, y: 2, z: 4, core: 2. Of those that a mesh axis runs over, the one named last changes fastest.
Arguments:
- inputs: bfloat16 [32, 1024, 768], P(('dp', 'shard')), may hold values from -6 to 6
- cotangent: bfloat16 [32, 1024, 768], P(('dp', 'shard')), may hold values from -6 to 6
- w_in: float32 [768, 3352], P('shard'), may hold values from -0.21875 to 0.21875
- w_out: float32 [1536, 768], P('shard'), may hold values from -0.15625 to 0.15625
- vectors: float32 [11336], P('shard'), may hold values from -7 to 3, as said below
- first_in: float32 [768, 3352], P('shard'), may hold values from -56 to 56
- second_in: float32 [768, 3352], P('shard'), may hold values from 65.536 to 655.36
- first_out: float32 [1536, 768], P('shard'), may hold values from -56 to 56
- second_out: float32 [1536, 768], P('shard'), may hold values from 65.536 to 655.36
- first_vec: float32 [11336], P('shard'), may hold values from -56 to 56
- second_vec: float32 [11336], P('shard'), may hold values from 65.536 to 655.36
Outputs:
- outputs: bfloat16 [32, 1024, 768], P(('dp', 'shard'))
- input_grad: float32 [32, 1024, 768], P(('dp', 'shard'))
- grad_in: float32 [768, 3352], P('shard')
- grad_out: float32 [1536, 768], P('shard')
- grad_vec: float32 [11336], P('shard')
- new_w_in: float32 [768, 3352], P('shard')
- new_w_out: float32 [1536, 768], P('shard')
- new_vectors: float32 [11336], P('shard')
- new_first_in: float32 [768, 3352], P('shard')
- new_second_in: float32 [768, 3352], P('shard')
- new_first_out: float32 [1536, 768], P('shard')
- new_second_out: float32 [1536, 768], P('shard')
- new_first_vec: float32 [11336], P('shard')
- new_second_vec: float32 [11336], P('shard')
Inputs may be any that keep to these rules, and one draw needn't show every extreme that they name: vectors holds conv_w, conv_b, dt_bias, a_log, d_skip, norm_w, gain in that order as in the first step; norm_w and gain are positive, a_log is nonnegative.
All inputs are finite; a program needn't handle non-finite values.
Results may differ from a plain program's by a relative error of at most 0.012.
The roundings to bfloat16 on the way count: a program that leaves them out, or rounds other values in their place, can miss the bound.
Values may be sent and summed in bfloat16 or wider, within the bound.
A program may use at most 256 MiB of HBM per device.

v0:
```python
import math

import jax
import jax.numpy as jnp
from jax import lax
from jax.sharding import PartitionSpec as P

D = 768
INNER = 1536
STATE = 128
HEADDIM = 64
CONV = 4
SPAN = 256
STEP_COUNT = 3


norm_epsilon = 1e-05
beta_first = 0.9
beta_second = 0.95
adam_epsilon = 1e-08
rate_matrix = 0.01
rate_vector = 0.1
decay_matrix = 0.1
highest = lax.Precision.HIGHEST


def layout():
    channels = INNER + 2 * STATE
    heads = INNER // HEADDIM
    return [(CONV, channels), (channels,), (heads,), (heads,), (heads,), (INNER,), (D,)]


def unpack(flat_values):
    pieces = []
    offset = 0
    for shape in layout():
        count = math.prod(shape)
        pieces.append(flat_values[offset : offset + count].reshape(shape))
        offset += count
    return pieces


def contract_rows(left, right, precision=None):
    return lax.dot_general(
        left,
        right,
        (((0,), (0,)), ((), ())),
        precision=precision,
        preferred_element_type=jnp.float32,
    )


def contract_cols(left, right, precision=None):
    return lax.dot_general(
        left,
        right,
        (((1,), (1,)), ((), ())),
        precision=precision,
        preferred_element_type=jnp.float32,
    )


def span_step(in_state, block):
    x_scaled, log_decay, b_input, q_input = block
    heads, length = log_decay.shape
    cumul = jnp.cumsum(log_decay, axis=1)
    lower = jnp.arange(length)[:, None] >= jnp.arange(length)[None, :]
    spread_log = cumul[:, :, None] - cumul[:, None, :]
    decay_mat = jnp.exp(jnp.where(lower[None, :, :], spread_log, -1000000000.0))
    scores = contract_cols(q_input, b_input, highest)
    weighted = decay_mat * scores[None, :, :]
    x_heads = x_scaled.reshape(length, heads, HEADDIM)
    within = jnp.einsum("hts,shp->thp", weighted, x_heads, precision=highest).reshape(length, INNER)
    state_flat = in_state.reshape(INNER, in_state.shape[-1])
    carried = contract_cols(q_input, state_flat, highest) * jnp.repeat(
        jnp.exp(cumul).T, HEADDIM, axis=1
    )
    to_end = jnp.exp(cumul[:, -1:] - cumul)
    moved = x_scaled * jnp.repeat(to_end.T, HEADDIM, axis=1)
    added = contract_rows(moved, b_input, highest).reshape(in_state.shape)
    out_state = in_state * jnp.exp(cumul[:, -1])[:, None, None] + added
    return (out_state, within + carried)


def mix_sequence(projected, conv_w, conv_b, dt_bias, a_log, d_skip, norm_w):
    length = projected.shape[0]
    channels = INNER + 2 * STATE
    heads = INNER // HEADDIM
    gate_part = projected[:, :INNER]
    conv_in = projected[:, INNER : INNER + channels]
    step_raw = projected[:, INNER + channels :]
    padded = jnp.pad(conv_in, ((CONV - 1, 0), (0, 0)))
    convolved = conv_b[None, :] + conv_w[0][None, :] * padded[0:length]
    for tap in range(1, CONV):
        convolved = convolved + conv_w[tap][None, :] * padded[tap : tap + length]
    activated = jax.nn.silu(convolved)
    x_flat = activated[:, :INNER]
    b_all = activated[:, INNER : INNER + STATE]
    q_all = activated[:, INNER + STATE :]
    time_step = jax.nn.softplus(step_raw + dt_bias[None, :])
    log_decay = -time_step * jnp.exp(a_log)[None, :]
    x_scaled = x_flat * jnp.repeat(time_step, HEADDIM, axis=1)
    blocks = length // SPAN
    decay_heads = log_decay.T.reshape(heads, blocks, SPAN).transpose(1, 0, 2)
    start_state = jnp.zeros((heads, HEADDIM, STATE), jnp.float32)
    final_state, results = lax.scan(
        jax.checkpoint(span_step),
        start_state,
        (
            x_scaled.reshape(blocks, SPAN, INNER),
            decay_heads,
            b_all.reshape(blocks, SPAN, STATE),
            q_all.reshape(blocks, SPAN, STATE),
        ),
    )
    scanned = results.reshape(length, INNER) + jnp.repeat(d_skip, HEADDIM)[None, :] * x_flat
    gated = scanned * jax.nn.silu(gate_part)
    factor = lax.rsqrt(jnp.mean(gated * gated, axis=-1, keepdims=True) + norm_epsilon)
    return gated * factor * norm_w[None, :]


def prenorm(values, gain_values):
    return (
        values
        * lax.rsqrt(jnp.mean(values * values, axis=-1, keepdims=True) + norm_epsilon)
        * gain_values
    )


def adam(param, grad, first, second, rate, decay):
    new_first = beta_first * first + (1.0 - beta_first) * grad
    new_second = beta_second * second + (1.0 - beta_second) * grad * grad
    fix_first = 1.0 - beta_first**STEP_COUNT
    fix_second = 1.0 - beta_second**STEP_COUNT
    update = new_first / fix_first / (jnp.sqrt(new_second / fix_second) + adam_epsilon)
    return (param - rate * (update + decay * param), new_first, new_second)


def shards(
    inputs,
    cotangent,
    w_in,
    w_out,
    vectors,
    first_in,
    second_in,
    first_out,
    second_out,
    first_vec,
    second_vec,
):
    vec_len = vectors.shape[0]
    w_in_all, w_out_all, vec_all = (
        lax.all_gather(w_in.astype(jnp.bfloat16), "shard", axis=0, tiled=True),
        lax.all_gather(w_out.astype(jnp.bfloat16), "shard", axis=0, tiled=True),
        lax.all_gather(vectors.astype(jnp.bfloat16), "shard", axis=0, tiled=True),
    )
    conv_w, conv_b, dt_bias, a_log, d_skip, norm_w, gain = unpack(vec_all)
    seqs_here, length, width = inputs.shape
    token_rows = inputs.astype(jnp.float32).reshape(seqs_here * length, width)
    normed, prenorm_back = jax.vjp(prenorm, token_rows, gain.astype(jnp.float32))
    normed_low = normed.astype(jnp.bfloat16)
    projected = jnp.dot(normed_low, w_in_all, preferred_element_type=jnp.float32)

    def mix_all(proj_values, conv_wf, conv_bf, dt_biasf, a_logf, d_skipf, norm_wf):
        shaped = proj_values.reshape(seqs_here, length, proj_values.shape[-1])
        result = jax.vmap(mix_sequence, in_axes=(0, None, None, None, None, None, None))(
            shaped, conv_wf, conv_bf, dt_biasf, a_logf, d_skipf, norm_wf
        )
        return result.reshape(seqs_here * length, INNER)

    mixer_out, mix_back = jax.vjp(
        mix_all,
        projected,
        conv_w.astype(jnp.float32),
        conv_b.astype(jnp.float32),
        dt_bias.astype(jnp.float32),
        a_log.astype(jnp.float32),
        d_skip.astype(jnp.float32),
        norm_w.astype(jnp.float32),
    )
    mixer_low = mixer_out.astype(jnp.bfloat16)
    branch = jnp.dot(mixer_low, w_out_all, preferred_element_type=jnp.float32)
    outputs = (token_rows + branch).astype(jnp.bfloat16).reshape(inputs.shape)
    cot_rows = cotangent.reshape(seqs_here * length, width)
    grad_w_out = contract_rows(mixer_low, cot_rows)
    d_mixer = contract_cols(cot_rows, w_out_all)
    d_projected, d_conv_w, d_conv_b, d_dt_bias, d_a_log, d_skip_grad, d_norm_w = mix_back(d_mixer)
    d_proj_low = d_projected.astype(jnp.bfloat16)
    grad_w_in = contract_rows(normed_low, d_proj_low)
    d_normed = contract_cols(d_proj_low, w_in_all)
    d_rows, d_gain = prenorm_back(d_normed)
    input_grad = (cot_rows.astype(jnp.float32) + d_rows).reshape(inputs.shape)
    small_grad = jnp.concatenate(
        [
            piece.reshape(-1)
            for piece in (d_conv_w, d_conv_b, d_dt_bias, d_a_log, d_skip_grad, d_norm_w, d_gain)
        ]
    )
    summed = lax.psum((grad_w_in, grad_w_out, small_grad), "dp")
    grad_in, grad_out, grad_vec = (
        lax.psum_scatter(summed[0], "shard", scatter_dimension=0, tiled=True),
        lax.psum_scatter(summed[1], "shard", scatter_dimension=0, tiled=True),
        lax.psum_scatter(summed[2], "shard", scatter_dimension=0, tiled=True),
    )
    new_w_in, new_first_in, new_second_in = adam(
        w_in, grad_in, first_in, second_in, rate_matrix, decay_matrix
    )
    new_w_out, new_first_out, new_second_out = adam(
        w_out, grad_out, first_out, second_out, rate_matrix, decay_matrix
    )
    conv_count = CONV * (INNER + 2 * STATE)
    positions = lax.axis_index("shard") * vec_len + jnp.arange(vec_len, dtype=jnp.int32)
    is_matrix = positions < conv_count
    rate = jnp.where(is_matrix, rate_matrix, rate_vector)
    decay = jnp.where(is_matrix, decay_matrix, 0.0)
    new_vectors, new_first_vec, new_second_vec = adam(
        vectors, grad_vec, first_vec, second_vec, rate, decay
    )
    return (
        outputs,
        input_grad,
        grad_in,
        grad_out,
        grad_vec,
        new_w_in,
        new_w_out,
        new_vectors,
        new_first_in,
        new_second_in,
        new_first_out,
        new_second_out,
        new_first_vec,
        new_second_vec,
    )


def solution(mesh):
    in_specs = (
        P(("dp", "shard"), None, None),
        P(("dp", "shard"), None, None),
        P("shard", None),
        P("shard", None),
        P("shard"),
        P("shard", None),
        P("shard", None),
        P("shard", None),
        P("shard", None),
        P("shard"),
        P("shard"),
    )
    out_specs = (
        P(("dp", "shard"), None, None),
        P(("dp", "shard"), None, None),
        P("shard", None),
        P("shard", None),
        P("shard"),
        P("shard", None),
        P("shard", None),
        P("shard"),
        P("shard", None),
        P("shard", None),
        P("shard", None),
        P("shard", None),
        P("shard"),
        P("shard"),
    )
    return jax.shard_map(shards, mesh=mesh, in_specs=in_specs, out_specs=out_specs, check_vma=False)
```

profile of v0, /device:TPU:0, one launch (start us, length us, event | category | flops | bytes accessed | tf_op | source)
XLA Modules:
  0.0 1124.3 jit_solution(13574905176750395918)
XLA Ops:
  14.3 13.8 %all-reduce.17 = bf16[11336]{0:T(1024)(128)(2,1)S(1)} all-reduce(bf16[11336]{0:T(1024)(128)(2,1)S(1)} %dynamic-update-slice), channel_id=1, replica_groups=mesh['dp'=8,'shard'=4] {'shard'}, use_global_device_ids=true, to_apply=%add.17 | all-reduce | flops 11336 | bytes 45344
  30.2 24.0 %all-gather.3.cloned.1.call-done = bf16[768,3352]{1,0:T(8,128)(2,1)} async-done(((bf16[192,3352]{1,0:T(8,128)(2,1)}), bf16[768,3352]{1,0:T(8,128)(2,1)}) %all-gather.3.cloned.1.call-update) | async-done | bytes 5148688 | tf_op jit(solution)/shard_map/all_gather | solution.py:154
  54.2 8.5 convolution_bitcast_fusion.5
  62.7 4.3 slice.168
  70.9 19.5 %fusion.78 = (f32[1,1024,1792]{1,2,0:T(8,128)S(1)}, f32[1,1024,1792]{1,2,0:T(8,128)}) fusion(f32[1,1024,1792]{1,2,0:T(8,128)} %slice.168, f32[1792]{0:T(1024)S(1)} %get-tuple-element.675, f32[1792]{0:T(1024)S(1)} %get-tuple-element.676, f32[1792]{0:T(1024)S(1)} %get-tuple-element.677, f32[1792]{0:T(1024)S(1)} %get-tuple-element.674, ...), kind=kLoop, calls=%fused_computation.133 | loop fusion | flops 22020096 | bytes 22055936 | tf_op jit(solution)/shard_map/jvp(vmap(jit(silu)))/mul | solution.py:96
  95.4 3.6 bitcast_multiply_fusion.7
  102.2 104.0 %while.39 = (s32[]{:T(128)}, f32[1,24,64,128]{3,2,1,0:T(8,128)}, f32[4,1,256,1536]{3,2,1,0:T(8,128)}, f32[4,1,24,64,128]{4,3,2,1,0:T(8,128)}, f32[4,1,24,256]{3,...) while((s32[]{:T(128)}, f32[1,24,64,128]{3,2,1,0:T(8,128)}, ...), condition=%wide.region_4.5_spmd.clone, body=%wide.region_1.4_spmd.clone.sunk | while | flops 2523869184 | bytes 34812440 | solution.py:106
  108.4 8.1 fusion.219
  123.7 3.6 fusion.220
  133.5 8.1 fusion.219
  150.0 3.6 fusion.220
  159.8 8.1 fusion.219
  176.3 3.6 fusion.220
  186.1 8.1 fusion.219
  202.6 3.6 fusion.220
  206.2 6.5 copy.270
  212.7 7.8 multiply_reduce_fusion.7
  223.1 4.5 fusion.109
  227.6 9.0 fusion.83
  236.7 19.2 %multiply_reduce_fusion.6 = (f32[1536]{0:T(1024)}, f32[1,1024,1536]{1,2,0:T(8,128)}, f32[1,1024,1536]{1,2,0:T(8,128)}) fusion(f32[1,1024,1792]{1,2,0:T(8,128)} %copy-done.1, f32[1,1024,3352]{1,2,0:T(8,128)} %copy-done.2, f32[1,1024,1536]{1,2,0:T(8,128)} %copy-done.5, f32[1024]{0:T(1024)S(1)} %multiply_multiply_fusion.4, f32[1024]{0:T(1024)S(1)} %fusion.128, ...), kind=kLoop, calls=%fused_computation.144 | loop fusion | flops 33028608 | bytes 44066816 | tf_op jit(solution)/shard_map/transpose(jvp(vmap()))/reduce_sum | solution.py:116
  255.9 7.0 copy.271
  268.4 513.0 %while.40 = (s32[]{:T(128)}, f32[1,24,64,128]{3,2,1,0:T(8,128)}, f32[4,1,256,1536]{2,0,3,1:T(4,128)}, f32[4,1,24,256]{3,0,2,1:T(4,128)}, f32[4,1,256,128]{2,0,3,...) while((s32[]{:T(128)}, f32[1,24,64,128]{3,2,1,0:T(8,128)}, ...), condition=%wide.region_19.20_spmd.clone, body=%wide.region_7.19_spmd.clone.sunk | while | flops 5762910208 | bytes 82753480 | solution.py:106
  299.6 3.7 fusion.241
  314.1 11.2 fusion.246
  325.3 6.3 fusion.244
  335.9 3.5 fusion.252
  345.0 7.7 copy.378
  357.6 3.9 dynamic_update_slice.70
  361.6 34.3 %dynamic_update_slice.68 = f32[4,1,256,1536]{2,0,3,1:T(4,128)} dynamic-update-slice(f32[4,1,256,1536]{2,0,3,1:T(4,128)} %get-tuple-element.916, f32[1,1,256,1536]{2,0,3,1:T(1,128)} %copy.378, s32[]{:T(128)S(6)} %sub.233, s32[]{:T(128)} %constant.162.clone.1..sunk.1, s32[]{:T(128)} %constant.162.clone.1..sunk.1, s32[]{:T(128)} %constant.162.clone.1..sunk.1) | dynamic-update-slice | bytes 3145732 | tf_op jit(solution)/shard_map/transpose(jvp(vmap()))/while/body/jit(dynamic_update_index_in_dim)/dynamic_update_slice | solution.py:106
  428.0 3.7 fusion.241
  442.5 11.2 fusion.246
  453.7 6.3 fusion.244
  464.3 3.5 fusion.252
  473.4 7.7 copy.378
  486.0 3.9 dynamic_update_slice.70
  489.9 34.3 %dynamic_update_slice.68 = f32[4,1,256,1536]{2,0,3,1:T(4,128)} dynamic-update-slice(f32[4,1,256,1536]{2,0,3,1:T(4,128)} %get-tuple-element.916, f32[1,1,256,1536]{2,0,3,1:T(1,128)} %copy.378, s32[]{:T(128)S(6)} %sub.233, s32[]{:T(128)} %constant.162.clone.1..sunk.1, s32[]{:T(128)} %constant.162.clone.1..sunk.1, s32[]{:T(128)} %constant.162.clone.1..sunk.1) | dynamic-update-slice | bytes 3145732 | tf_op jit(solution)/shard_map/transpose(jvp(vmap()))/while/body/jit(dynamic_update_index_in_dim)/dynamic_update_slice | solution.py:106
  556.3 3.7 fusion.241
  570.8 11.2 fusion.246
  582.0 6.3 fusion.244
  601.7 7.7 copy.378
  614.4 3.9 dynamic_update_slice.70
  618.3 34.3 %dynamic_update_slice.68 = f32[4,1,256,1536]{2,0,3,1:T(4,128)} dynamic-update-slice(f32[4,1,256,1536]{2,0,3,1:T(4,128)} %get-tuple-element.916, f32[1,1,256,1536]{2,0,3,1:T(1,128)} %copy.378, s32[]{:T(128)S(6)} %sub.233, s32[]{:T(128)} %constant.162.clone.1..sunk.1, s32[]{:T(128)} %constant.162.clone.1..sunk.1, s32[]{:T(128)} %constant.162.clone.1..sunk.1) | dynamic-update-slice | bytes 3145732 | tf_op jit(solution)/shard_map/transpose(jvp(vmap()))/while/body/jit(dynamic_update_index_in_dim)/dynamic_update_slice | solution.py:106
  684.7 3.7 fusion.241
  699.2 11.2 fusion.246
  710.4 6.3 fusion.244
  730.1 7.7 copy.378
  742.8 3.9 dynamic_update_slice.70
  746.7 34.3 %dynamic_update_slice.68 = f32[4,1,256,1536]{2,0,3,1:T(4,128)} dynamic-update-slice(f32[4,1,256,1536]{2,0,3,1:T(4,128)} %get-tuple-element.916, f32[1,1,256,1536]{2,0,3,1:T(1,128)} %copy.378, s32[]{:T(128)S(6)} %sub.233, s32[]{:T(128)} %constant.162.clone.1..sunk.1, s32[]{:T(128)} %constant.162.clone.1..sunk.1, s32[]{:T(128)} %constant.162.clone.1..sunk.1) | dynamic-update-slice | bytes 3145732 | tf_op jit(solution)/shard_map/transpose(jvp(vmap()))/while/body/jit(dynamic_update_index_in_dim)/dynamic_update_slice | solution.py:106
  784.9 8.3 transpose.158
  793.2 12.0 %slice_multiply_fusion = (f32[1,1024,1536]{1,2,0:T(8,128)}, f32[1,1024,1536]{1,2,0:T(8,128)}) fusion(f32[1,1024,1536]{1,2,0:T(8,128)} %transpose.158, f32[1,1024,1792]{1,2,0:T(8,128)} %copy-done.1, f32[1024,24]{0,1:T(8,128)S(1)} %copy-done.20, f32[1,1024,1536]{1,2,0:T(8,128)} %get-tuple-element.646, f32[1536]{0:T(1024)S(1)} %mul.619), kind=kLoop, calls=%fused_computation.150 | loop fusion | flops 6291456 | bytes 31561728 | tf_op jit(solution)/shard_map/transpose(jvp(vmap()))/mul | solution.py:102
  805.2 3.7 reduce_sum.216
  810.6 20.2 %multiply_reduce_fusion.4 = (f32[1792]{0:T(1024)S(1)}, f32[1792]{0:T(1024)S(1)}, f32[1792]{0:T(1024)S(1)}, f32[1792]{0:T(1024)S(1)}, f32[1792]{0:T(1024)S(1)}, /*index=5*/f32[1,1024,1792]{1,2,0:T(8,128)S(1)}) fusion(f32[1,1024,1792]{1,2,0:T(8,128)} %slice.168, f32[1,1024,3352]{1,2,0:T(8,128)} %copy-done.2, f32[1,1024,1792]{1,2,0:T(8,128)} %get-tuple-element.653, ...), kind=kLoop, calls=%fused_computation.130 | loop fusion | flops 36691200 | bytes 36736000 | tf_op jit(solution)/shard_map/transpose(jvp(vmap()))/reduce_sum | solution.py:95
  830.8 8.3 broadcast_multiply_fusion
  839.2 12.5 %pad_add_fusion = f32[1,1024,1792]{1,2,0:T(8,128)} fusion(f32[1,1024,1792]{1,2,0:T(8,128)} %get-tuple-element.667, f32[1,1024,1792]{1,2,0:T(8,128)} %get-tuple-element.668, f32[1,1024,1792]{1,2,0:T(8,128)} %get-tuple-element.669, f32[1,1024,1792]{1,2,0:T(8,128)S(1)} %get-tuple-element.666), kind=kLoop, calls=%fused_computation.125 | loop fusion | flops 5505024 | bytes 36700160 | tf_op jit(solution)/shard_map/transpose(jvp(vmap()))/add_any | solution.py:93
  851.7 15.2 %fusion.106 = f32[768,3352]{1,0:T(8,128)} fusion(bf16[1,1024,768]{2,1,0:T(8,128)(2,1)S(1)} %copy-done.13, f32[768]{0:T(1024)S(1)} %copy-done.43, f32[1024]{0:T(1024)S(1)} %copy-done.46, f32[1,1024,1536]{1,2,0:T(8,128)} %get-tuple-element.662, f32[1,1024,1792]{1,2,0:T(8,128)} %pad_add_fusion, f32[1,1024,24]{1,2,0:T(8,128)S(1)} %get-tuple-element.648), kind=kOutput, calls=%fused_computation.182 | convolution fusion | flops 5285683200 | bytes 25607168 | tf_op jit(solution)/shard_map/dot_general | solution.py:44
  868.6 83.9 %reduce-scatter.3.cloned.1.call-done = f32[192,3352]{1,0:T(8,128)} async-done(((f32[768,3352]{1,0:T(8,128)}), f32[192,3352]{1,0:T(8,128)}) %reduce-scatter.3.cloned.1.call-update) | async-done | bytes 2574352 | tf_op jit(solution)/shard_map/reduce_scatter | solution.py:202
  952.6 12.4 %fusion.94 = (f32[768]{0:T(1024)S(1)}, f32[1024]{0:T(1024)S(1)}, f32[1024,768]{1,0:T(8,128)}) fusion(bf16[1,1024,768]{2,1,0:T(8,128)(2,1)S(1)} %copy-done.13, f32[1024]{0:T(1024)S(1)} %copy-done.47, f32[768]{0:T(1024)S(1)} %copy-done.43, bf16[768,3352]{1,0:T(8,128)(2,1)} %all-gather.3.cloned.1.call-done, f32[1,1024,1536]{1,2,0:T(8,128)} %get-tuple-element.662, ...), kind=kOutput, calls=%fused_computation.167 | convolution fusion | flops 5288040448 | bytes 23611392 | tf_op jit(solution)/shard_map/dot_general | solution.py:54
  965.2 11.3 %all-reduce.18 = f32[11336]{0:T(1024)S(1)} all-reduce(f32[11336]{0:T(1024)S(1)} %concatenate.3), channel_id=4, replica_groups=mesh['dp'=8,'shard'=4] {'shard'}, use_global_device_ids=true, to_apply=%region_38.39.clone | all-reduce | flops 11336 | bytes 90688
  976.6 39.2 %psum.26 = f32[2834]{0:T(1024)S(1)} all-reduce(f32[2834]{0:T(1024)S(1)} %dynamic-slice.2), channel_id=1, replica_groups=mesh['dp'=8,'shard'=4] {'dp'}, use_global_device_ids=true, to_apply=%region_37.38 | all-reduce | flops 2834 | bytes 22672 | tf_op jit(solution)/shard_map/psum | solution.py:200
  1016.5 4.5 fusion.101
  1021.0 7.0 fusion.117
  1028.0 75.6 %all-reduce.22.cloned.1.call-done = (f32[192,3352]{1,0:T(8,128)}, f32[384,768]{1,0:T(8,128)}) async-done(((f32[192,3352]{1,0:T(8,128)}, f32[384,768]{1,0:T(8,128)}), (f32[192,3352]{1,0:T(8,128)}, f32[384,768]{1,0:T(8,128)})) %all-reduce.22.cloned.1.call-update) | async-done | bytes 3754000 | tf_op jit(solution)/shard_map/psum | solution.py:200
  1103.6 4.8 multiply_subtract_fusion.1
  1108.5 6.5 multiply_subtract_fusion
  (575 shorter events, 331.2 us)
Async XLA Ops:
  7.2 21.9 %copy-start.12 = (bf16[1,1024,768]{2,1,0:T(8,128)(2,1)S(1)}, bf16[1,1024,768]{2,1,0:T(8,128)(2,1)}, u32[]{:S(2)}) copy-start(bf16[1,1024,768]{2,1,0:T(8,128)(2,1)} %param.15) | copy-start | bytes 4718596
  7.2 47.0 %all-gather.3.cloned.1.call-start = ((), (), s32[]{:S(2)}) async-start(), calls=%async_computation.2 | async-start | bytes 6635520 | tf_op jit(solution)/shard_map/all_gather | solution.py:154
  10.3 217.3 %all-gather.5.cloned.1.call-start = ((), (), s32[]{:S(2)}) async-start(), calls=%async_computation.3 | async-start | bytes 2949120 | tf_op jit(solution)/shard_map/all_gather | solution.py:155
  12.6 856.1 %reduce-scatter.5.cloned.1.call-start = ((), (), s32[]{:S(2)}) async-start(), calls=%async_computation.5 | async-start | bytes 5898240 | tf_op jit(solution)/shard_map/reduce_scatter | solution.py:203
  28.1 34.6 %copy-start.22 = (bf16[11336]{0:T(1024)(128)(2,1)}, bf16[11336]{0:T(1024)(128)(2,1)S(1)}, u32[]{:S(2)}) copy-start(bf16[11336]{0:T(1024)(128)(2,1)S(1)} %all-reduce.17) | copy-start | bytes 68020
  28.2 38.9 %copy-start.56 = (f32[24]{0:T(128)}, f32[24]{0:T(128)S(1)}, u32[]{:S(2)}) copy-start(f32[24]{0:T(128)S(1)} %fusion.129) | copy-start | bytes 292
  28.3 38.8 %copy-start.54 = (f32[24]{0:T(128)}, f32[24]{0:T(128)S(1)}, u32[]{:S(2)}) copy-start(f32[24]{0:T(128)S(1)} %get-tuple-element.679) | copy-start | bytes 292
  28.3 34.4 %copy-start.42 = (f32[768]{0:T(1024)}, f32[768]{0:T(1024)S(1)}, u32[]{:S(2)}) copy-start(f32[768]{0:T(1024)S(1)} %slice_convert_fusion.3) | copy-start | bytes 9220
  29.5 33.2 %copy-start.45 = (f32[1024]{0:T(1024)}, f32[1024]{0:T(1024)S(1)}, u32[]{:S(2)}) copy-start(f32[1024]{0:T(1024)S(1)} %fusion.127) | copy-start | bytes 12292
  30.2 40.7 %copy-start.25 = (f32[1792]{0:T(1024)}, f32[1792]{0:T(1024)S(1)}, u32[]{:S(2)}) copy-start(f32[1792]{0:T(1024)S(1)} %get-tuple-element.674) | copy-start | bytes 21508
  30.2 40.7 %copy-start.27 = (f32[1792]{0:T(1024)}, f32[1792]{0:T(1024)S(1)}, u32[]{:S(2)}) copy-start(f32[1792]{0:T(1024)S(1)} %get-tuple-element.675) | copy-start | bytes 21508
  30.2 40.7 %copy-start.29 = (f32[1792]{0:T(1024)}, f32[1792]{0:T(1024)S(1)}, u32[]{:S(2)}) copy-start(f32[1792]{0:T(1024)S(1)} %get-tuple-element.676) | copy-start | bytes 21508
  30.2 40.7 %copy-start.31 = (f32[1792]{0:T(1024)}, f32[1792]{0:T(1024)S(1)}, u32[]{:S(2)}) copy-start(f32[1792]{0:T(1024)S(1)} %get-tuple-element.677) | copy-start | bytes 21508
  70.2 25.2 %copy-start.19 = (f32[1024,24]{0,1:T(8,128)}, f32[1024,24]{0,1:T(8,128)S(1)}, u32[]{:S(2)}) copy-start(f32[1024,24]{0,1:T(8,128)S(1)} %get-tuple-element.664) | copy-start | bytes 294916
  212.7 10.4 copy-start.17
  212.7 10.4 copy-start.39
  220.5 16.2 %copy-start.48 = (f32[1024]{0:T(1024)}, f32[1024]{0:T(1024)S(1)}, u32[]{:S(2)}) copy-start(f32[1024]{0:T(1024)S(1)} %fusion.128) | copy-start | bytes 12292
  236.7 715.8 %reduce-scatter.3.cloned.1.call-start = ((), (), s32[]{:S(2)}) async-start(), calls=%async_computation.4 | async-start | bytes 13271040 | tf_op jit(solution)/shard_map/reduce_scatter | solution.py:202
  288.8 10.8 copy-start.50
  314.1 11.2 copy-start.3
  314.1 11.2 copy-start.11
  314.1 11.2 copy-start.16
  314.1 11.2 copy-start.21
  342.9 10.1 copy-start.6
  417.2 10.8 copy-start.50
  442.4 11.2 copy-start.3
  442.4 11.2 copy-start.11
  442.5 11.2 copy-start.16
  442.5 11.2 copy-start.21
  471.3 10.1 copy-start.6
  545.5 10.8 copy-start.50
  570.8 11.2 copy-start.3
  570.8 11.2 copy-start.11
  570.8 11.2 copy-start.16
  570.8 11.2 copy-start.21
  599.7 10.1 copy-start.6
  673.9 10.8 copy-start.50
  699.2 11.2 copy-start.3
  699.2 11.2 copy-start.11
  699.2 11.2 copy-start.16
  699.2 11.2 copy-start.21
  810.6 41.1 %copy-start.23 = (f32[1,1024,24]{1,2,0:T(8,128)}, f32[1,1024,24]{1,2,0:T(8,128)S(1)}, u32[]{:S(2)}) copy-start(f32[1,1024,24]{1,2,0:T(8,128)S(1)} %get-tuple-element.648) | copy-start | bytes 294916
  810.6 20.2 %copy-start.26 = (f32[1792]{0:T(1024)S(1)}, f32[1792]{0:T(1024)}, u32[]{:S(2)}) copy-start(f32[1792]{0:T(1024)} %copy-done.25) | copy-start | bytes 21508
  810.6 20.2 %copy-start.28 = (f32[1792]{0:T(1024)S(1)}, f32[1792]{0:T(1024)}, u32[]{:S(2)}) copy-start(f32[1792]{0:T(1024)} %copy-done.27) | copy-start | bytes 21508
  810.6 20.2 %copy-start.30 = (f32[1792]{0:T(1024)S(1)}, f32[1792]{0:T(1024)}, u32[]{:S(2)}) copy-start(f32[1792]{0:T(1024)} %copy-done.29) | copy-start | bytes 21508
  810.6 20.2 %copy-start.32 = (f32[1792]{0:T(1024)S(1)}, f32[1792]{0:T(1024)}, u32[]{:S(2)}) copy-start(f32[1792]{0:T(1024)} %copy-done.31) | copy-start | bytes 21508
  839.2 12.5 %copy-start.13 = (bf16[1,1024,768]{2,1,0:T(8,128)(2,1)S(1)}, bf16[1,1024,768]{2,1,0:T(8,128)(2,1)}, u32[]{:S(2)}) copy-start(bf16[1,1024,768]{2,1,0:T(8,128)(2,1)} %param.15) | copy-start | bytes 4718596
  839.2 12.5 %copy-start.43 = (f32[768]{0:T(1024)S(1)}, f32[768]{0:T(1024)}, u32[]{:S(2)}) copy-start(f32[768]{0:T(1024)} %copy-done.42) | copy-start | bytes 9220
  839.2 12.5 %copy-start.46 = (f32[1024]{0:T(1024)S(1)}, f32[1024]{0:T(1024)}, u32[]{:S(2)}) copy-start(f32[1024]{0:T(1024)} %copy-done.45) | copy-start | bytes 12292
  866.9 85.6 %copy-start.24 = (f32[1,1024,24]{1,2,0:T(8,128)S(1)}, f32[1,1024,24]{1,2,0:T(8,128)}, u32[]{:S(2)}) copy-start(f32[1,1024,24]{1,2,0:T(8,128)} %copy-done.23) | copy-start | bytes 294916
  866.9 85.6 %copy-start.47 = (f32[1024]{0:T(1024)S(1)}, f32[1024]{0:T(1024)}, u32[]{:S(2)}) copy-start(f32[1024]{0:T(1024)} %copy-done.45) | copy-start | bytes 12292
  866.9 236.7 %all-reduce.22.cloned.1.call-start = ((), (), s32[]{:S(2)}) async-start(), calls=%async_computation.6 | async-start | bytes 7667712 | tf_op jit(solution)/shard_map/psum | solution.py:200
  952.6 12.5 %copy-start.53 = (f32[1536]{0:T(1024)S(1)}, f32[1536]{0:T(1024)}, u32[]{:S(2)}) copy-start(f32[1536]{0:T(1024)} %get-tuple-element.578) | copy-start | bytes 18436
  952.6 12.5 %copy-start.58 = (f32[24]{0:T(128)S(1)}, f32[24]{0:T(128)}, u32[]{:S(2)}) copy-start(f32[24]{0:T(128)} %get-tuple-element.647) | copy-start | bytes 292
  952.6 63.2 %copy-start.38 = (f32[1024]{0:T(1024)S(1)}, f32[1024]{0:T(1024)}, u32[]{:S(2)}) copy-start(f32[1024]{0:T(1024)} %copy-done.37) | copy-start | bytes 12292
  952.6 63.2 %copy-start.35 = (f32[2834]{0:T(1024)S(1)}, f32[2834]{0:T(1024)}, u32[]{:S(2)}) copy-start(f32[2834]{0:T(1024)} %param.19) | copy-start | bytes 34012
  952.6 63.2 %copy-start.51 = (f32[2834]{0:T(1024)S(1)}, f32[2834]{0:T(1024)}, u32[]{:S(2)}) copy-start(f32[2834]{0:T(1024)} %param.24) | copy-start | bytes 34012
  952.6 63.2 %copy-start.52 = (f32[2834]{0:T(1024)S(1)}, f32[2834]{0:T(1024)}, u32[]{:S(2)}) copy-start(f32[2834]{0:T(1024)} %param.25) | copy-start | bytes 34012
  952.6 63.8 %copy-start.18 = (bf16[1,1024,768]{2,1,0:T(8,128)(2,1)S(1)}, bf16[1,1024,768]{2,1,0:T(8,128)(2,1)}, u32[]{:S(2)}) copy-start(bf16[1,1024,768]{2,1,0:T(8,128)(2,1)} %param.16) | copy-start | bytes 4718596
  952.6 63.8 %copy-start.44 = (f32[768]{0:T(1024)S(1)}, f32[768]{0:T(1024)}, u32[]{:S(2)}) copy-start(f32[768]{0:T(1024)} %copy-done.42) | copy-start | bytes 9220
  965.1 55.9 %copy-start.40 = (f32[1536]{0:T(1024)S(1)}, f32[1536]{0:T(1024)}, u32[]{:S(2)}) copy-start(f32[1536]{0:T(1024)} %slice_convert_fusion.1) | copy-start | bytes 18436
  965.1 55.9 %copy-start.49 = (f32[1024]{0:T(1024)S(1)}, f32[1024]{0:T(1024)}, u32[]{:S(2)}) copy-start(f32[1024]{0:T(1024)} %copy-done.48) | copy-start | bytes 12292
  1015.8 12.2 %copy-start.36 = (f32[2834]{0:T(1024)}, f32[2834]{0:T(1024)S(1)}, u32[]{:S(2)}) copy-start(f32[2834]{0:T(1024)S(1)} %psum.26) | copy-start | bytes 34012
  1028.0 80.4 %copy-start.9 = (f32[192,3352]{1,0:T(8,128)S(1)}, f32[192,3352]{1,0:T(8,128)}, u32[]{:S(2)}) copy-start(f32[192,3352]{1,0:T(8,128)} %param.17) | copy-start | bytes 7723012
  (35 other events, 234.8 us)
Sparse Core Ops, SparseCore 0:
  10.5 43.6 all-gather.2
  56.3 24.1 all-gather.4
  236.8 48.2 reduce-scatter.4
  867.1 85.4 reduce-scatter.2
  956.1 147.5 all-reduce.21
where the time goes:
time: 1140 us; the launch traced here: 1120 us
  local copies, waits for them, and re-layouts  389 us (34%)
  matrix products  261 us (23%)
  other arithmetic  208 us (18%)
  waiting for transfers between devices  184 us (16%)
  blocking collectives  64.3 us (6%)
  between operations  16 us (1%)
    dynamic_update_slice x20, local copies, waits for them, and re-layouts, mix_sequence(): lax.scan(jax.checkpoint(span_step), start_state, (x_scaled.reshape(blocks...  191 us
    dot_general x12, matrix products, span_step(): jnp.einsum('hts,shp->thp', weighted, x_heads, precision=highest)  103 us
    dot_general x34, matrix products, contract_cols(): lax.dot_general(left, right, (((1,), (1,)), ((), ())), precision=precisio...  91.2 us
    reduce_scatter x1, waiting for transfers between devices, shards(): lax.psum_scatter(summed[0], 'shard', scatter_dimension=0, tiled=True)  83.9 us
    psum x1, waiting for transfers between devices, shards(): summed = lax.psum((grad_w_in, grad_w_out, small_grad), 'dp')  75.6 us
    dot_general x14, matrix products, contract_rows(): lax.dot_general(left, right, (((0,), (0,)), ((), ())), precision=precisio...  52.2 us
    psum x1, blocking collectives, shards(): summed = lax.psum((grad_w_in, grad_w_out, small_grad), 'dp')  39.2 us
    squeeze x20, local copies, waits for them, and re-layouts, mix_sequence(): lax.scan(jax.checkpoint(span_step), start_state, (x_scaled.reshape(blocks...  29.1 us
  transfers between devices with their start and end apart: 5, of which 3 were waited for; matrix products, arithmetic and copies ran while one was open for 73% of the time, Pallas kernels for 0%

commit v1 on v0

v1 whole, which is shorter than its diff:
```python
import math
import jax
import jax.numpy as jnp
from jax import lax
from jax.experimental import pallas as pl
from jax.experimental.pallas import tpu as pltpu
from jax.sharding import PartitionSpec as P

INNER = 1536
STATE = 128
D = 768
STEP_COUNT = 3
HEADDIM = 64
HEADS = 24
CONV = 4
CHANNELS = INNER + 2 * STATE
Q = 128
PAIRS = INNER // 128
WIDTH = INNER + CHANNELS + 128
R_OFF = INNER + CHANNELS
LOG2E = math.log2(math.e)
f32 = jnp.float32
bf16 = jnp.bfloat16
highest = lax.Precision.HIGHEST
norm_epsilon = 1e-05


def mm(a, b):
    return lax.dot_general(a, b, (((1,), (0,)), ((), ())), preferred_element_type=f32)


def mm_t(a, b):
    return lax.dot_general(a, b, (((1,), (1,)), ((), ())), preferred_element_type=f32)


def mm_exact(a, b):
    return lax.dot_general(a, b, (((1,), (0,)), ((), ())), precision=highest, preferred_element_type=f32)


def sigmoid(v):
    return 0.5 * jnp.tanh(0.5 * v) + 0.5


def softplus(v):
    return jnp.maximum(v, 0.0) + jnp.log1p(jnp.exp(-jnp.abs(v)))


def fold8(v):
    return v.reshape(Q // 8, 8, v.shape[1]).sum(axis=0)


def pair_of(lo, values, j):
    return jnp.where(lo, values[:, 2 * j : 2 * j + 1], values[:, 2 * j + 1 : 2 * j + 2])


def head_sums(j, rows, offset):
    k = lax.broadcasted_iota(jnp.int32, (rows, 128), 0)
    n = lax.broadcasted_iota(jnp.int32, (rows, 128), 1)
    head = 2 * j + jnp.where(k % 128 >= 64, 1, 0)
    return jnp.where(n == head + offset(k), 1.0, 0.0).astype(bf16)


def forward_kernel(
    proj_ref, dmix_ref, cw_ref, cb_ref, hp_ref, dsk_ref, nw_ref, es_ref,
    mixer_ref, dz_ref, ds_ref, st_ref, dt_ref, cum_ref, ps_ref, dnw_ref,
    state, halo, s_scr,
):
    step = pl.program_id(0)

    @pl.when(step == 0)
    def _():
        state[...] = jnp.zeros_like(state)
        halo[...] = jnp.zeros_like(halo)
        dnw_ref[...] = jnp.zeros_like(dnw_ref)

    lane = lax.broadcasted_iota(jnp.int32, (Q, 128), 1)
    row = lax.broadcasted_iota(jnp.int32, (Q, 128), 0)
    lo = lane < 64
    lower = row >= lane
    dt = softplus(proj_ref[:, R_OFF : R_OFF + 128] + hp_ref[0:1, :])
    log_decay = dt * (jnp.exp(hp_ref[1:2, :]) * (-LOG2E))
    cum = mm_exact(jnp.where(lower, 1.0, 0.0), log_decay)
    cum_t = cum.T
    dt_ref[...] = dt
    cum_ref[...] = cum
    total = cum[Q - 1 : Q, :]

    def conv(col):
        ext = jnp.concatenate([halo[:, col : col + 128], proj_ref[:, INNER + col : INNER + col + 128]], axis=0)
        out = cb_ref[:, col : col + 128]
        for k in range(CONV):
            out = out + cw_ref[k : k + 1, col : col + 128] * ext[5 + k : 5 + k + Q]
        return out

    def act(col):
        c = conv(col)
        return c * sigmoid(c)

    b_low = act(INNER).astype(bf16)
    c_low = act(INNER + STATE).astype(bf16)
    b_t = b_low.T
    scores = jnp.where(lower, mm_t(c_low, b_low), 0.0)
    sq = jnp.zeros((Q, 128), f32)
    dot = jnp.zeros((Q, 128), f32)
    for j in range(PAIRS):
        col = slice(128 * j, 128 * j + 128)
        x = act(128 * j)
        xs = x * pair_of(lo, dt, j)
        xs_low = xs.astype(bf16)
        cum0 = jnp.broadcast_to(cum[:, 2 * j : 2 * j + 1], (Q, 128))
        cum1 = jnp.broadcast_to(cum[:, 2 * j + 1 : 2 * j + 2], (Q, 128))
        m0 = jnp.exp2(jnp.minimum(cum0 - cum_t[2 * j : 2 * j + 1, :], 0.0)) * scores
        m1 = jnp.exp2(jnp.minimum(cum1 - cum_t[2 * j + 1 : 2 * j + 2, :], 0.0)) * scores
        weights = jnp.concatenate([m0.astype(bf16), m1.astype(bf16)], axis=1)
        zero = jnp.zeros_like(xs_low)
        stacked = jnp.concatenate([jnp.where(lo, xs_low, zero), jnp.where(lo, zero, xs_low)], axis=0)
        cum_e = jnp.where(lo, cum0, cum1)
        tot_e = pair_of(lo[0:1], total, j)
        old = state[:, col]
        old_low = old.astype(bf16)
        st_ref[0, :, col] = old_low
        y = mm(weights, stacked) + jnp.exp2(cum_e) * mm(c_low, old_low)
        moved = (xs * jnp.exp2(tot_e - cum_e)).astype(bf16)
        state[:, col] = old * jnp.exp2(tot_e) + mm(b_t, moved)
        s = y + dsk_ref[:, col] * x
        s_scr[:, col] = s
        z = proj_ref[:, col]
        g = s * (z * sigmoid(z))
        sq = sq + g * g
        dot = dot + g * (dmix_ref[:, col] * nw_ref[:, col])
    halo[...] = proj_ref[Q - 8 : Q, INNER : INNER + CHANNELS]
    mean = jnp.sum(sq, axis=1, keepdims=True) * (1.0 / INNER)
    factor = lax.rsqrt(mean + norm_epsilon)
    back = factor * factor * factor * (jnp.sum(dot, axis=1, keepdims=True) * (1.0 / INNER))
    factor = jnp.broadcast_to(factor, (Q, 128))
    back = jnp.broadcast_to(back, (Q, 128))
    ps = jnp.zeros((Q, 128), f32)
    for j in range(PAIRS):
        col = slice(128 * j, 128 * j + 128)
        s = s_scr[:, col]
        z = proj_ref[:, col]
        sig = sigmoid(z)
        sz = z * sig
        g = s * sz
        dm = dmix_ref[:, col]
        gf = g * factor
        mixer_ref[:, col] = (gf * nw_ref[:, col]).astype(bf16)
        dnw_ref[:, col] += fold8(dm * gf)
        dg = dm * nw_ref[:, col] * factor - g * back
        dz_ref[:, col] = (dg * s * (sig + sz * (1.0 - sig))).astype(bf16)
        ds_low = (dg * sz).astype(bf16)
        ds_ref[:, col] = ds_low
        prod = ds_low.astype(f32) * s
        hi = prod.astype(bf16)
        rest = (prod - hi.astype(f32)).astype(bf16)
        ps = ps + mm(jnp.concatenate([hi, rest], axis=1), es_ref[j, 0:256, :])
    ps_ref[...] = ps


def backward_kernel(
    proj_ref, prev_ref, ds_ref, st_ref, dt_ref, cum_ref, ps_ref, cw_ref, cb_ref, hp_ref, dsk_ref, es_ref,
    du_ref, dcw_ref, dcb_ref, dhp_ref, dsk_out_ref,
    dstate, dc_next, dyc_scr, moved_scr, dlow_scr,
):
    step = pl.program_id(0)
    blocks = pl.num_programs(0)
    chunk = blocks - 1 - step

    @pl.when(step == 0)
    def _():
        dstate[...] = jnp.zeros_like(dstate)
        dc_next[...] = jnp.zeros_like(dc_next)
        dcw_ref[...] = jnp.zeros_like(dcw_ref)
        dcb_ref[...] = jnp.zeros_like(dcb_ref)
        dhp_ref[...] = jnp.zeros_like(dhp_ref)
        dsk_out_ref[...] = jnp.zeros_like(dsk_out_ref)

    lane = lax.broadcasted_iota(jnp.int32, (Q, 128), 1)
    row = lax.broadcasted_iota(jnp.int32, (Q, 128), 0)
    lo = lane < 64
    upper = row <= lane
    have_prev = jnp.where(chunk > 0, 1.0, 0.0)
    dt = dt_ref[...]
    cum = cum_ref[...]
    cum_t = cum.T
    total = cum[Q - 1 : Q, :]

    def taps(col):
        ext = jnp.concatenate([prev_ref[:, INNER + col : INNER + col + 128] * have_prev, proj_ref[:, INNER + col : INNER + col + 128]], axis=0)
        return [ext[5 + k : 5 + k + Q] for k in range(CONV)]

    def conv(shifted, col):
        out = cb_ref[:, col : col + 128]
        for k in range(CONV):
            out = out + cw_ref[k : k + 1, col : col + 128] * shifted[k]
        return out

    def conv_back(dx, c, sig, shifted, col):
        dc = dx * (sig + c * sig * (1.0 - sig))
        for k in range(CONV):
            dcw_ref[k, :, col : col + 128] += fold8(dc * shifted[k])
        dcb_ref[:, col : col + 128] += fold8(dc)
        ext = jnp.concatenate([dc, dc_next[:, col : col + 128]], axis=0)
        du = cw_ref[CONV - 1 : CONV, col : col + 128] * dc
        for k in range(CONV - 1):
            du = du + cw_ref[k : k + 1, col : col + 128] * ext[CONV - 1 - k : CONV - 1 - k + Q]
        dc_next[:, col : col + 128] = dc[0:8]
        du_ref[:, col : col + 128] = du.astype(bf16)

    b_taps = taps(INNER)
    b_conv = conv(b_taps, INNER)
    b_low = (b_conv * sigmoid(b_conv)).astype(bf16)
    c_taps = taps(INNER + STATE)
    c_conv = conv(c_taps, INNER + STATE)
    c_low = (c_conv * sigmoid(c_conv)).astype(bf16)
    c_t = c_low.T
    scores = jnp.where(upper, mm_t(b_low, c_low), 0.0)
    dscores = jnp.zeros((Q, 128), f32)
    sums = jnp.zeros((Q, 128), f32)
    carry = jnp.zeros((8, 128), f32)
    for j in range(PAIRS):
        col = slice(128 * j, 128 * j + 128)
        shifted = taps(128 * j)
        c = conv(shifted, 128 * j)
        sig = sigmoid(c)
        x = c * sig
        dt_e = pair_of(lo, dt, j)
        xs = x * dt_e
        xs_low = xs.astype(bf16)
        dy = ds_ref[:, col]
        dyf = dy.astype(f32)
        cum0 = jnp.broadcast_to(cum[:, 2 * j : 2 * j + 1], (Q, 128))
        cum1 = jnp.broadcast_to(cum[:, 2 * j + 1 : 2 * j + 2], (Q, 128))
        l0 = jnp.exp2(jnp.minimum(cum_t[2 * j : 2 * j + 1, :] - cum0, 0.0))
        l1 = jnp.exp2(jnp.minimum(cum_t[2 * j + 1 : 2 * j + 2, :] - cum1, 0.0))
        weights = jnp.concatenate([(l0 * scores).astype(bf16), (l1 * scores).astype(bf16)], axis=1)
        zero = jnp.zeros_like(dy)
        stacked = jnp.concatenate([jnp.where(lo, dy, zero), jnp.where(lo, zero, dy)], axis=0)
        dxw = mm(weights, stacked)
        dm = mm_t(xs_low, stacked)
        dscores = dscores + l0 * dm[:, :128] + l1 * dm[:, 128:]
        cum_e = jnp.where(lo, cum0, cum1)
        tot_e = pair_of(lo[0:1], total, j)
        to_end = jnp.exp2(tot_e - cum_e)
        dnew = dstate[:, col]
        dnew_low = dnew.astype(bf16)
        dlow_scr[:, col] = dnew_low
        dxe = to_end * mm(b_low, dnew_low)
        moved_scr[:, col] = (xs * to_end).astype(bf16)
        dyc = (dyf * jnp.exp2(cum_e)).astype(bf16)
        dyc_scr[:, col] = dyc
        kept = dnew * jnp.exp2(tot_e)
        dstate[:, col] = kept + mm(c_t, dyc)
        inner = fold8(kept * st_ref[0, :, col].astype(f32))
        inner_hi = inner.astype(bf16)
        inner_lo = (inner - inner_hi.astype(f32)).astype(bf16)
        carry = carry + mm(jnp.concatenate([inner_hi, inner_lo], axis=1), es_ref[j, 0:256, :])
        dxs = dxw + dxe
        dyx = dyf * x
        dsk_out_ref[:, col] += fold8(dyx)
        w1 = xs_low.astype(f32) * dxw + dsk_ref[:, col] * dyx
        hi = w1.astype(bf16)
        rest = (w1 - hi.astype(f32)).astype(bf16)
        many = jnp.concatenate([hi, rest, (xs * dxe).astype(bf16), (x * dxs).astype(bf16)], axis=1)
        sums = sums + mm(many, es_ref[j])
        conv_back(dxs * dt_e + dsk_ref[:, col] * dyf, c, sig, shifted, 128 * j)
    dscores = jnp.where(upper, dscores, 0.0).astype(bf16)
    db = mm(dscores, c_low) + mm_t(moved_scr[...], dlow_scr[...])
    dcc = mm(dscores.T, b_low) + mm_t(dyc_scr[...], st_ref[0])
    conv_back(db, b_conv, sigmoid(b_conv), b_taps, INNER)
    conv_back(dcc, c_conv, sigmoid(c_conv), c_taps, INNER + STATE)
    head = lane < HEADS
    q = jnp.where(head, pltpu.roll(sums, 96, 1), 0.0)
    v = jnp.where(head, pltpu.roll(sums, 64, 1), 0.0)
    p = jnp.where(head, ps_ref[...] - sums, 0.0)
    ones = jnp.where(upper, 1.0, 0.0)
    da = mm_exact(ones, p) + mm_exact(1.0 - ones, q) + jnp.sum(carry, axis=0, keepdims=True)
    rate = jnp.exp(hp_ref[1:2, :])
    raw = proj_ref[:, R_OFF : R_OFF + 128] + hp_ref[0:1, :]
    dr = jnp.where(head, (v - rate * da) * jax.nn.sigmoid(raw), 0.0)
    dhp_ref[0] += fold8(dr)
    dhp_ref[1] += fold8(jnp.where(head, da * dt * -rate, 0.0))
    du_ref[:, CHANNELS : CHANNELS + 128] = dr.astype(bf16)


def selectors():
    k = jnp.arange(512)
    off = jnp.where(k < 256, 0, jnp.where(k < 384, 32, 64))
    local = jnp.where(k % 128 >= 64, 1, 0)
    target = off[None, :] + 2 * jnp.arange(PAIRS)[:, None] + local[None, :]
    return (target[:, :, None] == jnp.arange(128)[None, None, :]).astype(bf16)


def whole(shape):
    return pl.BlockSpec(shape, lambda i: (0,) * len(shape))


def mix_forward(proj, dmix, cw, cb, hp, dsk, nw, es):
    length = proj.shape[0]
    blocks = length // Q

    def rows(width):
        return pl.BlockSpec((Q, width), lambda i: (i, 0))

    return pl.pallas_call(
        forward_kernel,
        grid=(blocks,),
        in_specs=[
            rows(WIDTH), rows(INNER), whole((CONV, CHANNELS)), whole((1, CHANNELS)), whole((8, 128)),
            whole((1, INNER)), whole((1, INNER)), whole((PAIRS, 512, 128)),
        ],
        out_specs=[
            rows(INNER), rows(INNER), rows(INNER), pl.BlockSpec((1, STATE, INNER), lambda i: (i, 0, 0)),
            rows(128), rows(128), rows(128), whole((8, INNER)),
        ],
        out_shape=[
            jax.ShapeDtypeStruct((length, INNER), bf16),
            jax.ShapeDtypeStruct((length, INNER), bf16),
            jax.ShapeDtypeStruct((length, INNER), bf16),
            jax.ShapeDtypeStruct((blocks, STATE, INNER), bf16),
            jax.ShapeDtypeStruct((length, 128), f32),
            jax.ShapeDtypeStruct((length, 128), f32),
            jax.ShapeDtypeStruct((length, 128), f32),
            jax.ShapeDtypeStruct((8, INNER), f32),
        ],
        scratch_shapes=[
            pltpu.VMEM((STATE, INNER), f32),
            pltpu.VMEM((8, CHANNELS), f32),
            pltpu.VMEM((Q, INNER), f32),
        ],
        compiler_params=pltpu.CompilerParams(vmem_limit_bytes=48 * 1024 * 1024),
        name="mix_forward",
    )(proj, dmix, cw, cb, hp, dsk, nw, es)


def mix_backward(proj, ds, st, dt, cum, ps, cw, cb, hp, dsk, es):
    length = proj.shape[0]
    blocks = length // Q

    def rows(width):
        return pl.BlockSpec((Q, width), lambda i: (blocks - 1 - i, 0))

    return pl.pallas_call(
        backward_kernel,
        grid=(blocks,),
        in_specs=[
            rows(WIDTH),
            pl.BlockSpec((8, WIDTH), lambda i: (jnp.maximum((blocks - 1 - i) * (Q // 8) - 1, 0), 0)),
            rows(INNER), pl.BlockSpec((1, STATE, INNER), lambda i: (blocks - 1 - i, 0, 0)),
            rows(128), rows(128), rows(128),
            whole((CONV, CHANNELS)), whole((1, CHANNELS)), whole((8, 128)),
            whole((1, INNER)), whole((PAIRS, 512, 128)),
        ],
        out_specs=[
            rows(CHANNELS + 128), whole((CONV, 8, CHANNELS)), whole((8, CHANNELS)), whole((2, 8, 128)), whole((8, INNER)),
        ],
        out_shape=[
            jax.ShapeDtypeStruct((length, CHANNELS + 128), bf16),
            jax.ShapeDtypeStruct((CONV, 8, CHANNELS), f32),
            jax.ShapeDtypeStruct((8, CHANNELS), f32),
            jax.ShapeDtypeStruct((2, 8, 128), f32),
            jax.ShapeDtypeStruct((8, INNER), f32),
        ],
        scratch_shapes=[
            pltpu.VMEM((STATE, INNER), f32),
            pltpu.VMEM((8, CHANNELS), f32),
            pltpu.VMEM((Q, INNER), bf16),
            pltpu.VMEM((Q, INNER), bf16),
            pltpu.VMEM((STATE, INNER), bf16),
        ],
        compiler_params=pltpu.CompilerParams(vmem_limit_bytes=48 * 1024 * 1024),
        name="mix_backward",
    )(proj, proj, ds, st, dt, cum, ps, cw, cb, hp, dsk, es)

beta_first = 0.9
beta_second = 0.95
adam_epsilon = 1e-08
rate_matrix = 0.01
rate_vector = 0.1
decay_matrix = 0.1


def layout():
    return [(CONV, CHANNELS), (CHANNELS,), (HEADS,), (HEADS,), (HEADS,), (INNER,), (D,)]


def unpack(flat_values):
    pieces = []
    offset = 0
    for shape in layout():
        count = math.prod(shape)
        pieces.append(flat_values[offset : offset + count].reshape(shape))
        offset += count
    return pieces


def mm_rows(left, right):
    return lax.dot_general(left, right, (((0,), (0,)), ((), ())), preferred_element_type=f32)


def prenorm(values, gain_values):
    return (
        values
        * lax.rsqrt(jnp.mean(values * values, axis=-1, keepdims=True) + norm_epsilon)
        * gain_values
    )


def adam(param, grad, first, second, rate, decay):
    new_first = beta_first * first + (1.0 - beta_first) * grad
    new_second = beta_second * second + (1.0 - beta_second) * grad * grad
    fix_first = 1.0 - beta_first**STEP_COUNT
    fix_second = 1.0 - beta_second**STEP_COUNT
    update = new_first / fix_first / (jnp.sqrt(new_second / fix_second) + adam_epsilon)
    return (param - rate * (update + decay * param), new_first, new_second)


def reduce_grad(grad):
    part = lax.psum_scatter(grad.astype(bf16), "shard", scatter_dimension=0, tiled=True)
    return lax.psum(part, "dp")


def shards(
    inputs, cotangent, w_in, w_out, vectors, first_in, second_in, first_out, second_out, first_vec, second_vec,
):
    vec_len = vectors.shape[0]
    in_width = w_in.shape[1]
    w_in_low = jnp.pad(w_in.astype(bf16), ((0, 0), (0, WIDTH - in_width)))
    w_all = lax.all_gather(w_in_low, "shard", axis=0, tiled=True)
    w_out_all = lax.all_gather(w_out.astype(bf16), "shard", axis=0, tiled=True)
    vec_all = lax.all_gather(vectors.astype(bf16), "shard", axis=0, tiled=True).astype(f32)
    conv_w, conv_b, dt_bias, a_log, d_skip, norm_w, gain = unpack(vec_all)
    hp = jnp.stack([jnp.pad(v, (0, 128 - HEADS)) for v in (dt_bias, a_log)] + [jnp.zeros((128,), f32)] * 6)
    dsk = jnp.repeat(d_skip, HEADDIM)[None, :]
    es = selectors()
    seqs_here, length, width = inputs.shape
    rows = inputs.astype(f32).reshape(seqs_here * length, width)
    cot = cotangent.reshape(seqs_here * length, width)
    normed, prenorm_back = jax.vjp(prenorm, rows, gain)
    normed_low = normed.astype(bf16)
    proj = mm(normed_low, w_all)
    dmix = mm_t(cot, w_out_all)
    forward = []
    for n in range(seqs_here):
        part = slice(n * length, (n + 1) * length)
        forward.append(mix_forward(proj[part], dmix[part], conv_w, conv_b[None], hp, dsk, norm_w[None], es))
    mixer_low = jnp.concatenate([f[0] for f in forward], axis=0)
    dz = jnp.concatenate([f[1] for f in forward], axis=0)
    outputs = (rows + mm(mixer_low, w_out_all)).astype(bf16).reshape(inputs.shape)
    grad_out = reduce_grad(mm_rows(mixer_low, cot))
    grad_z = reduce_grad(mm_rows(normed_low, dz))
    backward = []
    for n in range(seqs_here):
        part = slice(n * length, (n + 1) * length)
        _, _, ds, st, dt, cum, ps, _ = forward[n]
        backward.append(mix_backward(proj[part], ds, st, dt, cum, ps, conv_w, conv_b[None], hp, dsk, es))
    du = jnp.concatenate([b[0] for b in backward], axis=0)
    grad_u = reduce_grad(mm_rows(normed_low, du))
    d_normed = mm_t(dz, w_all[:, :INNER]) + mm_t(du, w_all[:, INNER:])
    d_rows, d_gain = prenorm_back(d_normed)
    input_grad = (cot.astype(f32) + d_rows).reshape(inputs.shape)

    def total(values):
        return sum(values[1:], values[0])

    dcw = total([b[1] for b in backward]).sum(axis=1)
    dcb = total([b[2] for b in backward]).sum(axis=0)
    dhp = total([b[3] for b in backward]).sum(axis=1)
    dskip = total([b[4] for b in backward]).sum(axis=0).reshape(HEADS, HEADDIM).sum(axis=1)
    dnw = total([f[7] for f in forward]).sum(axis=0)
    small = jnp.concatenate([dcw.reshape(-1), dcb, dhp[0, :HEADS], dhp[1, :HEADS], dskip, dnw, d_gain])
    grad_vec = lax.psum(lax.psum_scatter(small, "shard", scatter_dimension=0, tiled=True), "dp")
    grad_in = jnp.concatenate([grad_z.astype(f32), grad_u.astype(f32)[:, : in_width - INNER]], axis=1)
    grad_out = grad_out.astype(f32)
    new_w_in, new_first_in, new_second_in = adam(w_in, grad_in, first_in, second_in, rate_matrix, decay_matrix)
    new_w_out, new_first_out, new_second_out = adam(
        w_out, grad_out, first_out, second_out, rate_matrix, decay_matrix
    )
    conv_count = CONV * CHANNELS
    positions = lax.axis_index("shard") * vec_len + jnp.arange(vec_len, dtype=jnp.int32)
    is_matrix = positions < conv_count
    rate = jnp.where(is_matrix, rate_matrix, rate_vector)
    decay = jnp.where(is_matrix, decay_matrix, 0.0)
    new_vectors, new_first_vec, new_second_vec = adam(vectors, grad_vec, first_vec, second_vec, rate, decay)
    return (
        outputs, input_grad, grad_in, grad_out, grad_vec, new_w_in, new_w_out, new_vectors,
        new_first_in, new_second_in, new_first_out, new_second_out, new_first_vec, new_second_vec,
    )


def solution(mesh):
    tokens = P(("dp", "shard"), None, None)
    matrix = P("shard", None)
    vector = P("shard")
    in_specs = (tokens, tokens, matrix, matrix, vector, matrix, matrix, matrix, matrix, vector, vector)
    out_specs = (
        tokens, tokens, matrix, matrix, vector, matrix, matrix, vector,
        matrix, matrix, matrix, matrix, vector, vector,
    )
    return jax.shard_map(shards, mesh=mesh, in_specs=in_specs, out_specs=out_specs, check_vma=False)
```

time: 1140 us -> 355 us (0.31); the launches traced: 1120 us -> 355 us
  local copies, waits for them, and re-layouts: 389 us -> 5.07 us
  matrix products: 261 us -> 55.4 us
  other arithmetic: 208 us -> 21.5 us
  Pallas kernels: 0 us -> 75.2 us
  waiting for transfers between devices: 184 us -> 118 us
    dot_general x62 -> x8, matrix products: 261 us -> 55.4 us  [the longest x3 20.4 us: mm_t(): lax.dot_general(a, b, (((1,), (1,)), ((), ())), preferred_element_type=f32)]
    dynamic_update_slice x20 -> x0, local copies, waits for them, and re-layouts: 191 us -> none  [mix_sequence(): lax.scan(jax.checkpoint(span_step), start_state, (x_scaled.reshape(blocks...]
    pallas_call x0 -> x2, Pallas kernels: none -> 75.2 us  [the longest x1 46.8 us: mix_backward(): pl.pallas_call(backward_kernel, grid=(blocks,), in_specs=[rows(WIDTH), pl...]
    reduce_sum x22 -> x6, other arithmetic: 63.1 us -> 0.26 us  [the longest x2 0.14 us: shards(): total([b[4] for b in backward]).sum(axis=0).reshape(HEADS, HEADDIM)]
    mul x13 -> x1, other arithmetic: 53.2 us -> 0.01 us  [selectors(): target = off[None, :] + 2 * jnp.arange(PAIRS)[:, None] + local[None, :]]
    reduce_scatter x2 -> x3, waiting for transfers between devices: 83.9 us -> 31.9 us  [reduce_grad(): lax.psum_scatter(grad.astype(bf16), 'shard', scatter_dimension=0, tiled=T...]
    psum x1, waiting for transfers between devices: 75.6 us -> 43.9 us  [reduce_grad(): return lax.psum(part, 'dp')]
    transpose x12 -> x0, local copies, waits for them, and re-layouts: 30.1 us -> none  [the longest x1 8.33 us: mix_sequence(): x_scaled.reshape(blocks, SPAN, INNER)]
  transfers between devices with their start and end apart: 5 -> 6, of which waited for: 3 -> 4; matrix products, arithmetic and copies ran while one was open for 73% -> 14% of each run, Pallas kernels for 0% -> 13%
where the time goes in v1:
time: 355 us
  waiting for transfers between devices  118 us (33%)
  Pallas kernels  75.2 us (21%)
  blocking collectives  62.7 us (18%)
  matrix products  55.4 us (16%)
  other arithmetic  21.5 us (6%)
  between operations  15.8 us (4%)
  local copies, waits for them, and re-layouts  5.07 us (1%)
    pallas_call x1, Pallas kernels, mix_backward(): pl.pallas_call(backward_kernel, grid=(blocks,), in_specs=[rows(WIDTH), pl...  46.8 us
    psum x1, waiting for transfers between devices, reduce_grad(): return lax.psum(part, 'dp')  43.9 us
    psum x1, blocking collectives, shards(): lax.psum(lax.psum_scatter(small, 'shard', scatter_dimension=0, tiled=True...  38.4 us
    all_gather x1, waiting for transfers between devices, shards(): w_all = lax.all_gather(w_in_low, 'shard', axis=0, tiled=True)  35.7 us
    reduce_scatter x3, waiting for transfers between devices, reduce_grad(): lax.psum_scatter(grad.astype(bf16), 'shard', scatter_dimension=0, tiled=T...  31.9 us
    pallas_call x1, Pallas kernels, mix_forward(): pl.pallas_call(forward_kernel, grid=(blocks,), in_specs=[rows(WIDTH), row...  28.4 us
    unnamed x2, blocking collectives  24.4 us
    dot_general x3, matrix products, mm_t(): lax.dot_general(a, b, (((1,), (1,)), ((), ())), preferred_element_type=f32)  20.4 us
  transfers between devices with their start and end apart: 6, of which 4 were waited for; matrix products, arithmetic and copies ran while one was open for 14% of the time, Pallas kernels for 13%

profile of v1, /device:TPU:0, one launch (start us, length us, event | category | flops | bytes accessed | tf_op | source)
XLA Modules:
  0.0 354.8 jit_solution(14135391844373350537)
XLA Ops:
  7.2 0.0 all-gather.5.cloned.1.call-start
  7.2 2.1 convert_element_type.50
  9.4 0.0 all-gather.5.cloned.1.call-update
  9.4 0.0 all-gather.3.cloned.1.call-start
  9.4 1.9 convert_element_type.49
  11.3 0.0 copy-start.12
  11.4 0.0 copy-start.22
  11.4 0.0 copy-start.3
  11.4 1.2 pad.11
  12.5 0.0 all-gather.3.cloned.1.call-update
  12.6 0.0 reduce-scatter.8.cloned.1.call-start
  12.7 0.6 fusion.38
  13.9 0.3 dynamic-update-slice
  14.2 13.8 %all-reduce.3 = bf16[11336]{0:T(1024)(128)(2,1)S(1)} all-reduce(bf16[11336]{0:T(1024)(128)(2,1)S(1)} %dynamic-update-slice), channel_id=1, replica_groups=mesh['dp'=8,'shard'=4] {'shard'}, use_global_device_ids=true, to_apply=%add.3 | all-reduce | flops 11336 | bytes 45344
  28.1 0.1 slice.49
  28.1 0.1 slice.55
  28.2 0.1 pad.19.clone
  28.3 0.1 pad.18.clone
  28.4 0.1 fusion.37
  28.5 0.1 broadcast_in_dim.49
  28.6 0.1 broadcast_in_dim_reshape.3.dsk_ref
  28.7 0.4 fusion.6
  29.1 0.1 maximum_maximum_fusion.hp_ref
  29.1 0.1 add_add_fusion.1
  29.2 1.1 fusion.9.es_ref
  30.3 6.9 %all-gather.5.cloned.1.call-done = bf16[1536,768]{1,0:T(8,128)(2,1)} async-done(((bf16[384,768]{1,0:T(8,128)(2,1)}), bf16[1536,768]{1,0:T(8,128)(2,1)}) %all-gather.5.cloned.1.call-update) | async-done | bytes 2359312 | tf_op jit(solution)/shard_map/all_gather | solution.py:430
  37.2 7.4 %fusion.19.dmix_ref = f32[1024,1536]{1,0:T(8,128)} fusion(bf16[1536,768]{1,0:T(8,128)(2,1)} %all-gather.5.cloned.1.call-done, bf16[1,1024,768]{2,1,0:T(8,128)(2,1)} %param.12), kind=kOutput, calls=%fused_computation.31 | convolution fusion | flops 2415919104 | bytes 10223616 | tf_op jit(solution)/shard_map/dot_general | solution.py:33
  44.6 35.7 %all-gather.3.cloned.1.call-done = bf16[768,3456]{1,0:T(8,128)(2,1)} async-done(((bf16[192,3456]{1,0:T(8,128)(2,1)}), bf16[768,3456]{1,0:T(8,128)(2,1)}) %all-gather.3.cloned.1.call-update) | async-done | bytes 5308432 | tf_op jit(solution)/shard_map/all_gather | solution.py:429
  80.2 11.7 %fusion.32.proj_ref.prev_ref = f32[1024,3456]{1,0:T(8,128)} fusion(bf16[768,3456]{1,0:T(8,128)(2,1)} %all-gather.3.cloned.1.call-done, bf16[1,1024,768]{2,1,0:T(8,128)(2,1)S(1)} %copy-done.3, f32[768]{0:T(1024)S(1)} %slice.49, f32[1024]{0:T(1024)S(1)} %fusion.24), kind=kOutput, calls=%fused_computation.63 | convolution fusion | flops 5438963712 | bytes 21044224 | tf_op jit(solution)/shard_map/dot_general | solution.py:29
  91.9 28.4 %mix_forward.1 = (bf16[1024,1536]{1,0:T(8,128)(2,1)}, bf16[1024,1536]{1,0:T(8,128)(2,1)}, bf16[1024,1536]{1,0:T(8,128)(2,1)}, bf16[8,128,1536]{2,1,0:T(8,128)(2,...) custom-call(f32[1024,3456]{1,0:T(8,128)} %fusion.32.proj_ref.prev_ref, ...), custom_call_target="tpu_custom_call" | custom-call | tf_op jit(solution)/shard_map/mix_forward/pallas_call | solution.py:305
  120.4 6.0 %convolution_convert_fusion = bf16[1536,768]{1,0:T(8,128)(2,1)} fusion(bf16[1024,1536]{1,0:T(8,128)(2,1)} %get-tuple-element.27, bf16[1,1024,768]{2,1,0:T(8,128)(2,1)S(1)} %copy-done.9), kind=kOutput, calls=%fused_computation.9 | convolution fusion | flops 2417098752 | bytes 7077888 | tf_op jit(solution)/shard_map/dot_general | solution.py:398
  126.3 0.0 reduce-scatter.8.cloned.1.call-update
  126.3 0.2 reduce-scatter.4.cloned.1.call-start
  126.6 6.6 %convolution_convert_fusion.1 = bf16[768,1536]{1,0:T(8,128)(2,1)} fusion(bf16[1024,1536]{1,0:T(8,128)(2,1)} %get-tuple-element.28, bf16[1,1024,768]{2,1,0:T(8,128)(2,1)} %param.11, f32[768]{0:T(1024)S(1)} %slice.49, f32[1024]{0:T(1024)S(1)} %fusion.24), kind=kOutput, calls=%fused_computation.10 | convolution fusion | flops 2420244480 | bytes 7085056 | tf_op jit(solution)/shard_map/dot_general | solution.py:398
  133.2 0.0 reduce-scatter.4.cloned.1.call-update
  133.2 0.0 reduce-scatter.6.cloned.1.call-start
  133.2 0.0 copy-start.4
  133.3 0.0 copy-start.15
  133.3 46.8 %mix_backward.1 = (bf16[1024,1920]{1,0:T(8,128)(2,1)}, f32[4,8,1792]{2,1,0:T(8,128)S(1)}, f32[8,1792]{1,0:T(8,128)S(1)}, f32[2,8,128]{2,1,0:T(8,128)S(1)}, f32[8,1536]{1,0:T(8,128)S(1)}) custom-call(f32[1024,3456]{1,0:T(8,128)} %fusion.32.proj_ref.prev_ref, f32[1024,3456]{1,0:T(8,128)} %fusion.32.proj_ref.prev_ref, ...), custom_call_target="tpu_custom_call" | custom-call | tf_op jit(solution)/shard_map/mix_backward/pallas_call | solution.py:343
  180.1 0.6 copy-done
  180.7 7.1 %convolution_convert_fusion.2 = bf16[768,1920]{1,0:T(8,128)(2,1)} fusion(bf16[1024,1920]{1,0:T(8,128)(2,1)} %get-tuple-element.34, bf16[1,1024,768]{2,1,0:T(8,128)(2,1)S(1)} %copy-done.4, f32[768]{0:T(1024)S(1)} %copy-done.15, f32[1024]{0:T(1024)S(1)} %copy-done.18), kind=kOutput, calls=%fused_computation.11 | convolution fusion | flops 3024519168 | bytes 8461312 | tf_op jit(solution)/shard_map/dot_general | solution.py:398
  187.8 0.0 reduce-scatter.6.cloned.1.call-update
  187.9 0.3 all-reduce.8.cloned.1.call-start
  188.8 0.1 reduce_sum.91
  189.0 0.1 reshape.143
  189.0 0.1 reduce_sum.95
  189.2 0.0 copy-start.5
  189.2 0.0 copy-start.16
  189.2 6.6 %fusion.10 = f32[1024,768]{1,0:T(8,128)S(1)} fusion(bf16[1024,1920]{1,0:T(8,128)(2,1)} %get-tuple-element.34, bf16[768,3456]{1,0:T(8,128)(2,1)} %all-gather.3.cloned.1.call-done), kind=kOutput, calls=%fused_computation.21 | convolution fusion | flops 3019898880 | bytes 10027008 | tf_op jit(solution)/shard_map/dot_general | solution.py:33
  195.9 6.4 %fusion.3 = (f32[768]{0:T(1024)S(1)}, f32[1024]{0:T(1024)S(1)}, f32[1024,768]{1,0:T(8,128)}) fusion(bf16[1,1024,768]{2,1,0:T(8,128)(2,1)S(1)} %copy-done.5, f32[1024]{0:T(1024)S(1)} %copy-done.19, f32[768]{0:T(1024)S(1)} %copy-done.16, f32[1024,768]{1,0:T(8,128)S(1)} %fusion.10, bf16[1024,1536]{1,0:T(8,128)(2,1)S(1)} %copy-done.24, ...), kind=kOutput, calls=%fused_computation.13 | convolution fusion | flops 2422208768 | bytes 13383680 | tf_op jit(solution)/shard_map/dot_general | solution.py:33
  202.3 31.9 %reduce-scatter.6.cloned.1.call-done = bf16[192,1920]{1,0:T(8,128)(2,1)} async-done(((bf16[768,1920]{1,0:T(8,128)(2,1)}), bf16[192,1920]{1,0:T(8,128)(2,1)}) %reduce-scatter.6.cloned.1.call-update) | async-done | bytes 737296 | tf_op jit(solution)/shard_map/reduce_scatter | solution.py:419
  234.2 0.0 all-reduce.8.cloned.1.call-update
  234.2 0.1 concatenate.11
  234.3 10.5 %all-reduce.4 = f32[11336]{0:T(1024)S(1)} all-reduce(f32[11336]{0:T(1024)S(1)} %concatenate.11), channel_id=5, replica_groups=mesh['dp'=8,'shard'=4] {'shard'}, use_global_device_ids=true, to_apply=%region_15.16.clone | all-reduce | flops 11336 | bytes 90688
  244.9 0.1 dynamic-slice.2
  244.9 38.4 %psum.31 = f32[2834]{0:T(1024)S(1)} all-reduce(f32[2834]{0:T(1024)S(1)} %dynamic-slice.2), channel_id=1, replica_groups=mesh['dp'=8,'shard'=4] {'dp'}, use_global_device_ids=true, to_apply=%region_16.17 | all-reduce | flops 2834 | bytes 22672 | tf_op jit(solution)/shard_map/psum | solution.py:472
  283.4 0.6 multiply_subtract_fusion.2
  284.0 4.6 %fusion.5 = f32[1,1024,768]{2,1,0:T(8,128)} fusion(f32[1024,768]{1,0:T(8,128)} %get-tuple-element.63, bf16[1,1024,768]{2,1,0:T(8,128)(2,1)S(1)} %copy-done.10, bf16[1,1024,768]{2,1,0:T(8,128)(2,1)S(1)} %copy-done.5, f32[1024]{0:T(1024)S(1)} %multiply_multiply_fusion.3, f32[768]{0:T(1024)S(1)} %copy-done.16, f32[1024]{0:T(1024)S(1)} %copy-done.19), kind=kLoop, calls=%fused_computation.15 | loop fusion | flops 6291456 | bytes 9448448 | tf_op jit(solution)/shard_map/reshape | solution.py:461
  288.6 3.7 %fusion.21 = bf16[1,1024,768]{2,1,0:T(8,128)(2,1)} fusion(bf16[1024,1536]{1,0:T(8,128)(2,1)S(1)} %copy-done.23, bf16[1536,768]{1,0:T(8,128)(2,1)S(1)} %copy-done.25, bf16[1,1024,768]{2,1,0:T(8,128)(2,1)S(1)} %copy-done.5), kind=kOutput, calls=%fused_computation.33 | convolution fusion | flops 2418278400 | bytes 8650752 | tf_op jit(solution)/shard_map/dot_general | solution.py:29
  292.3 43.9 %all-reduce.8.cloned.1.call-done = (bf16[192,1920]{1,0:T(8,128)(2,1)}, bf16[192,1536]{1,0:T(8,128)(2,1)}, bf16[384,768]{1,0:T(8,128)(2,1)}) async-done(((bf16[192,1920]{1,0:T(8,128)(2,1)}, bf16[192,1536]{1,0:T(8,128)(2,1)}, bf16[384,768]{1,0:T(8,128)(2,1)}), (bf16[192,1920]{1,0:T(8,128)(2,1)}, bf16[192,1536]{1,0:T(8,128)(2,1)}, bf16[384,768]{1,0:T(8,128)(2,1)})) %all-reduce.8.cloned.1.call-update) | async-done | bytes 1916944 | tf_op jit(solution)/shard_map/psum | solution.py:420
  336.2 4.6 %multiply_subtract_fusion.1 = (f32[384,768]{1,0:T(8,128)}, f32[384,768]{1,0:T(8,128)}, f32[384,768]{1,0:T(8,128)}, f32[384,768]{1,0:T(8,128)}) fusion(f32[384,768]{1,0:T(8,128)S(1)} %copy-done.6, f32[384,768]{1,0:T(8,128)} %param.18, f32[384,768]{1,0:T(8,128)} %param.19, bf16[384,768]{1,0:T(8,128)(2,1)} %get-tuple-element.44), kind=kLoop, calls=%fused_computation.36 | loop fusion | flops 4718592 | bytes 8847360 | tf_op jit(solution)/shard_map/sub | solution.py:415
  340.8 1.3 copy-done.8
  342.1 0.1 copy-done.11
  342.3 5.7 %multiply_subtract_fusion = (f32[192,3352]{1,0:T(8,128)}, f32[192,3352]{1,0:T(8,128)}, f32[192,3352]{1,0:T(8,128)}, f32[192,3352]{1,0:T(8,128)}) fusion(f32[192,3352]{1,0:T(8,128)S(1)} %copy-done.2, f32[192,3352]{1,0:T(8,128)S(1)} %copy-done.7, f32[192,3352]{1,0:T(8,128)S(1)} %copy-done.8, bf16[192,1816]{1,0:T(8,128)(2,1)S(1)} %bitcast.43, ...), kind=kLoop, calls=%fused_computation.24 | loop fusion | flops 12228096 | bytes 19307520 | tf_op jit(solution)/shard_map/sub | solution.py:415
  (64 shorter events, 0.3 us)
Async XLA Ops:
  7.2 30.0 %all-gather.5.cloned.1.call-start = ((), (), s32[]{:S(2)}) async-start(), calls=%async_computation.4 | async-start | bytes 2949120 | tf_op jit(solution)/shard_map/all_gather | solution.py:430
  9.4 70.8 %all-gather.3.cloned.1.call-start = ((), (), s32[]{:S(2)}) async-start(), calls=%async_computation.3 | async-start | bytes 6635520 | tf_op jit(solution)/shard_map/all_gather | solution.py:429
  11.3 1.3 copy-start.12
  11.4 1.3 copy-start.22
  11.4 17.3 %copy-start.3 = (bf16[1,1024,768]{2,1,0:T(8,128)(2,1)S(1)}, bf16[1,1024,768]{2,1,0:T(8,128)(2,1)}, u32[]{:S(2)}) copy-start(bf16[1,1024,768]{2,1,0:T(8,128)(2,1)} %param.11) | copy-start | bytes 4718596
  12.6 189.8 %reduce-scatter.8.cloned.1.call-start = ((), (), s32[]{:S(2)}) async-start(), calls=%async_computation.7 | async-start | bytes 2949120 | tf_op jit(solution)/shard_map/reduce_scatter | solution.py:419
  28.1 98.4 %copy-start.14 = (f32[768]{0:T(1024)}, f32[768]{0:T(1024)S(1)}, u32[]{:S(2)}) copy-start(f32[768]{0:T(1024)S(1)} %slice.49) | copy-start | bytes 9220
  29.1 97.5 %copy-start.17 = (f32[1024]{0:T(1024)}, f32[1024]{0:T(1024)S(1)}, u32[]{:S(2)}) copy-start(f32[1024]{0:T(1024)S(1)} %fusion.24) | copy-start | bytes 12292
  91.9 28.4 %copy-start.9 = (bf16[1,1024,768]{2,1,0:T(8,128)(2,1)S(1)}, bf16[1,1024,768]{2,1,0:T(8,128)(2,1)}, u32[]{:S(2)}) copy-start(bf16[1,1024,768]{2,1,0:T(8,128)(2,1)} %param.12) | copy-start | bytes 4718596
  126.3 76.0 %reduce-scatter.4.cloned.1.call-start = ((), (), s32[]{:S(2)}) async-start(), calls=%async_computation.5 | async-start | bytes 2949120 | tf_op jit(solution)/shard_map/reduce_scatter | solution.py:419
  133.2 101.0 %reduce-scatter.6.cloned.1.call-start = ((), (), s32[]{:S(2)}) async-start(), calls=%async_computation.6 | async-start | bytes 3686400 | tf_op jit(solution)/shard_map/reduce_scatter | solution.py:419
  133.2 47.5 %copy-start.4 = (bf16[1,1024,768]{2,1,0:T(8,128)(2,1)S(1)}, bf16[1,1024,768]{2,1,0:T(8,128)(2,1)}, u32[]{:S(2)}) copy-start(bf16[1,1024,768]{2,1,0:T(8,128)(2,1)} %param.11) | copy-start | bytes 4718596
  133.3 47.5 %copy-start.15 = (f32[768]{0:T(1024)S(1)}, f32[768]{0:T(1024)}, u32[]{:S(2)}) copy-start(f32[768]{0:T(1024)} %copy-done.14) | copy-start | bytes 9220
  133.3 47.5 %copy-start.18 = (f32[1024]{0:T(1024)S(1)}, f32[1024]{0:T(1024)}, u32[]{:S(2)}) copy-start(f32[1024]{0:T(1024)} %copy-done.17) | copy-start | bytes 12292
  180.1 0.6 copy-start
  187.8 1.1 copy-start.1
  187.9 148.3 %all-reduce.8.cloned.1.call-start = ((), (), s32[]{:S(2)}) async-start(), calls=%async_computation.8 | async-start | bytes 3833856 | tf_op jit(solution)/shard_map/psum | solution.py:420
  189.2 6.7 %copy-start.5 = (bf16[1,1024,768]{2,1,0:T(8,128)(2,1)S(1)}, bf16[1,1024,768]{2,1,0:T(8,128)(2,1)}, u32[]{:S(2)}) copy-start(bf16[1,1024,768]{2,1,0:T(8,128)(2,1)} %param.11) | copy-start | bytes 4718596
  189.2 6.7 %copy-start.16 = (f32[768]{0:T(1024)S(1)}, f32[768]{0:T(1024)}, u32[]{:S(2)}) copy-start(f32[768]{0:T(1024)} %copy-done.14) | copy-start | bytes 9220
  189.2 6.7 %copy-start.19 = (f32[1024]{0:T(1024)S(1)}, f32[1024]{0:T(1024)}, u32[]{:S(2)}) copy-start(f32[1024]{0:T(1024)} %copy-done.17) | copy-start | bytes 12292
  189.2 6.7 %copy-start.24 = (bf16[1024,1536]{1,0:T(8,128)(2,1)S(1)}, bf16[1024,1536]{1,0:T(8,128)(2,1)}, u32[]{:S(2)}) copy-start(bf16[1024,1536]{1,0:T(8,128)(2,1)} %get-tuple-element.28) | copy-start | bytes 9437188
  195.9 87.5 %copy-start.20 = (f32[2834]{0:T(1024)S(1)}, f32[2834]{0:T(1024)}, u32[]{:S(2)}) copy-start(f32[2834]{0:T(1024)} %param.20) | copy-start | bytes 34012
  195.9 87.5 %copy-start.21 = (f32[2834]{0:T(1024)S(1)}, f32[2834]{0:T(1024)}, u32[]{:S(2)}) copy-start(f32[2834]{0:T(1024)} %param.21) | copy-start | bytes 34012
  202.3 81.7 %copy-start.10 = (bf16[1,1024,768]{2,1,0:T(8,128)(2,1)S(1)}, bf16[1,1024,768]{2,1,0:T(8,128)(2,1)}, u32[]{:S(2)}) copy-start(bf16[1,1024,768]{2,1,0:T(8,128)(2,1)} %param.12) | copy-start | bytes 4718596
  283.3 5.3 %copy-start.13 = (f32[2834]{0:T(1024)}, f32[2834]{0:T(1024)S(1)}, u32[]{:S(2)}) copy-start(f32[2834]{0:T(1024)S(1)} %psum.31) | copy-start | bytes 34012
  284.0 4.6 %copy-start.23 = (bf16[1024,1536]{1,0:T(8,128)(2,1)S(1)}, bf16[1024,1536]{1,0:T(8,128)(2,1)}, u32[]{:S(2)}) copy-start(bf16[1024,1536]{1,0:T(8,128)(2,1)} %get-tuple-element.27) | copy-start | bytes 9437188
  284.0 4.6 %copy-start.25 = (bf16[1536,768]{1,0:T(8,128)(2,1)S(1)}, bf16[1536,768]{1,0:T(8,128)(2,1)}, u32[]{:S(2)}) copy-start(bf16[1536,768]{1,0:T(8,128)(2,1)} %all-gather.5.cloned.1.call-done) | copy-start | bytes 7077892
  288.6 47.6 %copy-start.6 = (f32[384,768]{1,0:T(8,128)S(1)}, f32[384,768]{1,0:T(8,128)}, u32[]{:S(2)}) copy-start(f32[384,768]{1,0:T(8,128)} %param.14) | copy-start | bytes 3538948
  336.2 4.6 %copy-start.2 = (f32[192,3352]{1,0:T(8,128)S(1)}, f32[192,3352]{1,0:T(8,128)}, u32[]{:S(2)}) copy-start(f32[192,3352]{1,0:T(8,128)} %param.13) | copy-start | bytes 7723012
  336.2 4.6 %copy-start.7 = (f32[192,3352]{1,0:T(8,128)S(1)}, f32[192,3352]{1,0:T(8,128)}, u32[]{:S(2)}) copy-start(f32[192,3352]{1,0:T(8,128)} %param.16) | copy-start | bytes 7723012
  336.2 5.9 %copy-start.8 = (f32[192,3352]{1,0:T(8,128)S(1)}, f32[192,3352]{1,0:T(8,128)}, u32[]{:S(2)}) copy-start(f32[192,3352]{1,0:T(8,128)} %param.17) | copy-start | bytes 7723012
  336.2 6.0 %copy-start.11 = (bf16[192,1920]{1,0:T(8,128)(2,1)S(1)}, bf16[192,1920]{1,0:T(8,128)(2,1)}, u32[]{:S(2)}) copy-start(bf16[192,1920]{1,0:T(8,128)(2,1)} %get-tuple-element.42) | copy-start | bytes 2211844
Sparse Core Ops, SparseCore 0:
  10.1 27.0 all-gather.4
  39.3 40.8 all-gather.2
  126.5 32.8 reduce-scatter.7
  162.3 32.8 reduce-scatter.3
  197.6 36.5 reduce-scatter.5
  237.9 98.2 all-reduce.7

commit v2 on v1

--- a/solution.py
+++ b/solution.py
@@ -1,3 +1,4 @@
+import functools
 import math
 import jax
 import jax.numpy as jnp
@@ -16,7 +17,7 @@
 CHANNELS = INNER + 2 * STATE
 Q = 128
 PAIRS = INNER // 128
-WIDTH = INNER + CHANNELS + 128
+WIDTH = INNER + CHANNELS + 256
 R_OFF = INNER + CHANNELS
 LOG2E = math.log2(math.e)
 f32 = jnp.float32
@@ -27,6 +28,10 @@
 
 def mm(a, b):
     return lax.dot_general(a, b, (((1,), (0,)), ((), ())), preferred_element_type=f32)
+
+
+def mm_rows(a, b):
+    return lax.dot_general(a, b, (((0,), (0,)), ((), ())), preferred_element_type=f32)
 
 
 def mm_t(a, b):
@@ -281,6 +286,7 @@
     dhp_ref[0] += fold8(dr)
     dhp_ref[1] += fold8(jnp.where(head, da * dt * -rate, 0.0))
     du_ref[:, CHANNELS : CHANNELS + 128] = dr.astype(bf16)
+    du_ref[:, CHANNELS + 128 :] = jnp.zeros((Q, 128), bf16)
 
 
 def selectors():
@@ -352,10 +358,10 @@
             whole((1, INNER)), whole((PAIRS, 512, 128)),
         ],
         out_specs=[
-            rows(CHANNELS + 128), whole((CONV, 8, CHANNELS)), whole((8, CHANNELS)), whole((2, 8, 128)), whole((8, INNER)),
+            rows(CHANNELS + 256), whole((CONV, 8, CHANNELS)), whole((8, CHANNELS)), whole((2, 8, 128)), whole((8, INNER)),
         ],
         out_shape=[
-            jax.ShapeDtypeStruct((length, CHANNELS + 128), bf16),
+            jax.ShapeDtypeStruct((length, CHANNELS + 256), bf16),
             jax.ShapeDtypeStruct((CONV, 8, CHANNELS), f32),
             jax.ShapeDtypeStruct((8, CHANNELS), f32),
             jax.ShapeDtypeStruct((2, 8, 128), f32),
@@ -371,6 +377,380 @@
         compiler_params=pltpu.CompilerParams(vmem_limit_bytes=48 * 1024 * 1024),
         name="mix_backward",
     )(proj, proj, ds, st, dt, cum, ps, cw, cb, hp, dsk, es)
+
+
+PIECES_OUT = 3
+PIECES_IN = 7
+PIECES = PIECES_OUT + PIECES_IN
+TALL = 192
+WIDE = 512
+HALF = TALL // 2
+NEAR = 4
+COVER_BACK = 4
+MESH = pl.DeviceIdType.MESH
+
+
+def reduce_kernel(
+    far,
+    normed_hbm, cot_hbm, mixer_hbm, dz_hbm, du_hbm, x_hbm, w_hbm, wo_hbm, gain_ref, vec_ref,
+    gin_hbm, gout_hbm, dx_hbm, out_hbm,
+    normed, cot, mixer, dproj, x, w, wo, dn, dgain,
+    dx, out,
+    g, rc, ry, rx, rz, rf, f,
+    in_sem, out_sem, dx_sem, res_sem,
+    cs, cr, ys, yr, xs, xr, zs, zr, fs, fr, gs, gr, hs, hr,
+):
+    dp = lax.axis_index("dp")
+    shard = lax.axis_index("shard")
+    xbit = dp % 2
+    zpos = dp // 2
+    near = zpos % NEAR
+    group = zpos // NEAR
+    core = shard % 2
+    ybit = shard // 2
+    core_id = {"dp": dp, "shard": ybit * 2 + (1 - core)}
+    y_id = {"dp": dp, "shard": (1 - ybit) * 2 + core}
+    x_id = {"dp": zpos * 2 + (1 - xbit), "shard": shard}
+
+    def near_id(k):
+        return {"dp": (group * NEAR + (near + k) % NEAR) * 2 + xbit, "shard": shard}
+
+    def far_id(k):
+        return {"dp": (((group + k) % far) * NEAR + near) * 2 + xbit, "shard": shard}
+
+    keep_rows = pl.ds(pl.multiple_of(xbit * HALF, 32), HALF)
+    give_rows = pl.ds(pl.multiple_of((1 - xbit) * HALF, 32), HALF)
+
+    def cols(k):
+        return pl.ds(pl.multiple_of(((near + k) % NEAR) * 128, 128), 128)
+
+    def remote(src, dst, send, recv, target):
+        return pltpu.make_async_remote_copy(
+            src_ref=src, dst_ref=dst, send_sem=send, recv_sem=recv, device_id=target, device_id_type=MESH
+        )
+
+    copies = [
+        pltpu.make_async_copy(mixer_hbm, mixer, in_sem.at[0]),
+        pltpu.make_async_copy(cot_hbm, cot, in_sem.at[1]),
+        pltpu.make_async_copy(normed_hbm, normed, in_sem.at[2]),
+        pltpu.make_async_copy(dz_hbm, dproj.at[:, 0:INNER], in_sem.at[3]),
+        pltpu.make_async_copy(du_hbm, dproj.at[:, INNER:], in_sem.at[4]),
+        pltpu.make_async_copy(w_hbm, w, in_sem.at[5]),
+        pltpu.make_async_copy(x_hbm, x, in_sem.at[6]),
+        pltpu.make_async_copy(wo_hbm, wo, in_sem.at[7]),
+    ]
+    for k in (0, 1, 6, 7, 2, 3, 4, 5):
+        copies[k].start()
+    peers = [core_id, y_id, x_id] + [near_id(k) for k in range(1, NEAR)] + [far_id(k) for k in range(1, far)]
+    barrier = pltpu.get_barrier_semaphore()
+    for peer in peers:
+        pl.semaphore_signal(barrier, inc=1, device_id=peer, device_id_type=MESH)
+    pl.semaphore_wait(barrier, len(peers))
+
+    def core_copy(p):
+        return remote(g.at[p, 1 - core], rc.at[p], cs.at[p], cr.at[p], core_id)
+
+    def y_copy(p):
+        return remote(g.at[p, core, 1 - ybit], ry.at[p], ys.at[p], yr.at[p], y_id)
+
+    def x_copy(p):
+        return remote(g.at[p, core, ybit, give_rows], rx.at[p], xs.at[p], xr.at[p], x_id)
+
+    def z_copy(p, k):
+        return remote(
+            g.at[p, core, ybit, keep_rows, cols(k)], rz.at[p, NEAR - 1 - k], zs.at[p, k - 1], zr.at[p, NEAR - 1 - k],
+            near_id(k),
+        )
+
+    def z_arrival(p, k):
+        return remote(
+            g.at[p, core, ybit, keep_rows, cols(k)], rz.at[p, k - 1], zs.at[p, k - 1], zr.at[p, k - 1], near_id(k)
+        )
+
+    def far_copy(p, k):
+        return remote(
+            f.at[p, keep_rows, cols(0)], rf.at[p, far - 1 - k], hs.at[p, k - 1], hr.at[p, far - 1 - k], far_id(k)
+        )
+
+    def far_arrival(p, k):
+        return remote(f.at[p, keep_rows, cols(0)], rf.at[p, k - 1], hs.at[p, k - 1], hr.at[p, k - 1], far_id(k))
+
+    def spread_copy(p, k):
+        return remote(
+            f.at[p, keep_rows, cols(0)], f.at[p, keep_rows, cols(0)], fs.at[p, k - 1], fr.at[p, NEAR - 1 - k],
+            near_id(k),
+        )
+
+    def spread_arrival(p, k):
+        return remote(
+            f.at[p, keep_rows, cols(k)], f.at[p, keep_rows, cols(k)], fs.at[p, k - 1], fr.at[p, k - 1], near_id(k)
+        )
+
+    def pair_copy(p):
+        return remote(f.at[p, keep_rows], f.at[p, keep_rows], gs.at[p], gr.at[p], x_id)
+
+    def pair_arrival(p):
+        return remote(f.at[p, give_rows], f.at[p, give_rows], gs.at[p], gr.at[p], x_id)
+
+    def result_out(p, h):
+        return pltpu.make_async_copy(
+            f.at[p, :, 256 * h : 256 * h + 256],
+            gout_hbm.at[TALL * h : TALL * h + TALL, pl.ds(pl.multiple_of(p * 256, 256), 256)],
+            res_sem.at[p, h],
+        )
+
+    def result_in(p):
+        return pltpu.make_async_copy(
+            f.at[p],
+            gin_hbm.at[:, pl.ds(pl.multiple_of((p - PIECES_OUT) * WIDE, WIDE), WIDE)],
+            res_sem.at[p, 0],
+        )
+
+    def compute_out(p):
+        right = cot[:, pl.ds(pl.multiple_of(p * 256, 256), 256)]
+        for owner in range(4):
+            left = mixer[:, 2 * TALL * owner : 2 * TALL * (owner + 1)]
+            value = mm_rows(left, right).astype(bf16)
+            for h in range(2):
+                g[p, owner % 2, owner // 2, :, 256 * h : 256 * h + 256] = value[TALL * h : TALL * h + TALL]
+
+    def compute_in(p):
+        right = dproj[:, pl.ds(pl.multiple_of((p - PIECES_OUT) * WIDE, WIDE), WIDE)]
+        value = mm_rows(normed[...], right).astype(bf16)
+        for owner in range(4):
+            g[p, owner % 2, owner // 2] = value[TALL * owner : TALL * (owner + 1)]
+
+    def compute_small():
+        pieces = [dgain_row(k) for k in range(D // 128)] + [jnp.zeros((16 - D // 128, 128), f32)]
+        block = jnp.concatenate(pieces, axis=0).astype(bf16)
+        for owner in range(4):
+            g[PIECES - 1, owner % 2, owner // 2, :, WIDE - 128 :] = jnp.zeros((TALL, 128), bf16)
+            g[PIECES - 1, owner % 2, owner // 2, 0:32, WIDE - 128 :] = vec_ref[owner].astype(bf16)
+            g[PIECES - 1, owner % 2, owner // 2, 32:48, WIDE - 128 :] = block
+
+    def dgain_row(k):
+        return jnp.sum(dgain[:, 128 * k : 128 * k + 128], axis=0, keepdims=True)
+
+    def cover_back(n):
+        rows = pl.ds(pl.multiple_of(n * 256, 256), 256)
+        dn[...] = mm_t(dproj[rows, :], w[...])
+
+        def part(k, _):
+            sub = pl.ds(pl.multiple_of(k * 32, 32), 32)
+            here = pl.ds(pl.multiple_of(n * 256 + k * 32, 32), 32)
+            d = dn[sub, :]
+            xv = x[here, :].astype(f32)
+            factor = lax.rsqrt(jnp.mean(xv * xv, axis=1, keepdims=True) + norm_epsilon)
+            t = d * gain_ref[...]
+            back = jnp.mean(t * xv, axis=1, keepdims=True) * (factor * factor * factor)
+            dx[here, :] = cot[here, :].astype(f32) + (factor * t - back * xv)
+            dgain[...] += (d * (xv * factor)).reshape(4, 8, D).sum(axis=0)
+            return 0
+
+        lax.fori_loop(0, 8, part, 0)
+        result_dx(n).start()
+
+    def cover_out(n):
+        rows = pl.ds(pl.multiple_of(n * 256, 256), 256)
+        out[rows, :] = (x[rows, :].astype(f32) + mm(mixer[rows, :], wo[...])).astype(bf16)
+        result_rows(n).start()
+
+    def result_dx(n):
+        rows = pl.ds(pl.multiple_of(n * 256, 256), 256)
+        return pltpu.make_async_copy(dx.at[rows], dx_hbm.at[rows], dx_sem.at[n])
+
+    def result_rows(n):
+        rows = pl.ds(pl.multiple_of(n * 256, 256), 256)
+        return pltpu.make_async_copy(out.at[rows], out_hbm.at[rows], out_sem.at[n])
+
+    tiles = x.shape[0] // 256
+    dgain[...] = jnp.zeros_like(dgain)
+    copies[0].wait()
+    copies[1].wait()
+
+    def slot(i, _):
+        @pl.when(i < PIECES_OUT)
+        def _():
+            compute_out(i)
+
+        @pl.when(i == PIECES_OUT)
+        def _():
+            copies[2].wait()
+            copies[3].wait()
+            copies[4].wait()
+
+        @pl.when((i >= PIECES_OUT) & (i < PIECES))
+        def _():
+            compute_in(i)
+
+        @pl.when(i == PIECES - 1)
+        def _():
+            compute_small()
+
+        @pl.when(i < PIECES)
+        def _():
+            core_copy(i).start()
+
+        @pl.when(i == 0)
+        def _():
+            for copy in copies[6:8]:
+                copy.wait()
+
+        @pl.when(i < COVER_BACK)
+        def _():
+            lax.fori_loop(0, per_out, lambda k, c: (cover_out(i * per_out + k), c)[1], 0)
+
+        @pl.when(i == COVER_BACK)
+        def _():
+            copies[5].wait()
+
+        @pl.when((i >= COVER_BACK) & (i < COVER_BACK + 4))
+        def _():
+            lax.fori_loop(0, per_back, lambda k, c: (cover_back((i - COVER_BACK) * per_back + k), c)[1], 0)
+
+        @pl.when(i < PIECES)
+        def _():
+            core_copy(i).wait_recv()
+            give = 1 - ybit
+            g[i, core, give] = (g[i, core, give].astype(f32) + rc[i, give].astype(f32)).astype(bf16)
+            y_copy(i).start()
+
+        p1 = i - 1
+
+        @pl.when((p1 >= 0) & (p1 < PIECES))
+        def _():
+            y_copy(p1).wait_recv()
+            total = g[p1, core, ybit].astype(f32) + rc[p1, ybit].astype(f32) + ry[p1].astype(f32)
+            g[p1, core, ybit] = total.astype(bf16)
+            x_copy(p1).start()
+
+        p2 = i - 2
+
+        @pl.when((p2 >= 0) & (p2 < PIECES))
+        def _():
+            x_copy(p2).wait_recv()
+            g[p2, core, ybit, keep_rows] = (
+                g[p2, core, ybit, keep_rows].astype(f32) + rx[p2].astype(f32)
+            ).astype(bf16)
+            for k in range(1, NEAR):
+                z_copy(p2, k).start()
+
+        p3 = i - 3
+
+        @pl.when((p3 >= 0) & (p3 < PIECES))
+        def _():
+            total = g[p3, core, ybit, keep_rows, cols(0)].astype(f32)
+            for k in range(1, NEAR):
+                z_arrival(p3, k).wait_recv()
+                total = total + rz[p3, k - 1].astype(f32)
+            f[p3, keep_rows, cols(0)] = total.astype(bf16)
+            if far > 1:
+                for k in range(1, far):
+                    far_copy(p3, k).start()
+                for k in range(1, far):
+                    far_copy(p3, k).wait_send()
+                    far_arrival(p3, k).wait_recv()
+                    total = total + rf[p3, k - 1].astype(f32)
+                f[p3, keep_rows, cols(0)] = total.astype(bf16)
+            for k in range(1, NEAR):
+                spread_copy(p3, k).start()
+
+        p4 = i - 4
+
+        @pl.when((p4 >= 0) & (p4 < PIECES))
+        def _():
+            for k in range(1, NEAR):
+                spread_arrival(p4, k).wait_recv()
+            pair_copy(p4).start()
+
+        p5 = i - 5
+
+        @pl.when((p5 >= 0) & (p5 < PIECES))
+        def _():
+            pair_arrival(p5).wait_recv()
+
+        @pl.when((p5 >= 0) & (p5 < PIECES_OUT))
+        def _():
+            for h in range(2):
+                result_out(p5, h).start()
+
+        @pl.when((p5 >= PIECES_OUT) & (p5 < PIECES))
+        def _():
+            result_in(p5).start()
+
+        return 0
+
+    per_out = (tiles + COVER_BACK - 1) // COVER_BACK
+    per_back = tiles // 4
+    lax.fori_loop(0, PIECES + 5, slot, 0)
+
+    def drain(p, _):
+        core_copy(p).wait_send()
+        y_copy(p).wait_send()
+        x_copy(p).wait_send()
+        for k in range(1, NEAR):
+            z_copy(p, k).wait_send()
+            spread_copy(p, k).wait_send()
+        pair_copy(p).wait_send()
+        return 0
+
+    lax.fori_loop(0, PIECES, drain, 0)
+    for p in range(PIECES_OUT):
+        for h in range(2):
+            result_out(p, h).wait()
+    for p in range(PIECES_OUT, PIECES):
+        result_in(p).wait()
+    for n in range(tiles):
+        result_dx(n).wait()
+        result_rows(n).wait()
+
+
+def reduce_grads(mesh_dp, normed, cot, mixer, dz, du, x, w, wo, gain, vec):
+    length = x.shape[0]
+    far = mesh_dp // 2 // NEAR
+    any_space = pl.BlockSpec(memory_space=pl.ANY)
+    vmem = pl.BlockSpec(memory_space=pltpu.VMEM)
+    dma = pltpu.SemaphoreType.DMA
+    return pl.pallas_call(
+        functools.partial(reduce_kernel, far),
+        in_specs=[any_space] * 8 + [vmem] * 2,
+        out_specs=[any_space] * 4,
+        out_shape=[
+            jax.ShapeDtypeStruct((TALL, PIECES_IN * WIDE), bf16),
+            jax.ShapeDtypeStruct((2 * TALL, D), bf16),
+            jax.ShapeDtypeStruct((length, D), f32),
+            jax.ShapeDtypeStruct((length, D), bf16),
+        ],
+        scratch_shapes=[
+            pltpu.VMEM((length, D), bf16),
+            pltpu.VMEM((length, D), bf16),
+            pltpu.VMEM((length, INNER), bf16),
+            pltpu.VMEM((length, WIDTH), bf16),
+            pltpu.VMEM((length, D), bf16),
+            pltpu.VMEM((D, WIDTH), bf16),
+            pltpu.VMEM((INNER, D), bf16),
+            pltpu.VMEM((256, D), f32),
+            pltpu.VMEM((8, D), f32),
+            pltpu.VMEM((length, D), f32),
+            pltpu.VMEM((length, D), bf16),
+            pltpu.VMEM((PIECES, 2, 2, TALL, WIDE), bf16),
+            pltpu.VMEM((PIECES, 2, TALL, WIDE), bf16),
+            pltpu.VMEM((PIECES, TALL, WIDE), bf16),
+            pltpu.VMEM((PIECES, HALF, WIDE), bf16),
+            pltpu.VMEM((PIECES, NEAR - 1, HALF, 128), bf16),
+            pltpu.VMEM((PIECES, max(far - 1, 1), HALF, 128), bf16),
+            pltpu.VMEM((PIECES, TALL, WIDE), bf16),
+            dma((8,)), dma((length // 256,)), dma((length // 256,)), dma((PIECES, 2)),
+            dma((PIECES,)), dma((PIECES,)), dma((PIECES,)), dma((PIECES,)), dma((PIECES,)), dma((PIECES,)),
+            dma((PIECES, NEAR - 1)), dma((PIECES, NEAR - 1)), dma((PIECES, NEAR - 1)), dma((PIECES, NEAR - 1)),
+            dma((PIECES,)), dma((PIECES,)),
+            dma((PIECES, max(far - 1, 1))), dma((PIECES, max(far - 1, 1))),
+        ],
+        compiler_params=pltpu.CompilerParams(
+            collective_id=1, has_side_effects=True, vmem_limit_bytes=64 * 1024 * 1024 - 256 * 1024
+        ),
+        name="reduce_grads",
+    )(normed, cot, mixer, dz, du, x, w, wo, gain, vec)
 
 beta_first = 0.9
 beta_second = 0.95
@@ -394,10 +774,6 @@
     return pieces
 
 
-def mm_rows(left, right):
-    return lax.dot_general(left, right, (((0,), (0,)), ((), ())), preferred_element_type=f32)
-
-
 def prenorm(values, gain_values):
     return (
         values
@@ -413,11 +789,6 @@
     fix_second = 1.0 - beta_second**STEP_COUNT
     update = new_first / fix_first / (jnp.sqrt(new_second / fix_second) + adam_epsilon)
     return (param - rate * (update + decay * param), new_first, new_second)
-
-
-def reduce_grad(grad):
-    part = lax.psum_scatter(grad.astype(bf16), "shard", scatter_dimension=0, tiled=True)
-    return lax.psum(part, "dp")
 
 
 def shards(
@@ -434,10 +805,10 @@
     dsk = jnp.repeat(d_skip, HEADDIM)[None, :]
     es = selectors()
     seqs_here, length, width = inputs.shape
-    rows = inputs.astype(f32).reshape(seqs_here * length, width)
+    rows_low = inputs.reshape(seqs_here * length, width)
+    rows = rows_low.astype(f32)
     cot = cotangent.reshape(seqs_here * length, width)
-    normed, prenorm_back = jax.vjp(prenorm, rows, gain)
-    normed_low = normed.astype(bf16)
+    normed_low = prenorm(rows, gain).astype(bf16)
     proj = mm(normed_low, w_all)
     dmix = mm_t(cot, w_out_all)
     forward = []
@@ -446,20 +817,12 @@
         forward.append(mix_forward(proj[part], dmix[part], conv_w, conv_b[None], hp, dsk, norm_w[None], es))
     mixer_low = jnp.concatenate([f[0] for f in forward], axis=0)
     dz = jnp.concatenate([f[1] for f in forward], axis=0)
-    outputs = (rows + mm(mixer_low, w_out_all)).astype(bf16).reshape(inputs.shape)
-    grad_out = reduce_grad(mm_rows(mixer_low, cot))
-    grad_z = reduce_grad(mm_rows(normed_low, dz))
     backward = []
     for n in range(seqs_here):
         part = slice(n * length, (n + 1) * length)
         _, _, ds, st, dt, cum, ps, _ = forward[n]
         backward.append(mix_backward(proj[part], ds, st, dt, cum, ps, conv_w, conv_b[None], hp, dsk, es))
     du = jnp.concatenate([b[0] for b in backward], axis=0)
-    grad_u = reduce_grad(mm_rows(normed_low, du))
-    d_normed = mm_t(dz, w_all[:, :INNER]) + mm_t(du, w_all[:, INNER:])
-    d_rows, d_gain = prenorm_back(d_normed)
-    input_grad = (cot.astype(f32) + d_rows).reshape(inputs.shape)
-
     def total(values):
         return sum(values[1:], values[0])
 
@@ -468,10 +831,20 @@
     dhp = total([b[3] for b in backward]).sum(axis=1)
     dskip = total([b[4] for b in backward]).sum(axis=0).reshape(HEADS, HEADDIM).sum(axis=1)
     dnw = total([f[7] for f in forward]).sum(axis=0)
-    small = jnp.concatenate([dcw.reshape(-1), dcb, dhp[0, :HEADS], dhp[1, :HEADS], dskip, dnw, d_gain])
-    grad_vec = lax.psum(lax.psum_scatter(small, "shard", scatter_dimension=0, tiled=True), "dp")
-    grad_in = jnp.concatenate([grad_z.astype(f32), grad_u.astype(f32)[:, : in_width - INNER]], axis=1)
-    grad_out = grad_out.astype(f32)
+    small = jnp.concatenate([dcw.reshape(-1), dcb, dhp[0, :HEADS], dhp[1, :HEADS], dskip, dnw, jnp.zeros((D,), f32)])
+    owners = small.shape[0] // vec_len
+    small = jnp.pad(small.reshape(owners, vec_len), ((0, 0), (0, 32 * 128 - vec_len))).reshape(owners, 32, 128)
+    gin, gout, input_grad, outputs = reduce_grads(
+        lax.axis_size("dp"), normed_low, cot, mixer_low, dz, du, rows_low, w_all, w_out_all, gain[None], small
+    )
+    outputs = outputs.reshape(inputs.shape)
+    input_grad = input_grad.reshape(inputs.shape)
+    tail = gin[:, WIDTH - 128 :].astype(f32)
+    gain_grad = jnp.pad(tail[32 : 32 + D // 128].reshape(D), (owners * vec_len - D, 0))
+    start = lax.axis_index("shard") * vec_len
+    grad_vec = tail[:32].reshape(32 * 128)[:vec_len] + lax.dynamic_slice(gain_grad, (start,), (vec_len,))
+    grad_in = gin[:, :in_width].astype(f32)
+    grad_out = gout.astype(f32)
     new_w_in, new_first_in, new_second_in = adam(w_in, grad_in, first_in, second_in, rate_matrix, decay_matrix)
     new_w_out, new_first_out, new_second_out = adam(
         w_out, grad_out, first_out, second_out, rate_matrix, decay_matrix

time: 355 us -> 271 us (0.76)
  Pallas kernels: 75.2 us -> 153 us
  waiting for transfers between devices: 118 us -> 41.6 us
  blocking collectives: 62.7 us -> 13.8 us
  matrix products: 55.4 us -> 19 us
    pallas_call x0 -> x1, Pallas kernels: none -> 77.1 us  [reduce_grads(): pl.pallas_call(functools.partial(reduce_kernel, far), in_specs=[any_space...]
    psum x1 -> x0, waiting for transfers between devices: 43.9 us -> none  [reduce_grad(): return lax.psum(part, 'dp')]
    psum x1 -> x0, blocking collectives: 38.4 us -> none  [shards(): lax.psum(lax.psum_scatter(small, 'shard', scatter_dimension=0, tiled=True...]
    reduce_scatter x3 -> x0, waiting for transfers between devices: 31.9 us -> none  [reduce_grad(): lax.psum_scatter(grad.astype(bf16), 'shard', scatter_dimension=0, tiled=T...]
    dot_general x3 -> x0, matrix products: 19.6 us -> none  [mm_rows(): lax.dot_general(left, right, (((0,), (0,)), ((), ())), preferred_element_...]
    dot_general x3 -> x1, matrix products: 20.4 us -> 7.35 us  [mm_t(): lax.dot_general(a, b, (((1,), (1,)), ((), ())), preferred_element_type=f32)]
    unnamed x2 -> x1, blocking collectives: 24.4 us -> 13.8 us
    reshape x1 -> x0, other arithmetic: 4.59 us -> none  [shards(): input_grad = (cot.astype(f32) + d_rows).reshape(inputs.shape)]
  transfers between devices with their start and end apart: 6 -> 2, of which waited for: 4 -> 2; matrix products, arithmetic and copies ran while one was open for 14% -> 6% of each run, Pallas kernels for 13% -> 0%
where the time goes in v2:
time: 271 us; the launch traced here: 270 us
  Pallas kernels  153 us (56%)
  waiting for transfers between devices  41.6 us (15%)
  other arithmetic  19.9 us (7%)
  matrix products  19 us (7%)
  between operations  15 us (6%)
  blocking collectives  13.8 us (5%)
  local copies, waits for them, and re-layouts  7.6 us (3%)
    pallas_call x1, Pallas kernels, reduce_grads(): pl.pallas_call(functools.partial(reduce_kernel, far), in_specs=[any_space...  77.1 us
    pallas_call x1, Pallas kernels, mix_backward(): pl.pallas_call(backward_kernel, grid=(blocks,), in_specs=[rows(WIDTH), pl...  47.5 us
    all_gather x1, waiting for transfers between devices, shards(): w_all = lax.all_gather(w_in_low, 'shard', axis=0, tiled=True)  36.8 us
    pallas_call x1, Pallas kernels, mix_forward(): pl.pallas_call(forward_kernel, grid=(blocks,), in_specs=[rows(WIDTH), row...  28.7 us
    unnamed x1, blocking collectives  13.8 us
    dot_general x1, matrix products, mm(): lax.dot_general(a, b, (((1,), (0,)), ((), ())), preferred_element_type=f32)  11.6 us
    sub x3, other arithmetic, adam(): return (param - rate * (update + decay * param), new_first, new_second)  11.5 us
    dot_general x1, matrix products, mm_t(): lax.dot_general(a, b, (((1,), (1,)), ((), ())), preferred_element_type=f32)  7.35 us
  transfers between devices with their start and end apart: 2, of which 2 were waited for; matrix products, arithmetic and copies ran while one was open for 6% of the time, Pallas kernels for 0%

profile of v2, /device:TPU:0, one launch (start us, length us, event | category | flops | bytes accessed | tf_op | source)
XLA Modules:
  0.0 270.2 jit_solution(10098625557333152332)
XLA Ops:
  7.2 0.0 all-gather.5.cloned.1.call-start
  7.2 2.1 convert_element_type.46
  9.4 0.0 all-gather.5.cloned.1.call-update
  9.4 0.0 all-gather.3.cloned.1.call-start
  9.4 1.9 convert_element_type.45
  11.3 0.0 copy-start.8
  11.3 0.0 copy-start.11
  11.4 0.0 copy-start
  11.4 1.2 pad.19
  12.6 0.0 all-gather.3.cloned.1.call-update
  12.6 0.0 copy-done.8
  12.6 0.0 copy-done.11
  12.6 0.6 dynamic-slice
  13.9 0.3 dynamic-update-slice
  14.2 13.8 %all-reduce.5 = bf16[11336]{0:T(1024)(128)(2,1)S(1)} all-reduce(bf16[11336]{0:T(1024)(128)(2,1)S(1)} %dynamic-update-slice), channel_id=1, replica_groups=mesh['dp'=8,'shard'=4] {'shard'}, use_global_device_ids=true, to_apply=%add.5 | all-reduce | flops 11336 | bytes 45344
  28.0 0.1 slice.56
  28.1 0.1 slice.62
  28.2 0.1 pad.26.clone
  28.2 0.1 pad.27.clone
  28.3 0.1 fusion.19
  28.4 0.1 broadcast_in_dim.52
  28.5 0.1 broadcast_in_dim_reshape.3.dsk_ref
  28.6 0.6 broadcast_in_dim.58.gain_ref
  29.2 0.0 copy-done
  29.2 0.4 fusion
  29.6 0.1 maximum_maximum_fusion.hp_ref
  29.6 0.1 add_add_fusion
  29.7 1.1 fusion.3.es_ref
  30.8 1.6 fusion.2.normed_hbm
  32.4 4.8 %all-gather.5.cloned.1.call-done.wo_hbm = bf16[1536,768]{1,0:T(8,128)(2,1)} async-done(((bf16[384,768]{1,0:T(8,128)(2,1)}), bf16[1536,768]{1,0:T(8,128)(2,1)}) %all-gather.5.cloned.1.call-update) | async-done | bytes 2359312 | tf_op jit(solution)/shard_map/all_gather | solution.py:801
  37.2 7.3 %fusion.13.dmix_ref = f32[1024,1536]{1,0:T(8,128)} fusion(bf16[1536,768]{1,0:T(8,128)(2,1)} %all-gather.5.cloned.1.call-done.wo_hbm, bf16[1,1024,768]{2,1,0:T(8,128)(2,1)} %param.12), kind=kOutput, calls=%fused_computation.46 | convolution fusion | flops 2415919104 | bytes 10223616 | tf_op jit(solution)/shard_map/dot_general | solution.py:38
  44.5 36.8 %all-gather.3.cloned.1.call-done.w_hbm = bf16[768,3584]{1,0:T(8,128)(2,1)} async-done(((bf16[192,3584]{1,0:T(8,128)(2,1)}), bf16[768,3584]{1,0:T(8,128)(2,1)}) %all-gather.3.cloned.1.call-update) | async-done | bytes 5505040 | tf_op jit(solution)/shard_map/all_gather | solution.py:800
  81.3 0.0 copy-done.1
  81.3 11.6 %fusion.20.proj_ref.prev_ref = f32[1024,3584]{1,0:T(8,128)} fusion(bf16[1024,768]{1,0:T(8,128)(2,1)S(1)} %copy-done.1, bf16[768,3584]{1,0:T(8,128)(2,1)} %all-gather.3.cloned.1.call-done.w_hbm), kind=kOutput, calls=%fused_computation.49 | convolution fusion | flops 5637144576 | bytes 21757952 | tf_op jit(solution)/shard_map/dot_general | solution.py:30
  93.0 28.7 %mix_forward.1 = (bf16[1024,1536]{1,0:T(8,128)(2,1)}, bf16[1024,1536]{1,0:T(8,128)(2,1)}, bf16[1024,1536]{1,0:T(8,128)(2,1)}, bf16[8,128,1536]{2,1,0:T(8,128)(2,...) custom-call(f32[1024,3584]{1,0:T(8,128)} %fusion.20.proj_ref.prev_ref, ...), custom_call_target="tpu_custom_call" | custom-call | tf_op jit(solution)/shard_map/mix_forward/pallas_call | solution.py:311
  121.7 47.5 %mix_backward.1 = (bf16[1024,2048]{1,0:T(8,128)(2,1)}, f32[4,8,1792]{2,1,0:T(8,128)S(1)}, f32[8,1792]{1,0:T(8,128)S(1)}, f32[2,8,128]{2,1,0:T(8,128)S(1)}, f32[8,1536]{1,0:T(8,128)S(1)}) custom-call(f32[1024,3584]{1,0:T(8,128)} %fusion.20.proj_ref.prev_ref, f32[1024,3584]{1,0:T(8,128)} %fusion.20.proj_ref.prev_ref, ...), custom_call_target="tpu_custom_call" | custom-call | tf_op jit(solution)/shard_map/mix_backward/pallas_call | solution.py:349
  169.2 0.1 reduce_sum.64
  169.3 0.1 reshape.138
  169.4 0.1 reduce_sum.68
  169.6 0.1 concatenate.3
  169.7 0.1 reshape.139
  169.8 0.6 copy.27
  170.4 77.1 %reduce_grads.1 = (bf16[192,3584]{1,0:T(8,128)(2,1)}, bf16[384,768]{1,0:T(8,128)(2,1)}, f32[1024,768]{1,0:T(8,128)}, bf16[1024,768]{1,0:T(8,128)(2,1)}) custom-call(bf16[1024,768]{1,0:T(8,128)(2,1)} %fusion.2.normed_hbm, bf16[1024,768]{1,0:T(8,128)(2,1)} %bitcast.31, bf16[1024,1536]{1,0:T(8,128)(2,1)} %get-tuple-element.31.mixer_hbm, ...), custom_call_target="tpu_custom_call" | custom-call | tf_op jit(solution)/shard_map/reduce_grads/pallas_call | solution.py:714
  247.5 0.8 slice_convert_fusion.1
  248.3 0.0 copy-start.2
  248.3 0.0 copy-start.5
  248.4 0.0 copy-start.6
  248.4 0.0 copy-start.7
  248.4 8.4 %multiply_subtract_fusion = (f32[192,3352]{1,0:T(8,128)}, f32[192,3352]{1,0:T(8,128)}, f32[192,3352]{1,0:T(8,128)}, f32[192,3352]{1,0:T(8,128)}) fusion(f32[192,3352]{1,0:T(8,128)} %param.13, f32[192,3352]{1,0:T(8,128)} %param.16, f32[192,3352]{1,0:T(8,128)} %param.17, bf16[192,3584]{1,0:T(8,128)(2,1)} %get-tuple-element.46), kind=kLoop, calls=%fused_computation.9 | loop fusion | flops 10297344 | bytes 19307520 | tf_op jit(solution)/shard_map/sub | solution.py:791
  256.7 0.0 copy-done.2
  256.8 0.0 copy-done.5
  256.8 0.0 copy-done.6
  256.8 0.0 copy-done.7
  256.8 0.0 copy-start.9
  256.8 0.0 copy-start.10
  256.8 0.0 copy-start.4
  256.8 2.4 multiply_subtract_fusion.1
  259.2 0.0 copy-done.9
  259.2 0.0 copy-done.10
  259.2 0.7 multiply_subtract_fusion.2
  260.0 0.0 copy-done.4
  260.0 1.1 copy.31
  261.1 0.6 copy-done.3
  261.7 1.7 copy.32
  (25 shorter events, 0.2 us)
Async XLA Ops:
  7.2 30.0 %all-gather.5.cloned.1.call-start = ((), (), s32[]{:S(2)}) async-start(), calls=%async_computation.1 | async-start | bytes 2949120 | tf_op jit(solution)/shard_map/all_gather | solution.py:801
  9.4 71.9 %all-gather.3.cloned.1.call-start = ((), (), s32[]{:S(2)}) async-start(), calls=%async_computation | async-start | bytes 6881280 | tf_op jit(solution)/shard_map/all_gather | solution.py:800
  11.3 1.2 copy-start.8
  11.3 1.3 copy-start.11
  11.4 17.8 %copy-start = (bf16[1,1024,768]{2,1,0:T(8,128)(2,1)S(1)}, bf16[1,1024,768]{2,1,0:T(8,128)(2,1)}, u32[]{:S(2)}) copy-start(bf16[1,1024,768]{2,1,0:T(8,128)(2,1)} %param.11) | copy-start | bytes 4718596
  32.4 48.9 %copy-start.1 = (bf16[1024,768]{1,0:T(8,128)(2,1)S(1)}, bf16[1024,768]{1,0:T(8,128)(2,1)}, u32[]{:S(2)}) copy-start(bf16[1024,768]{1,0:T(8,128)(2,1)} %fusion.2.normed_hbm) | copy-start | bytes 4718596
  248.3 8.4 %copy-start.2 = (f32[384,768]{1,0:T(8,128)S(1)}, f32[384,768]{1,0:T(8,128)}, u32[]{:S(2)}) copy-start(f32[384,768]{1,0:T(8,128)} %param.14) | copy-start | bytes 3538948
  248.3 8.4 %copy-start.5 = (f32[384,768]{1,0:T(8,128)S(1)}, f32[384,768]{1,0:T(8,128)}, u32[]{:S(2)}) copy-start(f32[384,768]{1,0:T(8,128)} %param.18) | copy-start | bytes 3538948
  248.4 8.4 %copy-start.6 = (f32[384,768]{1,0:T(8,128)S(1)}, f32[384,768]{1,0:T(8,128)}, u32[]{:S(2)}) copy-start(f32[384,768]{1,0:T(8,128)} %param.19) | copy-start | bytes 3538948
  248.4 8.4 %copy-start.7 = (bf16[384,768]{1,0:T(8,128)(2,1)S(1)}, bf16[384,768]{1,0:T(8,128)(2,1)}, u32[]{:S(2)}) copy-start(bf16[384,768]{1,0:T(8,128)(2,1)} %get-tuple-element.47) | copy-start | bytes 1769476
  256.8 2.5 copy-start.9
  256.8 2.5 copy-start.10
  256.8 3.2 %copy-start.4 = (bf16[1024,768]{1,0:T(8,128)(2,1)S(1)}, bf16[1024,768]{1,0:T(8,128)(2,1)}, u32[]{:S(2)}) copy-start(bf16[1024,768]{1,0:T(8,128)(2,1)} %get-tuple-element.44) | copy-start | bytes 4718596
  259.2 2.5 copy-start.3
Sparse Core Ops, SparseCore 0:
  10.1 27.0 all-gather.4
  39.3 41.9 all-gather.2

commit v3 on v2

--- a/solution.py
+++ b/solution.py
@@ -752,34 +752,284 @@
         name="reduce_grads",
     )(normed, cot, mixer, dz, du, x, w, wo, gain, vec)
 
+
+GROUPS_OUT = 3
+GROUPS = GROUPS_OUT + WIDTH // 512
+VEC_ROWS = 32
+
+
+def flat_row(v, vec_len, start):
+    lane = lax.broadcasted_iota(jnp.int32, (1, 128), 1)
+    out = None
+    done = 0
+    while done < 128:
+        owner, local = (start + done) // vec_len, (start + done) % vec_len
+        if owner >= v.shape[0]:
+            break
+        r, off = local // 128, local % 128
+        count = min(128 - done, 128 - off, vec_len - local)
+        piece = v[owner, r : r + 1, :]
+        shift = (done - off) % 128
+        if shift:
+            piece = pltpu.roll(piece, shift, 1)
+        out = piece if out is None else jnp.where(lane >= done, piece, out)
+        done += count
+    return out
+
+
+def gather_kernel(
+    vec_len,
+    x_hbm, cot_hbm, win_hbm, wout_hbm, vec_ref,
+    proj_hbm, dmix_hbm, normed_hbm, w_hbm, wo_hbm, cw_ref, cb_ref, hp_ref, dsk_ref, nw_ref, gain_ref,
+    x, cot, normed, win, wout, w, wo, v, stage, dstage,
+    in_sem, proj_sem, dmix_sem, keep_sem, w_sem,
+    cs, cr, vs, vr, ys, yr, xs, xr, as_, ar, bs, br,
+):
+    dp = lax.axis_index("dp")
+    shard = lax.axis_index("shard")
+    xbit = dp % 2
+    core = shard % 2
+    ybit = shard // 2
+    near = ybit * 2 + (1 - core)
+    across = (1 - ybit) * 2 + core
+    diagonal = (1 - ybit) * 2 + (1 - core)
+    core_id = {"dp": dp, "shard": near}
+    y_id = {"dp": dp, "shard": across}
+    d_id = {"dp": dp, "shard": diagonal}
+    x_id = {"dp": (dp // 2) * 2 + (1 - xbit), "shard": shard}
+
+    def remote(src, dst, send, recv, target):
+        return pltpu.make_async_remote_copy(
+            src_ref=src, dst_ref=dst, send_sem=send, recv_sem=recv, device_id=target, device_id_type=MESH
+        )
+
+    loads = [
+        pltpu.make_async_copy(wout_hbm, wout, in_sem.at[0]),
+        pltpu.make_async_copy(win_hbm, win, in_sem.at[1]),
+        pltpu.make_async_copy(cot_hbm, cot, in_sem.at[2]),
+        pltpu.make_async_copy(x_hbm, x, in_sem.at[3]),
+    ]
+    for load in loads:
+        load.start()
+    peers = [core_id, y_id, d_id, x_id]
+    barrier = pltpu.get_barrier_semaphore()
+    for peer in peers:
+        pl.semaphore_signal(barrier, inc=1, device_id=peer, device_id_type=MESH)
+
+    def block(owner, k, half):
+        if k < GROUPS_OUT:
+            return wo.at[
+                pl.ds(pl.multiple_of(owner * 2 * TALL + 128 * k, 128), 128),
+                pl.ds(pl.multiple_of(half * (D // 2), 128), D // 2),
+            ]
+        return w.at[
+            pl.ds(pl.multiple_of(owner * TALL + half * HALF, 32), HALF),
+            512 * (k - GROUPS_OUT) : 512 * (k - GROUPS_OUT) + 512,
+        ]
+
+    def y_copy(k):
+        return remote(block(shard, k, xbit), block(shard, k, xbit), ys.at[k], yr.at[k], y_id)
+
+    def y_arrival(k):
+        return remote(block(across, k, xbit), block(across, k, xbit), ys.at[k], yr.at[k], y_id)
+
+    def x_copy(k):
+        return remote(block(across, k, xbit), block(across, k, xbit), xs.at[k], xr.at[k], x_id)
+
+    def x_arrival(k):
+        return remote(block(across, k, 1 - xbit), block(across, k, 1 - xbit), xs.at[k], xr.at[k], x_id)
+
+    def first_copy(k):
+        return remote(block(across, k, xbit), block(across, k, xbit), as_.at[k], ar.at[k], core_id)
+
+    def first_arrival(k):
+        return remote(block(diagonal, k, xbit), block(diagonal, k, xbit), as_.at[k], ar.at[k], core_id)
+
+    def second_copy(k):
+        return remote(block(across, k, 1 - xbit), block(across, k, 1 - xbit), bs.at[k], br.at[k], core_id)
+
+    def second_arrival(k):
+        return remote(block(diagonal, k, 1 - xbit), block(diagonal, k, 1 - xbit), bs.at[k], br.at[k], core_id)
+
+    def rows_of(owner, tall):
+        return pl.ds(pl.multiple_of(owner * tall, 64), tall)
+
+    core_wo = remote(wo.at[rows_of(shard, 2 * TALL)], wo.at[rows_of(shard, 2 * TALL)], cs.at[0], cr.at[0], core_id)
+    core_wo_in = remote(wo.at[rows_of(near, 2 * TALL)], wo.at[rows_of(near, 2 * TALL)], cs.at[0], cr.at[0], core_id)
+    core_w = remote(w.at[rows_of(shard, TALL)], w.at[rows_of(shard, TALL)], cs.at[1], cr.at[1], core_id)
+    core_w_in = remote(w.at[rows_of(near, TALL)], w.at[rows_of(near, TALL)], cs.at[1], cr.at[1], core_id)
+
+    loads[0].wait()
+    wo[rows_of(shard, 2 * TALL), :] = wout[...].astype(bf16)
+    v[shard] = vec_ref[...].astype(bf16).astype(f32)
+    pl.semaphore_wait(barrier, len(peers))
+    small = []
+    for n, target in enumerate((core_id, y_id, d_id)):
+        copy = remote(v.at[shard], v.at[shard], vs.at[n], vr.at[n], target)
+        copy.start()
+        small.append(copy)
+    for k in range(GROUPS_OUT):
+        y_copy(k).start()
+    core_wo.start()
+    loads[1].wait()
+    full = win.shape[1] // 128 * 128
+    w[rows_of(shard, TALL), 0:full] = win[:, 0:full].astype(bf16)
+    w[rows_of(shard, TALL), full:] = jnp.zeros((TALL, WIDTH - full), bf16)
+    w[rows_of(shard, TALL), full : win.shape[1]] = win[:, full:].astype(bf16)
+    for k in range(GROUPS_OUT, GROUPS):
+        y_copy(k).start()
+    core_w.start()
+    for n, owner in enumerate((near, across, diagonal)):
+        remote(v.at[owner], v.at[owner], vs.at[n], vr.at[n], core_id).wait_recv()
+    lane = lax.broadcasted_iota(jnp.int32, (1, 128), 1)
+
+    def row(start):
+        return flat_row(v, vec_len, start)
+
+    def spread(ref, r, start, count):
+        for k in range(count // 128):
+            ref[r : r + 1, 128 * k : 128 * k + 128] = row(start + 128 * k)
+
+    for k in range(CONV):
+        spread(cw_ref, k, k * CHANNELS, CHANNELS)
+    spread(cb_ref, 0, CONV * CHANNELS, CHANNELS)
+    base = (CONV + 1) * CHANNELS
+    hp_ref[...] = jnp.zeros_like(hp_ref)
+    hp_ref[0:1, :] = jnp.where(lane < HEADS, row(base), 0.0)
+    hp_ref[1:2, :] = jnp.where(lane < HEADS, row(base + HEADS), 0.0)
+    skip = row(base + 2 * HEADS)
+    for j in range(PAIRS):
+        dsk_ref[:, 128 * j : 128 * j + 128] = pair_of(lane < 64, skip, j)
+    spread(nw_ref, 0, base + 3 * HEADS, INNER)
+    spread(gain_ref, 0, base + 3 * HEADS + INNER, D)
+    loads[3].wait()
+
+    def norm_rows(n, _):
+        here = pl.ds(pl.multiple_of(n * 32, 32), 32)
+        xv = x[here, :].astype(f32)
+        factor = lax.rsqrt(jnp.mean(xv * xv, axis=1, keepdims=True) + norm_epsilon)
+        normed[here, :] = (xv * factor * gain_ref[...]).astype(bf16)
+        return 0
+
+    lax.fori_loop(0, x.shape[0] // 32, norm_rows, 0)
+    outs = [pltpu.make_async_copy(normed, normed_hbm, keep_sem.at[0])]
+    outs[0].start()
+
+    def dmix_half(side, n):
+        def tile(t, _):
+            start = pl.multiple_of(side * (INNER // 2) + t * 256, 256)
+            dstage[n, :, pl.ds(pl.multiple_of(t * 256, 256), 256)] = mm_t(cot[...], wo[pl.ds(start, 256), :])
+            return 0
+
+        lax.fori_loop(0, INNER // 512, tile, 0)
+        target = dmix_hbm.at[:, pl.ds(pl.multiple_of(side * (INNER // 2), 256), INNER // 2)]
+        copy = pltpu.make_async_copy(dstage.at[n], target, dmix_sem.at[n])
+        copy.start()
+        outs.append(copy)
+
+    def pass_on(k):
+        y_arrival(k).wait_recv()
+        x_copy(k).start()
+        first_copy(k).start()
+
+    def pass_second(k):
+        x_arrival(k).wait_recv()
+        second_copy(k).start()
+
+    def arrived(k):
+        first_arrival(k).wait_recv()
+        second_arrival(k).wait_recv()
+
+    loads[2].wait()
+    core_wo_in.wait_recv()
+    pass_on(0)
+    dmix_half(ybit, 0)
+    pass_on(1)
+    pass_second(0)
+    pass_on(2)
+    pass_second(1)
+    core_w_in.wait_recv()
+    projected = []
+    for k in range(GROUPS_OUT, GROUPS + 1):
+        if k < GROUPS:
+            pass_on(k)
+        pass_second(k - 1)
+        if k == GROUPS_OUT:
+            for n in range(GROUPS_OUT):
+                arrived(n)
+            dmix_half(1 - ybit, 1)
+            copy = pltpu.make_async_copy(wo, wo_hbm, keep_sem.at[1])
+            copy.start()
+            outs.append(copy)
+            continue
+        n = k - 1 - GROUPS_OUT
+        arrived(k - 1)
+        columns = slice(512 * n, 512 * n + 512)
+        if n >= 2:
+            projected[n - 2].wait()
+        stage[n % 2] = mm(normed[...], w[:, columns])
+        copy = pltpu.make_async_copy(stage.at[n % 2], proj_hbm.at[:, columns], proj_sem.at[n])
+        copy.start()
+        projected.append(copy)
+        copy = pltpu.make_async_copy(w.at[:, columns], w_hbm.at[:, columns], w_sem.at[n])
+        copy.start()
+        outs.append(copy)
+    for copy in projected[-2:] + outs:
+        copy.wait()
+    for copy in small + [core_wo, core_w]:
+        copy.wait_send()
+    for k in range(GROUPS):
+        y_copy(k).wait_send()
+        x_copy(k).wait_send()
+        first_copy(k).wait_send()
+        second_copy(k).wait_send()
+
+
+def gather_project(inputs, cot, w_in, w_out, vec, vec_len, owners):
+    length = inputs.shape[0]
+    any_space = pl.BlockSpec(memory_space=pl.ANY)
+    vmem = pl.BlockSpec(memory_space=pltpu.VMEM)
+    dma = pltpu.SemaphoreType.DMA
+    small = [(CONV, CHANNELS), (1, CHANNELS), (8, 128), (1, INNER), (1, INNER), (1, D)]
+    return pl.pallas_call(
+        functools.partial(gather_kernel, vec_len),
+        in_specs=[any_space] * 4 + [vmem],
+        out_specs=[any_space] * 5 + [vmem] * 6,
+        out_shape=[
+            jax.ShapeDtypeStruct((length, WIDTH), f32),
+            jax.ShapeDtypeStruct((length, INNER), f32),
+            jax.ShapeDtypeStruct((length, D), bf16),
+            jax.ShapeDtypeStruct((D, WIDTH), bf16),
+            jax.ShapeDtypeStruct((INNER, D), bf16),
+        ] + [jax.ShapeDtypeStruct(shape, f32) for shape in small],
+        scratch_shapes=[
+            pltpu.VMEM((length, D), bf16),
+            pltpu.VMEM((length, D), bf16),
+            pltpu.VMEM((length, D), bf16),
+            pltpu.VMEM(w_in.shape, f32),
+            pltpu.VMEM(w_out.shape, f32),
+            pltpu.VMEM((D, WIDTH), bf16),
+            pltpu.VMEM((INNER, D), bf16),
+            pltpu.VMEM((owners, VEC_ROWS, 128), f32),
+            pltpu.VMEM((2, length, 512), f32),
+            pltpu.VMEM((2, length, INNER // 2), f32),
+            dma((4,)), dma((WIDTH // 512,)), dma((2,)), dma((2,)), dma((WIDTH // 512,)),
+            dma((2,)), dma((2,)), dma((3,)), dma((3,)),
+            dma((GROUPS,)), dma((GROUPS,)), dma((GROUPS,)), dma((GROUPS,)),
+            dma((GROUPS,)), dma((GROUPS,)), dma((GROUPS,)), dma((GROUPS,)),
+        ],
+        compiler_params=pltpu.CompilerParams(
+            collective_id=2, has_side_effects=True, vmem_limit_bytes=56 * 1024 * 1024
+        ),
+        name="gather_project",
+    )(inputs, cot, w_in, w_out, vec)
+
 beta_first = 0.9
 beta_second = 0.95
 adam_epsilon = 1e-08
 rate_matrix = 0.01
 rate_vector = 0.1
 decay_matrix = 0.1
-
-
-def layout():
-    return [(CONV, CHANNELS), (CHANNELS,), (HEADS,), (HEADS,), (HEADS,), (INNER,), (D,)]
-
-
-def unpack(flat_values):
-    pieces = []
-    offset = 0
-    for shape in layout():
-        count = math.prod(shape)
-        pieces.append(flat_values[offset : offset + count].reshape(shape))
-        offset += count
-    return pieces
-
-
-def prenorm(values, gain_values):
-    return (
-        values
-        * lax.rsqrt(jnp.mean(values * values, axis=-1, keepdims=True) + norm_epsilon)
-        * gain_values
-    )
 
 
 def adam(param, grad, first, second, rate, decay):
@@ -796,32 +1046,26 @@
 ):
     vec_len = vectors.shape[0]
     in_width = w_in.shape[1]
-    w_in_low = jnp.pad(w_in.astype(bf16), ((0, 0), (0, WIDTH - in_width)))
-    w_all = lax.all_gather(w_in_low, "shard", axis=0, tiled=True)
-    w_out_all = lax.all_gather(w_out.astype(bf16), "shard", axis=0, tiled=True)
-    vec_all = lax.all_gather(vectors.astype(bf16), "shard", axis=0, tiled=True).astype(f32)
-    conv_w, conv_b, dt_bias, a_log, d_skip, norm_w, gain = unpack(vec_all)
-    hp = jnp.stack([jnp.pad(v, (0, 128 - HEADS)) for v in (dt_bias, a_log)] + [jnp.zeros((128,), f32)] * 6)
-    dsk = jnp.repeat(d_skip, HEADDIM)[None, :]
     es = selectors()
     seqs_here, length, width = inputs.shape
     rows_low = inputs.reshape(seqs_here * length, width)
-    rows = rows_low.astype(f32)
     cot = cotangent.reshape(seqs_here * length, width)
-    normed_low = prenorm(rows, gain).astype(bf16)
-    proj = mm(normed_low, w_all)
-    dmix = mm_t(cot, w_out_all)
+    owners = lax.axis_size("shard")
+    vec = jnp.pad(vectors, (0, VEC_ROWS * 128 - vec_len)).reshape(VEC_ROWS, 128)
+    proj, dmix, normed_low, w_all, w_out_all, conv_w, conv_b, hp, dsk, norm_w, gain = gather_project(
+        rows_low, cot, w_in, w_out, vec, vec_len, owners
+    )
     forward = []
     for n in range(seqs_here):
         part = slice(n * length, (n + 1) * length)
-        forward.append(mix_forward(proj[part], dmix[part], conv_w, conv_b[None], hp, dsk, norm_w[None], es))
+        forward.append(mix_forward(proj[part], dmix[part], conv_w, conv_b, hp, dsk, norm_w, es))
     mixer_low = jnp.concatenate([f[0] for f in forward], axis=0)
     dz = jnp.concatenate([f[1] for f in forward], axis=0)
     backward = []
     for n in range(seqs_here):
         part = slice(n * length, (n + 1) * length)
         _, _, ds, st, dt, cum, ps, _ = forward[n]
-        backward.append(mix_backward(proj[part], ds, st, dt, cum, ps, conv_w, conv_b[None], hp, dsk, es))
+        backward.append(mix_backward(proj[part], ds, st, dt, cum, ps, conv_w, conv_b, hp, dsk, es))
     du = jnp.concatenate([b[0] for b in backward], axis=0)
     def total(values):
         return sum(values[1:], values[0])
@@ -832,10 +1076,9 @@
     dskip = total([b[4] for b in backward]).sum(axis=0).reshape(HEADS, HEADDIM).sum(axis=1)
     dnw = total([f[7] for f in forward]).sum(axis=0)
     small = jnp.concatenate([dcw.reshape(-1), dcb, dhp[0, :HEADS], dhp[1, :HEADS], dskip, dnw, jnp.zeros((D,), f32)])
-    owners = small.shape[0] // vec_len
-    small = jnp.pad(small.reshape(owners, vec_len), ((0, 0), (0, 32 * 128 - vec_len))).reshape(owners, 32, 128)
+    small = jnp.pad(small.reshape(owners, vec_len), ((0, 0), (0, VEC_ROWS * 128 - vec_len))).reshape(owners, VEC_ROWS, 128)
     gin, gout, input_grad, outputs = reduce_grads(
-        lax.axis_size("dp"), normed_low, cot, mixer_low, dz, du, rows_low, w_all, w_out_all, gain[None], small
+        lax.axis_size("dp"), normed_low, cot, mixer_low, dz, du, rows_low, w_all, w_out_all, gain, small
     )
     outputs = outputs.reshape(inputs.shape)
     input_grad = input_grad.reshape(inputs.shape)

time: 271 us -> 223 us (0.82)
  Pallas kernels: 153 us -> 198 us
  waiting for transfers between devices: 41.6 us -> 0 us
  matrix products: 19 us -> 0 us
  between operations: 15 us -> 0.82 us
  blocking collectives: 13.8 us -> 0 us
  other arithmetic: 19.9 us -> 13.8 us
    pallas_call x0 -> x1, Pallas kernels: none -> 44.7 us  [gather_project(): pl.pallas_call(functools.partial(gather_kernel, vec_len), in_specs=[any_s...]
    all_gather x2 -> x0, waiting for transfers between devices: 41.6 us -> none  [the longest x1 36.8 us: shards(): w_all = lax.all_gather(w_in_low, 'shard', axis=0, tiled=True)]
    dot_general x2 -> x0, matrix products: 19 us -> none  [the longest x1 11.6 us: mm(): lax.dot_general(a, b, (((1,), (0,)), ((), ())), preferred_element_type=f32)]
    unnamed x1 -> x0, blocking collectives: 13.8 us -> none
    convert_element_type x4 -> x0, other arithmetic: 5.61 us -> none  [the longest x1 2.15 us: shards(): w_out_all = lax.all_gather(w_out.astype(bf16), 'shard', axis=0, tiled=True)]
    unnamed x31 -> x32, local copies, waits for them, and re-layouts: 5 us -> 8.29 us
  transfers between devices with their start and end apart: 2 -> 0, of which waited for: 2 -> 0; matrix products, arithmetic and copies ran while one was open for 6% -> 0% of each run, Pallas kernels for 0% -> 0%
where the time goes in v3:
time: 223 us; the launch traced here: 222 us
  Pallas kernels  198 us (89%)
  other arithmetic  13.8 us (6%)
  local copies, waits for them, and re-layouts  9.88 us (4%)
    pallas_call x1, Pallas kernels, reduce_grads(): pl.pallas_call(functools.partial(reduce_kernel, far), in_specs=[any_space...  78.4 us
    pallas_call x1, Pallas kernels, mix_backward(): pl.pallas_call(backward_kernel, grid=(blocks,), in_specs=[rows(WIDTH), pl...  46.5 us
    pallas_call x1, Pallas kernels, gather_project(): pl.pallas_call(functools.partial(gather_kernel, vec_len), in_specs=[any_s...  44.7 us
    pallas_call x1, Pallas kernels, mix_forward(): pl.pallas_call(forward_kernel, grid=(blocks,), in_specs=[rows(WIDTH), row...  28.2 us
    sub x3, other arithmetic, adam(): return (param - rate * (update + decay * param), new_first, new_second)  11.5 us
    unnamed x32, local copies, waits for them, and re-layouts  8.29 us

profile of v3, /device:TPU:0, one launch (start us, length us, event | category | flops | bytes accessed | tf_op | source)
XLA Modules:
  0.0 222.2 jit_solution(6819707665707822850)
XLA Ops:
  0.6 1.3 pad_bitcast_fusion.1.vec_ref
  2.0 44.7 %gather_project.1 = (f32[1024,3584]{1,0:T(8,128)}, f32[1024,1536]{1,0:T(8,128)}, bf16[1024,768]{1,0:T(8,128)(2,1)}, bf16[768,3584]{1,0:T(8,128)(2,1)}, bf16[1536...) custom-call(bf16[1024,768]{1,0:T(8,128)(2,1)} %bitcast.19, ...), custom_call_target="tpu_custom_call" | custom-call | tf_op jit(solution)/shard_map/gather_project/pallas_call | solution.py:994
  46.6 0.1 add_add_fusion
  46.7 1.1 fusion.es_ref
  47.8 0.0 copy-start
  47.9 0.7 copy-done
  48.6 0.0 copy-start.1
  48.6 0.7 copy-done.1
  49.3 0.0 copy-start.2
  49.3 0.7 copy-done.2
  50.0 0.0 copy-start.3
  50.0 0.7 copy-done.3
  50.7 0.0 copy-start.4
  50.7 0.7 copy-done.4
  51.4 28.2 %mix_forward.1 = (bf16[1024,1536]{1,0:T(8,128)(2,1)}, bf16[1024,1536]{1,0:T(8,128)(2,1)}, bf16[1024,1536]{1,0:T(8,128)(2,1)}, bf16[8,128,1536]{2,1,0:T(8,128)(2,...) custom-call(f32[1024,3584]{1,0:T(8,128)} %get-tuple-element.43.proj_ref, ...), custom_call_target="tpu_custom_call" | custom-call | tf_op jit(solution)/shard_map/mix_forward/pallas_call | solution.py:311
  79.6 46.5 %mix_backward.1 = (bf16[1024,2048]{1,0:T(8,128)(2,1)}, f32[4,8,1792]{2,1,0:T(8,128)S(1)}, f32[8,1792]{1,0:T(8,128)S(1)}, f32[2,8,128]{2,1,0:T(8,128)S(1)}, f32[8,1536]{1,0:T(8,128)S(1)}) custom-call(f32[1024,3584]{1,0:T(8,128)} %get-tuple-element.43.proj_ref.prev_ref, f32[1024,3584]{1,0:T(8,128)} %get-tuple-element.43.proj_ref.prev_ref, ...), custom_call_target="tpu_custom_call" | custom-call | tf_op jit(solution)/shard_map/mix_backward/pallas_call | solution.py:349
  126.0 0.1 reduce_sum.54
  126.2 0.1 reshape.129
  126.2 0.1 reduce_sum.58
  126.4 0.1 concatenate.3
  126.5 0.1 reshape.130
  126.6 0.6 copy.27
  127.3 0.0 copy-start.11
  127.3 0.0 copy-start.12
  127.3 0.0 copy-start.13
  127.3 78.4 %reduce_grads.1 = (bf16[192,3584]{1,0:T(8,128)(2,1)}, bf16[384,768]{1,0:T(8,128)(2,1)}, f32[1024,768]{1,0:T(8,128)}, bf16[1024,768]{1,0:T(8,128)(2,1)}) custom-call(bf16[1024,768]{1,0:T(8,128)(2,1)} %get-tuple-element.42.normed_hbm, bf16[1024,768]{1,0:T(8,128)(2,1)} %bitcast.22, bf16[1024,1536]{1,0:T(8,128)(2,1)} %get-tuple-element.50.mixer_hbm, ...), custom_call_target="tpu_custom_call" | custom-call | tf_op jit(solution)/shard_map/reduce_grads/pallas_call | solution.py:714
  205.7 0.8 slice_convert_fusion.1
  206.5 0.0 copy-done.11
  206.5 0.0 copy-done.12
  206.5 0.0 copy-done.13
  206.5 0.7 multiply_subtract_fusion.2
  207.2 0.0 copy-start.5
  207.3 0.0 copy-start.8
  207.3 0.0 copy-start.9
  207.3 0.0 copy-start.10
  207.3 8.4 %multiply_subtract_fusion = (f32[192,3352]{1,0:T(8,128)}, f32[192,3352]{1,0:T(8,128)}, f32[192,3352]{1,0:T(8,128)}, f32[192,3352]{1,0:T(8,128)}) fusion(f32[192,3352]{1,0:T(8,128)} %win_hbm.1, f32[192,3352]{1,0:T(8,128)} %param.16, f32[192,3352]{1,0:T(8,128)} %param.17, bf16[192,3584]{1,0:T(8,128)(2,1)} %get-tuple-element.68), kind=kLoop, calls=%fused_computation.4 | loop fusion | flops 10297344 | bytes 19307520 | tf_op jit(solution)/shard_map/sub | solution.py:1041
  215.6 0.0 copy-done.5
  215.6 0.0 copy-done.8
  215.6 0.0 copy-done.9
  215.6 0.0 copy-done.10
  215.7 0.0 copy-start.7
  215.7 2.4 %multiply_subtract_fusion.1 = (f32[384,768]{1,0:T(8,128)}, f32[384,768]{1,0:T(8,128)}, f32[384,768]{1,0:T(8,128)}, f32[384,768]{1,0:T(8,128)}) fusion(f32[384,768]{1,0:T(8,128)S(1)} %copy-done.5, f32[384,768]{1,0:T(8,128)S(1)} %copy-done.8, f32[384,768]{1,0:T(8,128)S(1)} %copy-done.9, bf16[384,768]{1,0:T(8,128)(2,1)S(1)} %copy-done.10), kind=kLoop, calls=%fused_computation.9 | loop fusion | flops 4718592 | bytes 8847360 | tf_op jit(solution)/shard_map/sub | solution.py:1041
  218.1 0.0 copy-start.6
  218.1 0.0 copy-done.7
  218.1 1.1 copy.30
  219.2 1.3 copy-done.6
  220.6 1.7 copy.31
  (12 shorter events, 0.1 us)
Async XLA Ops:
  47.8 0.7 copy-start
  48.6 0.7 copy-start.1
  49.3 0.7 copy-start.2
  50.0 0.7 copy-start.3
  50.7 0.7 copy-start.4
  127.3 79.2 %copy-start.11 = (f32[2834]{0:T(1024)S(1)}, f32[2834]{0:T(1024)}, u32[]{:S(2)}) copy-start(f32[2834]{0:T(1024)} %param.15) | copy-start | bytes 34012
  127.3 79.2 %copy-start.12 = (f32[2834]{0:T(1024)S(1)}, f32[2834]{0:T(1024)}, u32[]{:S(2)}) copy-start(f32[2834]{0:T(1024)} %param.20) | copy-start | bytes 34012
  127.3 79.2 %copy-start.13 = (f32[2834]{0:T(1024)S(1)}, f32[2834]{0:T(1024)}, u32[]{:S(2)}) copy-start(f32[2834]{0:T(1024)} %param.21) | copy-start | bytes 34012
  207.2 8.4 %copy-start.5 = (f32[384,768]{1,0:T(8,128)S(1)}, f32[384,768]{1,0:T(8,128)}, u32[]{:S(2)}) copy-start(f32[384,768]{1,0:T(8,128)} %wout_hbm.1) | copy-start | bytes 3538948
  207.3 8.4 %copy-start.8 = (f32[384,768]{1,0:T(8,128)S(1)}, f32[384,768]{1,0:T(8,128)}, u32[]{:S(2)}) copy-start(f32[384,768]{1,0:T(8,128)} %param.18) | copy-start | bytes 3538948
  207.3 8.4 %copy-start.9 = (f32[384,768]{1,0:T(8,128)S(1)}, f32[384,768]{1,0:T(8,128)}, u32[]{:S(2)}) copy-start(f32[384,768]{1,0:T(8,128)} %param.19) | copy-start | bytes 3538948
  207.3 8.4 %copy-start.10 = (bf16[384,768]{1,0:T(8,128)(2,1)S(1)}, bf16[384,768]{1,0:T(8,128)(2,1)}, u32[]{:S(2)}) copy-start(bf16[384,768]{1,0:T(8,128)(2,1)} %get-tuple-element.69) | copy-start | bytes 1769476
  215.7 2.4 %copy-start.7 = (bf16[1024,768]{1,0:T(8,128)(2,1)S(1)}, bf16[1024,768]{1,0:T(8,128)(2,1)}, u32[]{:S(2)}) copy-start(bf16[1024,768]{1,0:T(8,128)(2,1)} %get-tuple-element.66) | copy-start | bytes 4718596
  218.1 2.5 %copy-start.6 = (f32[1024,768]{1,0:T(8,128)S(1)}, f32[1024,768]{1,0:T(8,128)}, u32[]{:S(2)}) copy-start(f32[1024,768]{1,0:T(8,128)} %get-tuple-element.67) | copy-start | bytes 9437188

commit v4 on v3

--- a/solution.py
+++ b/solution.py
@@ -65,8 +65,179 @@
     return jnp.where(n == head + offset(k), 1.0, 0.0).astype(bf16)
 
 
+PIECES_OUT = 3
+WIDE = 512
+EARLY = PIECES_OUT + INNER // WIDE
+SLIM = 256
+LATE = (CHANNELS + 256) // SLIM
+TALL = 192
+HALF = TALL // 2
+NEAR = 4
+QUARTER = TALL // NEAR
+FIRST_TICK = 1
+STAGE_TICKS = (1, 3, 4, 5, 6, 7)
+MESH = pl.DeviceIdType.MESH
+
+
+class Reducer:
+    def __init__(self, far, g, rc, ry, rx, rz, rf, f, cs, cr, ys, yr, xs, xr, zs, zr, fs, fr, gs, gr, hs, hr):
+        dp = lax.axis_index("dp")
+        shard = lax.axis_index("shard")
+        xbit = dp % 2
+        zpos = dp // 2
+        near = zpos % NEAR
+        group = zpos // NEAR
+        core = shard % 2
+        ybit = shard // 2
+        core_id = {"dp": dp, "shard": ybit * 2 + (1 - core)}
+        y_id = {"dp": dp, "shard": (1 - ybit) * 2 + core}
+        x_id = {"dp": zpos * 2 + (1 - xbit), "shard": shard}
+        half = f.shape[2] // 2
+        keep = pl.ds(pl.multiple_of(xbit * half, 128), half)
+        give = pl.ds(pl.multiple_of((1 - xbit) * half, 128), half)
+
+        def near_id(k):
+            return {"dp": (group * NEAR + (near + k) % NEAR) * 2 + xbit, "shard": shard}
+
+        def far_id(k):
+            return {"dp": (((group + k) % far) * NEAR + near) * 2 + xbit, "shard": shard}
+
+        def rows(k):
+            return pl.ds(pl.multiple_of(((near + k) % NEAR) * QUARTER, 16), QUARTER)
+
+        def remote(src, dst, send, recv, target):
+            return pltpu.make_async_remote_copy(
+                src_ref=src, dst_ref=dst, send_sem=send, recv_sem=recv, device_id=target, device_id_type=MESH
+            )
+
+        def core_copy(p):
+            return remote(g.at[p, 1 - core], rc.at[p], cs.at[p], cr.at[p], core_id)
+
+        def y_copy(p):
+            return remote(g.at[p, core, 1 - ybit], ry.at[p], ys.at[p], yr.at[p], y_id)
+
+        def x_copy(p):
+            return remote(g.at[p, core, ybit, :, give], rx.at[p], xs.at[p], xr.at[p], x_id)
+
+        def z_copy(p, k):
+            there = NEAR - 1 - k
+            return remote(
+                g.at[p, core, ybit, rows(k), keep], rz.at[p, there], zs.at[p, k - 1], zr.at[p, there], near_id(k)
+            )
+
+        def z_arrival(p, k):
+            return remote(
+                g.at[p, core, ybit, rows(k), keep], rz.at[p, k - 1], zs.at[p, k - 1], zr.at[p, k - 1], near_id(k)
+            )
+
+        def far_copy(p, k):
+            there = far - 1 - k
+            return remote(f.at[p, rows(0), keep], rf.at[p, there], hs.at[p, k - 1], hr.at[p, there], far_id(k))
+
+        def far_arrival(p, k):
+            return remote(f.at[p, rows(0), keep], rf.at[p, k - 1], hs.at[p, k - 1], hr.at[p, k - 1], far_id(k))
+
+        def spread_copy(p, k):
+            here = f.at[p, rows(0), keep]
+            return remote(here, here, fs.at[p, k - 1], fr.at[p, NEAR - 1 - k], near_id(k))
+
+        def spread_arrival(p, k):
+            here = f.at[p, rows(k), keep]
+            return remote(here, here, fs.at[p, k - 1], fr.at[p, k - 1], near_id(k))
+
+        def pair_copy(p):
+            return remote(f.at[p, :, keep], f.at[p, :, keep], gs.at[p], gr.at[p], x_id)
+
+        def pair_arrival(p):
+            return remote(f.at[p, :, give], f.at[p, :, give], gs.at[p], gr.at[p], x_id)
+
+        def to_y(p):
+            core_copy(p).wait_recv()
+            other = 1 - ybit
+            g[p, core, other] = (g[p, core, other].astype(f32) + rc[p, other].astype(f32)).astype(bf16)
+            y_copy(p).start()
+
+        def to_x(p):
+            y_copy(p).wait_recv()
+            total = g[p, core, ybit].astype(f32) + rc[p, ybit].astype(f32) + ry[p].astype(f32)
+            g[p, core, ybit] = total.astype(bf16)
+            x_copy(p).start()
+
+        def to_z(p):
+            x_copy(p).wait_recv()
+            g[p, core, ybit, :, keep] = (g[p, core, ybit, :, keep].astype(f32) + rx[p].astype(f32)).astype(bf16)
+            for k in range(1, NEAR):
+                z_copy(p, k).start()
+
+        def to_spread(p):
+            total = g[p, core, ybit, rows(0), keep].astype(f32)
+            for k in range(1, NEAR):
+                z_arrival(p, k).wait_recv()
+                total = total + rz[p, k - 1].astype(f32)
+            f[p, rows(0), keep] = total.astype(bf16)
+            if far > 1:
+                for k in range(1, far):
+                    far_copy(p, k).start()
+                for k in range(1, far):
+                    far_copy(p, k).wait_send()
+                    far_arrival(p, k).wait_recv()
+                    total = total + rf[p, k - 1].astype(f32)
+                f[p, rows(0), keep] = total.astype(bf16)
+            for k in range(1, NEAR):
+                spread_copy(p, k).start()
+
+        def to_pair(p):
+            for k in range(1, NEAR):
+                spread_arrival(p, k).wait_recv()
+            pair_copy(p).start()
+
+        def finish(p):
+            pair_arrival(p).wait_recv()
+
+        def greet():
+            peers = [core_id, y_id, x_id] + [near_id(k) for k in range(1, NEAR)] + [far_id(k) for k in range(1, far)]
+            barrier = pltpu.get_barrier_semaphore()
+            for peer in peers:
+                pl.semaphore_signal(barrier, inc=1, device_id=peer, device_id_type=MESH)
+            pl.semaphore_wait(barrier, len(peers))
+
+        def drain(count):
+            def one(p, _):
+                core_copy(p).wait_send()
+                y_copy(p).wait_send()
+                x_copy(p).wait_send()
+                for k in range(1, NEAR):
+                    z_copy(p, k).wait_send()
+                    spread_copy(p, k).wait_send()
+                pair_copy(p).wait_send()
+                return 0
+
+            lax.fori_loop(0, count, one, 0)
+
+        self.g, self.f, self.greet, self.drain = g, f, greet, drain
+        self.start = lambda p: core_copy(p).start()
+        self.stages = (to_y, to_x, to_z, to_spread, to_pair, finish)
+
+
+def reducer_scratch(far, count, wide):
+    dma = pltpu.SemaphoreType.DMA
+    return [
+        pltpu.VMEM((count, 2, 2, TALL, wide), bf16),
+        pltpu.VMEM((count, 2, TALL, wide), bf16),
+        pltpu.VMEM((count, TALL, wide), bf16),
+        pltpu.VMEM((count, TALL, wide // 2), bf16),
+        pltpu.VMEM((count, NEAR - 1, QUARTER, wide // 2), bf16),
+        pltpu.VMEM((count, max(far - 1, 1), QUARTER, wide // 2), bf16),
+        pltpu.VMEM((count, TALL, wide), bf16),
+        dma((count,)), dma((count,)), dma((count,)), dma((count,)), dma((count,)), dma((count,)),
+        dma((count, NEAR - 1)), dma((count, NEAR - 1)), dma((count, NEAR - 1)), dma((count, NEAR - 1)),
+        dma((count,)), dma((count,)),
+        dma((count, max(far - 1, 1))), dma((count, max(far - 1, 1))),
+    ]
+
+
 def forward_kernel(
-    proj_ref, dmix_ref, cw_ref, cb_ref, hp_ref, dsk_ref, nw_ref, es_ref,
+    proj_ref, dmix_ref, pm_ref, es_ref,
     mixer_ref, dz_ref, ds_ref, st_ref, dt_ref, cum_ref, ps_ref, dnw_ref,
     state, halo, s_scr,
 ):
@@ -82,8 +253,8 @@
     row = lax.broadcasted_iota(jnp.int32, (Q, 128), 0)
     lo = lane < 64
     lower = row >= lane
-    dt = softplus(proj_ref[:, R_OFF : R_OFF + 128] + hp_ref[0:1, :])
-    log_decay = dt * (jnp.exp(hp_ref[1:2, :]) * (-LOG2E))
+    dt = softplus(proj_ref[:, R_OFF : R_OFF + 128] + pm_ref[8:9, 0:128])
+    log_decay = dt * (jnp.exp(pm_ref[9:10, 0:128]) * (-LOG2E))
     cum = mm_exact(jnp.where(lower, 1.0, 0.0), log_decay)
     cum_t = cum.T
     dt_ref[...] = dt
@@ -92,9 +263,9 @@
 
     def conv(col):
         ext = jnp.concatenate([halo[:, col : col + 128], proj_ref[:, INNER + col : INNER + col + 128]], axis=0)
-        out = cb_ref[:, col : col + 128]
+        out = pm_ref[4:5, col : col + 128]
         for k in range(CONV):
-            out = out + cw_ref[k : k + 1, col : col + 128] * ext[5 + k : 5 + k + Q]
+            out = out + pm_ref[k : k + 1, col : col + 128] * ext[5 + k : 5 + k + Q]
         return out
 
     def act(col):
@@ -127,12 +298,12 @@
         y = mm(weights, stacked) + jnp.exp2(cum_e) * mm(c_low, old_low)
         moved = (xs * jnp.exp2(tot_e - cum_e)).astype(bf16)
         state[:, col] = old * jnp.exp2(tot_e) + mm(b_t, moved)
-        s = y + dsk_ref[:, col] * x
+        s = y + pm_ref[5:6, col] * x
         s_scr[:, col] = s
         z = proj_ref[:, col]
         g = s * (z * sigmoid(z))
         sq = sq + g * g
-        dot = dot + g * (dmix_ref[:, col] * nw_ref[:, col])
+        dot = dot + g * (dmix_ref[:, col] * pm_ref[6:7, col])
     halo[...] = proj_ref[Q - 8 : Q, INNER : INNER + CHANNELS]
     mean = jnp.sum(sq, axis=1, keepdims=True) * (1.0 / INNER)
     factor = lax.rsqrt(mean + norm_epsilon)
@@ -149,9 +320,9 @@
         g = s * sz
         dm = dmix_ref[:, col]
         gf = g * factor
-        mixer_ref[:, col] = (gf * nw_ref[:, col]).astype(bf16)
+        mixer_ref[:, col] = (gf * pm_ref[6:7, col]).astype(bf16)
         dnw_ref[:, col] += fold8(dm * gf)
-        dg = dm * nw_ref[:, col] * factor - g * back
+        dg = dm * pm_ref[6:7, col] * factor - g * back
         dz_ref[:, col] = (dg * s * (sig + sz * (1.0 - sig))).astype(bf16)
         ds_low = (dg * sz).astype(bf16)
         ds_ref[:, col] = ds_low
@@ -163,13 +334,97 @@
 
 
 def backward_kernel(
-    proj_ref, prev_ref, ds_ref, st_ref, dt_ref, cum_ref, ps_ref, cw_ref, cb_ref, hp_ref, dsk_ref, es_ref,
-    du_ref, dcw_ref, dcb_ref, dhp_ref, dsk_out_ref,
+    far,
+    proj_ref, prev_ref, ds_ref, st_ref, dt_ref, cum_ref, ps_ref, pm_ref, es_ref,
+    mixer_hbm, cot_hbm, normed_hbm, dz_hbm,
+    du_ref, dcw_ref, dcb_ref, dhp_ref, dsk_out_ref, gout_hbm, gz_hbm,
     dstate, dc_next, dyc_scr, moved_scr, dlow_scr,
+    mixer, cot, normed, dz, in_sem, res_sem, *rest,
 ):
     step = pl.program_id(0)
     blocks = pl.num_programs(0)
     chunk = blocks - 1 - step
+    red = Reducer(far, *rest)
+    g, f = red.g, red.f
+    copies = [
+        pltpu.make_async_copy(mixer_hbm, mixer, in_sem.at[0]),
+        pltpu.make_async_copy(cot_hbm, cot, in_sem.at[1]),
+        pltpu.make_async_copy(normed_hbm, normed, in_sem.at[2]),
+        pltpu.make_async_copy(dz_hbm, dz, in_sem.at[3]),
+    ]
+
+    def result_out(p, h):
+        return pltpu.make_async_copy(
+            f.at[p, :, 256 * h : 256 * h + 256],
+            gout_hbm.at[TALL * h : TALL * h + TALL, pl.ds(pl.multiple_of(p * 256, 256), 256)],
+            res_sem.at[p, h],
+        )
+
+    def result_z(p):
+        return pltpu.make_async_copy(
+            f.at[p], gz_hbm.at[:, pl.ds(pl.multiple_of((p - PIECES_OUT) * WIDE, WIDE), WIDE)], res_sem.at[p, 0]
+        )
+
+    def compute_out(p):
+        right = cot[:, pl.ds(pl.multiple_of(p * 256, 256), 256)]
+        for owner in range(4):
+            left = mixer[:, 2 * TALL * owner : 2 * TALL * (owner + 1)]
+            value = mm_rows(left, right).astype(bf16)
+            for h in range(2):
+                g[p, owner % 2, owner // 2, :, 256 * h : 256 * h + 256] = value[TALL * h : TALL * h + TALL]
+
+    def compute_z(p):
+        value = mm_rows(normed[...], dz[:, pl.ds(pl.multiple_of((p - PIECES_OUT) * WIDE, WIDE), WIDE)]).astype(bf16)
+        for owner in range(4):
+            g[p, owner % 2, owner // 2] = value[TALL * owner : TALL * (owner + 1)]
+
+    def tick(t):
+        def at(delay):
+            since = t - FIRST_TICK - delay
+            p = 2 * ((since + 24) // 3 - 8) + (since + 24) % 3
+            return p, (since >= 0) & ((since + 24) % 3 < 2) & (p < EARLY)
+
+        @pl.when(t == FIRST_TICK)
+        def _():
+            copies[0].wait()
+            copies[1].wait()
+
+        @pl.when(t == FIRST_TICK + PIECES_OUT // 2 * 3 + PIECES_OUT % 2)
+        def _():
+            copies[2].wait()
+            copies[3].wait()
+
+        p0, on0 = at(0)
+
+        @pl.when(on0 & (p0 < PIECES_OUT))
+        def _():
+            compute_out(p0)
+
+        @pl.when(on0 & (p0 >= PIECES_OUT))
+        def _():
+            compute_z(p0)
+
+        @pl.when(on0)
+        def _():
+            red.start(p0)
+
+        for stage, delay in zip(red.stages, STAGE_TICKS):
+            p, on = at(delay)
+
+            @pl.when(on)
+            def _(stage=stage, p=p):
+                stage(p)
+
+        p, on = at(STAGE_TICKS[-1])
+
+        @pl.when(on & (p < PIECES_OUT))
+        def _():
+            for h in range(2):
+                result_out(p, h).start()
+
+        @pl.when(on & (p >= PIECES_OUT))
+        def _():
+            result_z(p).start()
 
     @pl.when(step == 0)
     def _():
@@ -179,6 +434,11 @@
         dcb_ref[...] = jnp.zeros_like(dcb_ref)
         dhp_ref[...] = jnp.zeros_like(dhp_ref)
         dsk_out_ref[...] = jnp.zeros_like(dsk_out_ref)
+        for copy in copies:
+            copy.start()
+        red.greet()
+
+    tick(2 * step)
 
     lane = lax.broadcasted_iota(jnp.int32, (Q, 128), 1)
     row = lax.broadcasted_iota(jnp.int32, (Q, 128), 0)
@@ -195,9 +455,9 @@
         return [ext[5 + k : 5 + k + Q] for k in range(CONV)]
 
     def conv(shifted, col):
-        out = cb_ref[:, col : col + 128]
+        out = pm_ref[4:5, col : col + 128]
         for k in range(CONV):
-            out = out + cw_ref[k : k + 1, col : col + 128] * shifted[k]
+            out = out + pm_ref[k : k + 1, col : col + 128] * shifted[k]
         return out
 
     def conv_back(dx, c, sig, shifted, col):
@@ -206,9 +466,9 @@
             dcw_ref[k, :, col : col + 128] += fold8(dc * shifted[k])
         dcb_ref[:, col : col + 128] += fold8(dc)
         ext = jnp.concatenate([dc, dc_next[:, col : col + 128]], axis=0)
-        du = cw_ref[CONV - 1 : CONV, col : col + 128] * dc
+        du = pm_ref[CONV - 1 : CONV, col : col + 128] * dc
         for k in range(CONV - 1):
-            du = du + cw_ref[k : k + 1, col : col + 128] * ext[CONV - 1 - k : CONV - 1 - k + Q]
+            du = du + pm_ref[k : k + 1, col : col + 128] * ext[CONV - 1 - k : CONV - 1 - k + Q]
         dc_next[:, col : col + 128] = dc[0:8]
         du_ref[:, col : col + 128] = du.astype(bf16)
 
@@ -224,6 +484,8 @@
     sums = jnp.zeros((Q, 128), f32)
     carry = jnp.zeros((8, 128), f32)
     for j in range(PAIRS):
+        if j == PAIRS // 2:
+            tick(2 * step + 1)
         col = slice(128 * j, 128 * j + 128)
         shifted = taps(128 * j)
         c = conv(shifted, 128 * j)
@@ -263,12 +525,12 @@
         dxs = dxw + dxe
         dyx = dyf * x
         dsk_out_ref[:, col] += fold8(dyx)
-        w1 = xs_low.astype(f32) * dxw + dsk_ref[:, col] * dyx
+        w1 = xs_low.astype(f32) * dxw + pm_ref[5:6, col] * dyx
         hi = w1.astype(bf16)
         rest = (w1 - hi.astype(f32)).astype(bf16)
         many = jnp.concatenate([hi, rest, (xs * dxe).astype(bf16), (x * dxs).astype(bf16)], axis=1)
         sums = sums + mm(many, es_ref[j])
-        conv_back(dxs * dt_e + dsk_ref[:, col] * dyf, c, sig, shifted, 128 * j)
+        conv_back(dxs * dt_e + pm_ref[5:6, col] * dyf, c, sig, shifted, 128 * j)
     dscores = jnp.where(upper, dscores, 0.0).astype(bf16)
     db = mm(dscores, c_low) + mm_t(moved_scr[...], dlow_scr[...])
     dcc = mm(dscores.T, b_low) + mm_t(dyc_scr[...], st_ref[0])
@@ -280,13 +542,22 @@
     p = jnp.where(head, ps_ref[...] - sums, 0.0)
     ones = jnp.where(upper, 1.0, 0.0)
     da = mm_exact(ones, p) + mm_exact(1.0 - ones, q) + jnp.sum(carry, axis=0, keepdims=True)
-    rate = jnp.exp(hp_ref[1:2, :])
-    raw = proj_ref[:, R_OFF : R_OFF + 128] + hp_ref[0:1, :]
+    rate = jnp.exp(pm_ref[9:10, 0:128])
+    raw = proj_ref[:, R_OFF : R_OFF + 128] + pm_ref[8:9, 0:128]
     dr = jnp.where(head, (v - rate * da) * jax.nn.sigmoid(raw), 0.0)
     dhp_ref[0] += fold8(dr)
     dhp_ref[1] += fold8(jnp.where(head, da * dt * -rate, 0.0))
     du_ref[:, CHANNELS : CHANNELS + 128] = dr.astype(bf16)
     du_ref[:, CHANNELS + 128 :] = jnp.zeros((Q, 128), bf16)
+
+    @pl.when(step == blocks - 1)
+    def _():
+        red.drain(EARLY)
+        for p in range(PIECES_OUT):
+            for h in range(2):
+                result_out(p, h).wait()
+        for p in range(PIECES_OUT, EARLY):
+            result_z(p).wait()
 
 
 def selectors():
@@ -301,7 +572,7 @@
     return pl.BlockSpec(shape, lambda i: (0,) * len(shape))
 
 
-def mix_forward(proj, dmix, cw, cb, hp, dsk, nw, es):
+def mix_forward(proj, dmix, pm, es):
     length = proj.shape[0]
     blocks = length // Q
 
@@ -312,8 +583,7 @@
         forward_kernel,
         grid=(blocks,),
         in_specs=[
-            rows(WIDTH), rows(INNER), whole((CONV, CHANNELS)), whole((1, CHANNELS)), whole((8, 128)),
-            whole((1, INNER)), whole((1, INNER)), whole((PAIRS, 512, 128)),
+            rows(WIDTH), rows(INNER), whole((16, CHANNELS)), whole((PAIRS, 512, 128)),
         ],
         out_specs=[
             rows(INNER), rows(INNER), rows(INNER), pl.BlockSpec((1, STATE, INNER), lambda i: (i, 0, 0)),
@@ -336,29 +606,33 @@
         ],
         compiler_params=pltpu.CompilerParams(vmem_limit_bytes=48 * 1024 * 1024),
         name="mix_forward",
-    )(proj, dmix, cw, cb, hp, dsk, nw, es)
-
-
-def mix_backward(proj, ds, st, dt, cum, ps, cw, cb, hp, dsk, es):
+    )(proj, dmix, pm, es)
+
+
+def mix_backward(mesh_dp, proj, ds, st, dt, cum, ps, pm, es, mixer, cot, normed, dz):
     length = proj.shape[0]
     blocks = length // Q
+    far = mesh_dp // 2 // NEAR
+    any_space = pl.BlockSpec(memory_space=pl.ANY)
+    dma = pltpu.SemaphoreType.DMA
+    assert 2 * blocks > FIRST_TICK + (EARLY - 1) // 2 * 3 + (EARLY - 1) % 2 + STAGE_TICKS[-1]
 
     def rows(width):
         return pl.BlockSpec((Q, width), lambda i: (blocks - 1 - i, 0))
 
     return pl.pallas_call(
-        backward_kernel,
+        functools.partial(backward_kernel, far),
         grid=(blocks,),
         in_specs=[
             rows(WIDTH),
             pl.BlockSpec((8, WIDTH), lambda i: (jnp.maximum((blocks - 1 - i) * (Q // 8) - 1, 0), 0)),
             rows(INNER), pl.BlockSpec((1, STATE, INNER), lambda i: (blocks - 1 - i, 0, 0)),
             rows(128), rows(128), rows(128),
-            whole((CONV, CHANNELS)), whole((1, CHANNELS)), whole((8, 128)),
-            whole((1, INNER)), whole((PAIRS, 512, 128)),
-        ],
+            whole((16, CHANNELS)), whole((PAIRS, 512, 128)),
+        ] + [any_space] * 4,
         out_specs=[
             rows(CHANNELS + 256), whole((CONV, 8, CHANNELS)), whole((8, CHANNELS)), whole((2, 8, 128)), whole((8, INNER)),
+            any_space, any_space,
         ],
         out_shape=[
             jax.ShapeDtypeStruct((length, CHANNELS + 256), bf16),
@@ -366,6 +640,8 @@
             jax.ShapeDtypeStruct((8, CHANNELS), f32),
             jax.ShapeDtypeStruct((2, 8, 128), f32),
             jax.ShapeDtypeStruct((8, INNER), f32),
+            jax.ShapeDtypeStruct((2 * TALL, D), bf16),
+            jax.ShapeDtypeStruct((TALL, INNER), bf16),
         ],
         scratch_shapes=[
             pltpu.VMEM((STATE, INNER), f32),
@@ -373,163 +649,68 @@
             pltpu.VMEM((Q, INNER), bf16),
             pltpu.VMEM((Q, INNER), bf16),
             pltpu.VMEM((STATE, INNER), bf16),
-        ],
-        compiler_params=pltpu.CompilerParams(vmem_limit_bytes=48 * 1024 * 1024),
+            pltpu.VMEM((length, INNER), bf16),
+            pltpu.VMEM((length, D), bf16),
+            pltpu.VMEM((length, D), bf16),
+            pltpu.VMEM((length, INNER), bf16),
+            dma((4,)), dma((EARLY, 2)),
+        ] + reducer_scratch(far, EARLY, WIDE),
+        compiler_params=pltpu.CompilerParams(
+            collective_id=3, has_side_effects=True, vmem_limit_bytes=48 * 1024 * 1024
+        ),
         name="mix_backward",
-    )(proj, proj, ds, st, dt, cum, ps, cw, cb, hp, dsk, es)
-
-
-PIECES_OUT = 3
-PIECES_IN = 7
-PIECES = PIECES_OUT + PIECES_IN
-TALL = 192
-WIDE = 512
-HALF = TALL // 2
-NEAR = 4
-COVER_BACK = 4
-MESH = pl.DeviceIdType.MESH
+    )(proj, proj, ds, st, dt, cum, ps, pm, es, mixer, cot, normed, dz)
+
+
+BACK_SLOT = 1
+OUT_SLOT = 7
 
 
 def reduce_kernel(
     far,
-    normed_hbm, cot_hbm, mixer_hbm, dz_hbm, du_hbm, x_hbm, w_hbm, wo_hbm, gain_ref, vec_ref,
-    gin_hbm, gout_hbm, dx_hbm, out_hbm,
-    normed, cot, mixer, dproj, x, w, wo, dn, dgain,
-    dx, out,
-    g, rc, ry, rx, rz, rf, f,
-    in_sem, out_sem, dx_sem, res_sem,
-    cs, cr, ys, yr, xs, xr, zs, zr, fs, fr, gs, gr, hs, hr,
+    normed_hbm, cot_hbm, mixer_hbm, dz_hbm, du_hbm, x_hbm, w_hbm, wo_hbm, gz_hbm, pm_ref, vec_ref,
+    gin_hbm, dx_hbm, out_hbm,
+    normed, cot, mixer, dproj, x, w, wo, gz, dn, dgain, dx, out,
+    in_sem, out_sem, dx_sem, res_sem, gz_sem, *rest,
 ):
-    dp = lax.axis_index("dp")
-    shard = lax.axis_index("shard")
-    xbit = dp % 2
-    zpos = dp // 2
-    near = zpos % NEAR
-    group = zpos // NEAR
-    core = shard % 2
-    ybit = shard // 2
-    core_id = {"dp": dp, "shard": ybit * 2 + (1 - core)}
-    y_id = {"dp": dp, "shard": (1 - ybit) * 2 + core}
-    x_id = {"dp": zpos * 2 + (1 - xbit), "shard": shard}
-
-    def near_id(k):
-        return {"dp": (group * NEAR + (near + k) % NEAR) * 2 + xbit, "shard": shard}
-
-    def far_id(k):
-        return {"dp": (((group + k) % far) * NEAR + near) * 2 + xbit, "shard": shard}
-
-    keep_rows = pl.ds(pl.multiple_of(xbit * HALF, 32), HALF)
-    give_rows = pl.ds(pl.multiple_of((1 - xbit) * HALF, 32), HALF)
-
-    def cols(k):
-        return pl.ds(pl.multiple_of(((near + k) % NEAR) * 128, 128), 128)
-
-    def remote(src, dst, send, recv, target):
-        return pltpu.make_async_remote_copy(
-            src_ref=src, dst_ref=dst, send_sem=send, recv_sem=recv, device_id=target, device_id_type=MESH
-        )
-
+    red = Reducer(far, *rest)
+    g, f = red.g, red.f
     copies = [
-        pltpu.make_async_copy(mixer_hbm, mixer, in_sem.at[0]),
-        pltpu.make_async_copy(cot_hbm, cot, in_sem.at[1]),
-        pltpu.make_async_copy(normed_hbm, normed, in_sem.at[2]),
-        pltpu.make_async_copy(dz_hbm, dproj.at[:, 0:INNER], in_sem.at[3]),
-        pltpu.make_async_copy(du_hbm, dproj.at[:, INNER:], in_sem.at[4]),
-        pltpu.make_async_copy(w_hbm, w, in_sem.at[5]),
-        pltpu.make_async_copy(x_hbm, x, in_sem.at[6]),
+        pltpu.make_async_copy(normed_hbm, normed, in_sem.at[0]),
+        pltpu.make_async_copy(du_hbm, dproj.at[:, INNER:], in_sem.at[1]),
+        pltpu.make_async_copy(dz_hbm, dproj.at[:, 0:INNER], in_sem.at[2]),
+        pltpu.make_async_copy(w_hbm, w, in_sem.at[3]),
+        pltpu.make_async_copy(x_hbm, x, in_sem.at[4]),
+        pltpu.make_async_copy(cot_hbm, cot, in_sem.at[5]),
+        pltpu.make_async_copy(mixer_hbm, mixer, in_sem.at[6]),
         pltpu.make_async_copy(wo_hbm, wo, in_sem.at[7]),
+        pltpu.make_async_copy(gz_hbm, gz, in_sem.at[8]),
     ]
-    for k in (0, 1, 6, 7, 2, 3, 4, 5):
-        copies[k].start()
-    peers = [core_id, y_id, x_id] + [near_id(k) for k in range(1, NEAR)] + [far_id(k) for k in range(1, far)]
-    barrier = pltpu.get_barrier_semaphore()
-    for peer in peers:
-        pl.semaphore_signal(barrier, inc=1, device_id=peer, device_id_type=MESH)
-    pl.semaphore_wait(barrier, len(peers))
-
-    def core_copy(p):
-        return remote(g.at[p, 1 - core], rc.at[p], cs.at[p], cr.at[p], core_id)
-
-    def y_copy(p):
-        return remote(g.at[p, core, 1 - ybit], ry.at[p], ys.at[p], yr.at[p], y_id)
-
-    def x_copy(p):
-        return remote(g.at[p, core, ybit, give_rows], rx.at[p], xs.at[p], xr.at[p], x_id)
-
-    def z_copy(p, k):
-        return remote(
-            g.at[p, core, ybit, keep_rows, cols(k)], rz.at[p, NEAR - 1 - k], zs.at[p, k - 1], zr.at[p, NEAR - 1 - k],
-            near_id(k),
-        )
-
-    def z_arrival(p, k):
-        return remote(
-            g.at[p, core, ybit, keep_rows, cols(k)], rz.at[p, k - 1], zs.at[p, k - 1], zr.at[p, k - 1], near_id(k)
-        )
-
-    def far_copy(p, k):
-        return remote(
-            f.at[p, keep_rows, cols(0)], rf.at[p, far - 1 - k], hs.at[p, k - 1], hr.at[p, far - 1 - k], far_id(k)
-        )
-
-    def far_arrival(p, k):
-        return remote(f.at[p, keep_rows, cols(0)], rf.at[p, k - 1], hs.at[p, k - 1], hr.at[p, k - 1], far_id(k))
-
-    def spread_copy(p, k):
-        return remote(
-            f.at[p, keep_rows, cols(0)], f.at[p, keep_rows, cols(0)], fs.at[p, k - 1], fr.at[p, NEAR - 1 - k],
-            near_id(k),
-        )
-
-    def spread_arrival(p, k):
-        return remote(
-            f.at[p, keep_rows, cols(k)], f.at[p, keep_rows, cols(k)], fs.at[p, k - 1], fr.at[p, k - 1], near_id(k)
-        )
-
-    def pair_copy(p):
-        return remote(f.at[p, keep_rows], f.at[p, keep_rows], gs.at[p], gr.at[p], x_id)
-
-    def pair_arrival(p):
-        return remote(f.at[p, give_rows], f.at[p, give_rows], gs.at[p], gr.at[p], x_id)
-
-    def result_out(p, h):
-        return pltpu.make_async_copy(
-            f.at[p, :, 256 * h : 256 * h + 256],
-            gout_hbm.at[TALL * h : TALL * h + TALL, pl.ds(pl.multiple_of(p * 256, 256), 256)],
-            res_sem.at[p, h],
-        )
+    for copy in copies:
+        copy.start()
+    red.greet()
 
     def result_in(p):
         return pltpu.make_async_copy(
-            f.at[p],
-            gin_hbm.at[:, pl.ds(pl.multiple_of((p - PIECES_OUT) * WIDE, WIDE), WIDE)],
-            res_sem.at[p, 0],
+            f.at[p], gin_hbm.at[:, pl.ds(pl.multiple_of(INNER + p * SLIM, SLIM), SLIM)], res_sem.at[p]
         )
 
-    def compute_out(p):
-        right = cot[:, pl.ds(pl.multiple_of(p * 256, 256), 256)]
-        for owner in range(4):
-            left = mixer[:, 2 * TALL * owner : 2 * TALL * (owner + 1)]
-            value = mm_rows(left, right).astype(bf16)
-            for h in range(2):
-                g[p, owner % 2, owner // 2, :, 256 * h : 256 * h + 256] = value[TALL * h : TALL * h + TALL]
-
     def compute_in(p):
-        right = dproj[:, pl.ds(pl.multiple_of((p - PIECES_OUT) * WIDE, WIDE), WIDE)]
+        right = dproj[:, pl.ds(pl.multiple_of(INNER + p * SLIM, SLIM), SLIM)]
         value = mm_rows(normed[...], right).astype(bf16)
         for owner in range(4):
             g[p, owner % 2, owner // 2] = value[TALL * owner : TALL * (owner + 1)]
+
+    def dgain_row(k):
+        return jnp.sum(dgain[:, 128 * k : 128 * k + 128], axis=0, keepdims=True)
 
     def compute_small():
         pieces = [dgain_row(k) for k in range(D // 128)] + [jnp.zeros((16 - D // 128, 128), f32)]
         block = jnp.concatenate(pieces, axis=0).astype(bf16)
         for owner in range(4):
-            g[PIECES - 1, owner % 2, owner // 2, :, WIDE - 128 :] = jnp.zeros((TALL, 128), bf16)
-            g[PIECES - 1, owner % 2, owner // 2, 0:32, WIDE - 128 :] = vec_ref[owner].astype(bf16)
-            g[PIECES - 1, owner % 2, owner // 2, 32:48, WIDE - 128 :] = block
-
-    def dgain_row(k):
-        return jnp.sum(dgain[:, 128 * k : 128 * k + 128], axis=0, keepdims=True)
+            g[LATE - 1, owner % 2, owner // 2, :, SLIM - 128 :] = jnp.zeros((TALL, 128), bf16)
+            g[LATE - 1, owner % 2, owner // 2, 0:32, SLIM - 128 :] = vec_ref[owner].astype(bf16)
+            g[LATE - 1, owner % 2, owner // 2, 32:48, SLIM - 128 :] = block
 
     def cover_back(n):
         rows = pl.ds(pl.multiple_of(n * 256, 256), 256)
@@ -541,7 +722,7 @@
             d = dn[sub, :]
             xv = x[here, :].astype(f32)
             factor = lax.rsqrt(jnp.mean(xv * xv, axis=1, keepdims=True) + norm_epsilon)
-            t = d * gain_ref[...]
+            t = d * pm_ref[7:8, 0:D]
             back = jnp.mean(t * xv, axis=1, keepdims=True) * (factor * factor * factor)
             dx[here, :] = cot[here, :].astype(f32) + (factor * t - back * xv)
             dgain[...] += (d * (xv * factor)).reshape(4, 8, D).sum(axis=0)
@@ -563,149 +744,70 @@
         rows = pl.ds(pl.multiple_of(n * 256, 256), 256)
         return pltpu.make_async_copy(out.at[rows], out_hbm.at[rows], out_sem.at[n])
 
+    kept = pltpu.make_async_copy(gz, gin_hbm.at[:, 0:INNER], gz_sem.at[0])
     tiles = x.shape[0] // 256
+    per_slot = tiles // 4
     dgain[...] = jnp.zeros_like(dgain)
     copies[0].wait()
     copies[1].wait()
 
     def slot(i, _):
-        @pl.when(i < PIECES_OUT)
-        def _():
-            compute_out(i)
-
-        @pl.when(i == PIECES_OUT)
-        def _():
-            copies[2].wait()
-            copies[3].wait()
-            copies[4].wait()
-
-        @pl.when((i >= PIECES_OUT) & (i < PIECES))
+        @pl.when(i < LATE - 1)
         def _():
             compute_in(i)
-
-        @pl.when(i == PIECES - 1)
-        def _():
+            red.start(i)
+
+        @pl.when(i == BACK_SLOT)
+        def _():
+            for copy in copies[2:6]:
+                copy.wait()
+
+        @pl.when((i >= BACK_SLOT) & (i < BACK_SLOT + 4))
+        def _():
+            lax.fori_loop(0, per_slot, lambda k, c: (cover_back((i - BACK_SLOT) * per_slot + k), c)[1], 0)
+
+        @pl.when(i == LATE - 1)
+        def _():
+            compute_in(i)
             compute_small()
-
-        @pl.when(i < PIECES)
-        def _():
-            core_copy(i).start()
-
-        @pl.when(i == 0)
-        def _():
-            for copy in copies[6:8]:
+            red.start(i)
+
+        @pl.when(i == OUT_SLOT)
+        def _():
+            for copy in copies[6:]:
                 copy.wait()
-
-        @pl.when(i < COVER_BACK)
-        def _():
-            lax.fori_loop(0, per_out, lambda k, c: (cover_out(i * per_out + k), c)[1], 0)
-
-        @pl.when(i == COVER_BACK)
-        def _():
-            copies[5].wait()
-
-        @pl.when((i >= COVER_BACK) & (i < COVER_BACK + 4))
-        def _():
-            lax.fori_loop(0, per_back, lambda k, c: (cover_back((i - COVER_BACK) * per_back + k), c)[1], 0)
-
-        @pl.when(i < PIECES)
-        def _():
-            core_copy(i).wait_recv()
-            give = 1 - ybit
-            g[i, core, give] = (g[i, core, give].astype(f32) + rc[i, give].astype(f32)).astype(bf16)
-            y_copy(i).start()
-
-        p1 = i - 1
-
-        @pl.when((p1 >= 0) & (p1 < PIECES))
-        def _():
-            y_copy(p1).wait_recv()
-            total = g[p1, core, ybit].astype(f32) + rc[p1, ybit].astype(f32) + ry[p1].astype(f32)
-            g[p1, core, ybit] = total.astype(bf16)
-            x_copy(p1).start()
-
-        p2 = i - 2
-
-        @pl.when((p2 >= 0) & (p2 < PIECES))
-        def _():
-            x_copy(p2).wait_recv()
-            g[p2, core, ybit, keep_rows] = (
-                g[p2, core, ybit, keep_rows].astype(f32) + rx[p2].astype(f32)
-            ).astype(bf16)
-            for k in range(1, NEAR):
-                z_copy(p2, k).start()
-
-        p3 = i - 3
-
-        @pl.when((p3 >= 0) & (p3 < PIECES))
-        def _():
-            total = g[p3, core, ybit, keep_rows, cols(0)].astype(f32)
-            for k in range(1, NEAR):
-                z_arrival(p3, k).wait_recv()
-                total = total + rz[p3, k - 1].astype(f32)
-            f[p3, keep_rows, cols(0)] = total.astype(bf16)
-            if far > 1:
-                for k in range(1, far):
-                    far_copy(p3, k).start()
-                for k in range(1, far):
-                    far_copy(p3, k).wait_send()
-                    far_arrival(p3, k).wait_recv()
-                    total = total + rf[p3, k - 1].astype(f32)
-                f[p3, keep_rows, cols(0)] = total.astype(bf16)
-            for k in range(1, NEAR):
-                spread_copy(p3, k).start()
-
-        p4 = i - 4
-
-        @pl.when((p4 >= 0) & (p4 < PIECES))
-        def _():
-            for k in range(1, NEAR):
-                spread_arrival(p4, k).wait_recv()
-            pair_copy(p4).start()
-
-        p5 = i - 5
-
-        @pl.when((p5 >= 0) & (p5 < PIECES))
-        def _():
-            pair_arrival(p5).wait_recv()
-
-        @pl.when((p5 >= 0) & (p5 < PIECES_OUT))
-        def _():
-            for h in range(2):
-                result_out(p5, h).start()
-
-        @pl.when((p5 >= PIECES_OUT) & (p5 < PIECES))
-        def _():
-            result_in(p5).start()
+            kept.start()
+
+        @pl.when((i >= OUT_SLOT) & (i < OUT_SLOT + 4))
+        def _():
+            lax.fori_loop(0, per_slot, lambda k, c: (cover_out((i - OUT_SLOT) * per_slot + k), c)[1], 0)
+
+        for n, stage in enumerate(red.stages):
+            p = i - n
+
+            @pl.when((p >= 0) & (p < LATE))
+            def _(stage=stage, p=p):
+                stage(p)
+
+        done = i - len(red.stages) + 1
+
+        @pl.when((done >= 0) & (done < LATE))
+        def _():
+            result_in(done).start()
 
         return 0
 
-    per_out = (tiles + COVER_BACK - 1) // COVER_BACK
-    per_back = tiles // 4
-    lax.fori_loop(0, PIECES + 5, slot, 0)
-
-    def drain(p, _):
-        core_copy(p).wait_send()
-        y_copy(p).wait_send()
-        x_copy(p).wait_send()
-        for k in range(1, NEAR):
-            z_copy(p, k).wait_send()
-            spread_copy(p, k).wait_send()
-        pair_copy(p).wait_send()
-        return 0
-
-    lax.fori_loop(0, PIECES, drain, 0)
-    for p in range(PIECES_OUT):
-        for h in range(2):
-            result_out(p, h).wait()
-    for p in range(PIECES_OUT, PIECES):
+    lax.fori_loop(0, LATE + 5, slot, 0)
+    red.drain(LATE)
+    kept.wait()
+    for p in range(LATE):
         result_in(p).wait()
     for n in range(tiles):
         result_dx(n).wait()
         result_rows(n).wait()
 
 
-def reduce_grads(mesh_dp, normed, cot, mixer, dz, du, x, w, wo, gain, vec):
+def reduce_grads(mesh_dp, normed, cot, mixer, dz, du, x, w, wo, gz, pm, vec):
     length = x.shape[0]
     far = mesh_dp // 2 // NEAR
     any_space = pl.BlockSpec(memory_space=pl.ANY)
@@ -713,11 +815,10 @@
     dma = pltpu.SemaphoreType.DMA
     return pl.pallas_call(
         functools.partial(reduce_kernel, far),
-        in_specs=[any_space] * 8 + [vmem] * 2,
-        out_specs=[any_space] * 4,
+        in_specs=[any_space] * 9 + [vmem] * 2,
+        out_specs=[any_space] * 3,
         out_shape=[
-            jax.ShapeDtypeStruct((TALL, PIECES_IN * WIDE), bf16),
-            jax.ShapeDtypeStruct((2 * TALL, D), bf16),
+            jax.ShapeDtypeStruct((TALL, WIDTH), bf16),
             jax.ShapeDtypeStruct((length, D), f32),
             jax.ShapeDtypeStruct((length, D), bf16),
         ],
@@ -729,28 +830,18 @@
             pltpu.VMEM((length, D), bf16),
             pltpu.VMEM((D, WIDTH), bf16),
             pltpu.VMEM((INNER, D), bf16),
+            pltpu.VMEM((TALL, INNER), bf16),
             pltpu.VMEM((256, D), f32),
             pltpu.VMEM((8, D), f32),
             pltpu.VMEM((length, D), f32),
             pltpu.VMEM((length, D), bf16),
-            pltpu.VMEM((PIECES, 2, 2, TALL, WIDE), bf16),
-            pltpu.VMEM((PIECES, 2, TALL, WIDE), bf16),
-            pltpu.VMEM((PIECES, TALL, WIDE), bf16),
-            pltpu.VMEM((PIECES, HALF, WIDE), bf16),
-            pltpu.VMEM((PIECES, NEAR - 1, HALF, 128), bf16),
-            pltpu.VMEM((PIECES, max(far - 1, 1), HALF, 128), bf16),
-            pltpu.VMEM((PIECES, TALL, WIDE), bf16),
-            dma((8,)), dma((length // 256,)), dma((length // 256,)), dma((PIECES, 2)),
-            dma((PIECES,)), dma((PIECES,)), dma((PIECES,)), dma((PIECES,)), dma((PIECES,)), dma((PIECES,)),
-            dma((PIECES, NEAR - 1)), dma((PIECES, NEAR - 1)), dma((PIECES, NEAR - 1)), dma((PIECES, NEAR - 1)),
-            dma((PIECES,)), dma((PIECES,)),
-            dma((PIECES, max(far - 1, 1))), dma((PIECES, max(far - 1, 1))),
-        ],
+            dma((9,)), dma((length // 256,)), dma((length // 256,)), dma((LATE,)), dma((1,)),
+        ] + reducer_scratch(far, LATE, SLIM),
         compiler_params=pltpu.CompilerParams(
-            collective_id=1, has_side_effects=True, vmem_limit_bytes=64 * 1024 * 1024 - 256 * 1024
+            collective_id=1, has_side_effects=True, vmem_limit_bytes=44 * 1024 * 1024
         ),
         name="reduce_grads",
-    )(normed, cot, mixer, dz, du, x, w, wo, gain, vec)
+    )(normed, cot, mixer, dz, du, x, w, wo, gz, pm, vec)
 
 
 GROUPS_OUT = 3
@@ -780,7 +871,7 @@
 def gather_kernel(
     vec_len,
     x_hbm, cot_hbm, win_hbm, wout_hbm, vec_ref,
-    proj_hbm, dmix_hbm, normed_hbm, w_hbm, wo_hbm, cw_ref, cb_ref, hp_ref, dsk_ref, nw_ref, gain_ref,
+    proj_hbm, dmix_hbm, normed_hbm, w_hbm, wo_hbm, pm_ref,
     x, cot, normed, win, wout, w, wo, v, stage, dstage,
     in_sem, proj_sem, dmix_sem, keep_sem, w_sem,
     cs, cr, vs, vr, ys, yr, xs, xr, as_, ar, bs, br,
@@ -890,25 +981,24 @@
         for k in range(count // 128):
             ref[r : r + 1, 128 * k : 128 * k + 128] = row(start + 128 * k)
 
-    for k in range(CONV):
-        spread(cw_ref, k, k * CHANNELS, CHANNELS)
-    spread(cb_ref, 0, CONV * CHANNELS, CHANNELS)
+    pm_ref[...] = jnp.zeros_like(pm_ref)
+    for k in range(CONV + 1):
+        spread(pm_ref, k, k * CHANNELS, CHANNELS)
     base = (CONV + 1) * CHANNELS
-    hp_ref[...] = jnp.zeros_like(hp_ref)
-    hp_ref[0:1, :] = jnp.where(lane < HEADS, row(base), 0.0)
-    hp_ref[1:2, :] = jnp.where(lane < HEADS, row(base + HEADS), 0.0)
+    pm_ref[8:9, 0:128] = jnp.where(lane < HEADS, row(base), 0.0)
+    pm_ref[9:10, 0:128] = jnp.where(lane < HEADS, row(base + HEADS), 0.0)
     skip = row(base + 2 * HEADS)
     for j in range(PAIRS):
-        dsk_ref[:, 128 * j : 128 * j + 128] = pair_of(lane < 64, skip, j)
-    spread(nw_ref, 0, base + 3 * HEADS, INNER)
-    spread(gain_ref, 0, base + 3 * HEADS + INNER, D)
+        pm_ref[5:6, 128 * j : 128 * j + 128] = pair_of(lane < 64, skip, j)
+    spread(pm_ref, 6, base + 3 * HEADS, INNER)
+    spread(pm_ref, 7, base + 3 * HEADS + INNER, D)
     loads[3].wait()
 
     def norm_rows(n, _):
         here = pl.ds(pl.multiple_of(n * 32, 32), 32)
         xv = x[here, :].astype(f32)
         factor = lax.rsqrt(jnp.mean(xv * xv, axis=1, keepdims=True) + norm_epsilon)
-        normed[here, :] = (xv * factor * gain_ref[...]).astype(bf16)
+        normed[here, :] = (xv * factor * pm_ref[7:8, 0:D]).astype(bf16)
         return 0
 
     lax.fori_loop(0, x.shape[0] // 32, norm_rows, 0)
@@ -990,18 +1080,18 @@
     any_space = pl.BlockSpec(memory_space=pl.ANY)
     vmem = pl.BlockSpec(memory_space=pltpu.VMEM)
     dma = pltpu.SemaphoreType.DMA
-    small = [(CONV, CHANNELS), (1, CHANNELS), (8, 128), (1, INNER), (1, INNER), (1, D)]
     return pl.pallas_call(
         functools.partial(gather_kernel, vec_len),
         in_specs=[any_space] * 4 + [vmem],
-        out_specs=[any_space] * 5 + [vmem] * 6,
+        out_specs=[any_space] * 5 + [vmem],
         out_shape=[
             jax.ShapeDtypeStruct((length, WIDTH), f32),
             jax.ShapeDtypeStruct((length, INNER), f32),
             jax.ShapeDtypeStruct((length, D), bf16),
             jax.ShapeDtypeStruct((D, WIDTH), bf16),
             jax.ShapeDtypeStruct((INNER, D), bf16),
-        ] + [jax.ShapeDtypeStruct(shape, f32) for shape in small],
+            jax.ShapeDtypeStruct((16, CHANNELS), f32),
+        ],
         scratch_shapes=[
             pltpu.VMEM((length, D), bf16),
             pltpu.VMEM((length, D), bf16),
@@ -1048,37 +1138,27 @@
     in_width = w_in.shape[1]
     es = selectors()
     seqs_here, length, width = inputs.shape
+    assert seqs_here == 1
     rows_low = inputs.reshape(seqs_here * length, width)
     cot = cotangent.reshape(seqs_here * length, width)
     owners = lax.axis_size("shard")
     vec = jnp.pad(vectors, (0, VEC_ROWS * 128 - vec_len)).reshape(VEC_ROWS, 128)
-    proj, dmix, normed_low, w_all, w_out_all, conv_w, conv_b, hp, dsk, norm_w, gain = gather_project(
+    proj, dmix, normed_low, w_all, w_out_all, pm = gather_project(
         rows_low, cot, w_in, w_out, vec, vec_len, owners
     )
-    forward = []
-    for n in range(seqs_here):
-        part = slice(n * length, (n + 1) * length)
-        forward.append(mix_forward(proj[part], dmix[part], conv_w, conv_b, hp, dsk, norm_w, es))
-    mixer_low = jnp.concatenate([f[0] for f in forward], axis=0)
-    dz = jnp.concatenate([f[1] for f in forward], axis=0)
-    backward = []
-    for n in range(seqs_here):
-        part = slice(n * length, (n + 1) * length)
-        _, _, ds, st, dt, cum, ps, _ = forward[n]
-        backward.append(mix_backward(proj[part], ds, st, dt, cum, ps, conv_w, conv_b, hp, dsk, es))
-    du = jnp.concatenate([b[0] for b in backward], axis=0)
-    def total(values):
-        return sum(values[1:], values[0])
-
-    dcw = total([b[1] for b in backward]).sum(axis=1)
-    dcb = total([b[2] for b in backward]).sum(axis=0)
-    dhp = total([b[3] for b in backward]).sum(axis=1)
-    dskip = total([b[4] for b in backward]).sum(axis=0).reshape(HEADS, HEADDIM).sum(axis=1)
-    dnw = total([f[7] for f in forward]).sum(axis=0)
+    mixer_low, dz, ds, st, dt, cum, ps, dnw = mix_forward(proj, dmix, pm, es)
+    du, dcw, dcb, dhp, dskip, gout, gz = mix_backward(
+        lax.axis_size("dp"), proj, ds, st, dt, cum, ps, pm, es, mixer_low, cot, normed_low, dz
+    )
+    dcw = dcw.sum(axis=1)
+    dcb = dcb.sum(axis=0)
+    dhp = dhp.sum(axis=1)
+    dskip = dskip.sum(axis=0).reshape(HEADS, HEADDIM).sum(axis=1)
+    dnw = dnw.sum(axis=0)
     small = jnp.concatenate([dcw.reshape(-1), dcb, dhp[0, :HEADS], dhp[1, :HEADS], dskip, dnw, jnp.zeros((D,), f32)])
     small = jnp.pad(small.reshape(owners, vec_len), ((0, 0), (0, VEC_ROWS * 128 - vec_len))).reshape(owners, VEC_ROWS, 128)
-    gin, gout, input_grad, outputs = reduce_grads(
-        lax.axis_size("dp"), normed_low, cot, mixer_low, dz, du, rows_low, w_all, w_out_all, gain, small
+    gin, input_grad, outputs = reduce_grads(
+        lax.axis_size("dp"), normed_low, cot, mixer_low, dz, du, rows_low, w_all, w_out_all, gz, pm, small
     )
     outputs = outputs.reshape(inputs.shape)
     input_grad = input_grad.reshape(inputs.shape)

time: 223 us -> 228 us (1.022)
  local copies, waits for them, and re-layouts: 9.88 us -> 14.9 us
    pallas_call x1, Pallas kernels: 78.4 us -> 49.4 us  [reduce_grads(): pl.pallas_call(functools.partial(reduce_kernel, far), in_specs=[any_space...]
    pallas_call x1, Pallas kernels: 46.5 us -> 74.4 us  [mix_backward(): pl.pallas_call(functools.partial(backward_kernel, far), grid=(blocks,), i...]
    unnamed x32 -> x46, local copies, waits for them, and re-layouts: 8.29 us -> 12.6 us
where the time goes in v4:
time: 228 us
  Pallas kernels  197 us (86%)
  other arithmetic  15.2 us (7%)
  local copies, waits for them, and re-layouts  14.9 us (7%)
    pallas_call x1, Pallas kernels, mix_backward(): pl.pallas_call(functools.partial(backward_kernel, far), grid=(blocks,), i...  74.4 us
    pallas_call x1, Pallas kernels, reduce_grads(): pl.pallas_call(functools.partial(reduce_kernel, far), in_specs=[any_space...  49.4 us
    pallas_call x1, Pallas kernels, gather_project(): pl.pallas_call(functools.partial(gather_kernel, vec_len), in_specs=[any_s...  44.7 us
    pallas_call x1, Pallas kernels, mix_forward(): pl.pallas_call(forward_kernel, grid=(blocks,), in_specs=[rows(WIDTH), row...  28.2 us
    unnamed x46, local copies, waits for them, and re-layouts  12.6 us
    sub x3, other arithmetic, adam(): return (param - rate * (update + decay * param), new_first, new_second)  11.5 us

profile of v4, /device:TPU:0, one launch (start us, length us, event | category | flops | bytes accessed | tf_op | source)
XLA Modules:
  0.0 227.6 jit_solution(7990824529456782116)
XLA Ops:
  0.6 1.3 pad_bitcast_fusion.1.vec_ref
  2.0 44.7 %gather_project.1 = (f32[1024,3584]{1,0:T(8,128)}, f32[1024,1536]{1,0:T(8,128)}, bf16[1024,768]{1,0:T(8,128)(2,1)}, bf16[768,3584]{1,0:T(8,128)(2,1)}, bf16[1536,768]{1,0:T(8,128)(2,1)}, /*index=5*/f32[16,1792]{1,0:T(8,128)}) custom-call(bf16[1024,768]{1,0:T(8,128)(2,1)} %bitcast.22, bf16[1024,768]{1,0:T(8,128)(2,1)} %bitcast.19, f32[192,3352]{1,0:T(8,128)} %win_hbm.1, ...), custom_call_target="tpu_custom_call" | custom-call | tf_op jit(solution)/shard_map/gather_project/pallas_call | solution.py:1083
  46.7 0.1 add_add_fusion
  46.7 1.1 fusion.es_ref
  47.9 0.0 copy-start.6
  47.9 0.9 copy-done.6
  48.8 0.0 copy-start.7
  48.8 28.2 %mix_forward.1 = (bf16[1024,1536]{1,0:T(8,128)(2,1)}, bf16[1024,1536]{1,0:T(8,128)(2,1)}, bf16[1024,1536]{1,0:T(8,128)(2,1)}, bf16[8,128,1536]{2,1,0:T(8,128)(2,...) custom-call(f32[1024,3584]{1,0:T(8,128)} %get-tuple-element.39.proj_ref, ...), custom_call_target="tpu_custom_call" | custom-call | tf_op jit(solution)/shard_map/mix_forward/pallas_call | solution.py:582
  76.9 0.0 copy-start.12
  76.9 0.6 copy-done.12
  77.5 0.0 copy-done.7
  77.5 0.0 copy-start
  77.5 0.0 copy-start.1
  77.5 74.4 %mix_backward.1 = (bf16[1024,2048]{1,0:T(8,128)(2,1)}, f32[4,8,1792]{2,1,0:T(8,128)S(1)}, f32[8,1792]{1,0:T(8,128)S(1)}, f32[2,8,128]{2,1,0:T(8,128)S(1)}, f32[8...) custom-call(f32[1024,3584]{1,0:T(8,128)} %get-tuple-element.39.proj_ref.prev_ref, ...), custom_call_target="tpu_custom_call" | custom-call | tf_op jit(solution)/shard_map/mix_backward/pallas_call | solution.py:623
  152.0 0.0 copy-start.8
  152.0 0.8 copy-done.8
  152.8 0.0 copy-start.10
  152.8 0.8 copy-done.10
  153.6 0.0 copy-start.13
  153.6 0.6 copy-done.13
  154.2 0.7 reduce_sum.54
  154.9 0.8 reshape.128
  155.7 0.8 reduce_sum.57
  156.5 0.1 reshape.129
  156.6 0.1 reduce_sum.58
  156.7 0.8 reduce_sum.59
  157.6 0.1 concatenate.3
  157.7 0.1 reshape.130
  157.8 0.0 copy-done
  157.8 0.0 copy-done.1
  157.8 0.0 copy-start.2
  157.8 1.4 copy-done.2
  159.2 0.0 copy-start.11
  159.2 1.1 copy-done.11
  160.3 0.0 copy-start.18
  160.3 0.0 copy-start.19
  160.3 0.0 copy-start.20
  160.3 49.4 %reduce_grads.1 = (bf16[192,3584]{1,0:T(8,128)(2,1)S(1)}, f32[1024,768]{1,0:T(8,128)}, bf16[1024,768]{1,0:T(8,128)(2,1)S(1)}) custom-call(bf16[1024,768]{1,0:T(8,128)(2,1)S(1)} %copy-done.1, bf16[1024,768]{1,0:T(8,128)(2,1)S(1)} %bitcast.21, bf16[1024,1536]{1,0:T(8,128)(2,1)} %get-tuple-element.42.mixer_hbm, bf16[1024,1536]{1,0:T(8,128)(2,1)} %get-tuple-element.43.dz_hbm, ...), custom_call_target="tpu_custom_call" | custom-call | tf_op jit(solution)/shard_map/reduce_grads/pallas_call | solution.py:816
  209.7 0.0 copy-start.3
  209.7 1.1 copy-done.3
  210.8 0.0 copy-start.5
  210.8 1.1 copy-done.5
  211.9 0.0 copy-done.18
  211.9 0.0 copy-done.19
  211.9 0.0 copy-done.20
  212.0 0.7 multiply_subtract_fusion.2
  212.7 0.0 copy-start.9
  212.7 0.0 copy-start.14
  212.7 0.0 copy-start.16
  212.7 0.0 copy-start.17
  212.7 8.4 %multiply_subtract_fusion = (f32[192,3352]{1,0:T(8,128)}, f32[192,3352]{1,0:T(8,128)}, f32[192,3352]{1,0:T(8,128)}, f32[192,3352]{1,0:T(8,128)}) fusion(f32[192,3352]{1,0:T(8,128)} %win_hbm.1, f32[192,3352]{1,0:T(8,128)} %param.16, f32[192,3352]{1,0:T(8,128)} %param.17, bf16[192,3584]{1,0:T(8,128)(2,1)} %copy-done.5), kind=kLoop, calls=%fused_computation.4 | loop fusion | flops 10297344 | bytes 19307520 | tf_op jit(solution)/shard_map/sub | solution.py:1131
  221.1 0.0 copy-done.9
  221.1 0.0 copy-done.14
  221.1 0.0 copy-done.16
  221.1 0.0 copy-done.17
  221.1 0.0 copy-start.4
  221.1 2.4 %multiply_subtract_fusion.1 = (f32[384,768]{1,0:T(8,128)}, f32[384,768]{1,0:T(8,128)}, f32[384,768]{1,0:T(8,128)}, f32[384,768]{1,0:T(8,128)}) fusion(f32[384,768]{1,0:T(8,128)S(1)} %copy-done.14, f32[384,768]{1,0:T(8,128)S(1)} %copy-done.16, f32[384,768]{1,0:T(8,128)S(1)} %copy-done.17, bf16[384,768]{1,0:T(8,128)(2,1)S(1)} %copy-done.9), kind=kLoop, calls=%fused_computation.9 | loop fusion | flops 4718592 | bytes 8847360 | tf_op jit(solution)/shard_map/sub | solution.py:1131
  223.5 0.0 copy-start.15
  223.5 0.0 copy-done.4
  223.5 1.1 copy.30
  224.7 1.3 copy-done.15
  226.0 1.7 copy.31
  (11 shorter events, 0.1 us)
Async XLA Ops:
  47.9 0.9 copy-start.6
  48.8 28.8 %copy-start.7 = (f32[16,1792]{1,0:T(8,128)S(1)}, f32[16,1792]{1,0:T(8,128)}, u32[]{:S(2)}) copy-start(f32[16,1792]{1,0:T(8,128)} %get-tuple-element.41.pm_ref) | copy-start | bytes 344068
  76.9 0.6 copy-start.12
  77.5 80.2 %copy-start = (bf16[1,1024,768]{2,1,0:T(8,128)(2,1)S(1)}, bf16[1,1024,768]{2,1,0:T(8,128)(2,1)}, u32[]{:S(2)}) copy-start(bf16[1,1024,768]{2,1,0:T(8,128)(2,1)} %param.12) | copy-start | bytes 4718596
  77.5 80.3 %copy-start.1 = (bf16[1024,768]{1,0:T(8,128)(2,1)S(1)}, bf16[1024,768]{1,0:T(8,128)(2,1)}, u32[]{:S(2)}) copy-start(bf16[1024,768]{1,0:T(8,128)(2,1)} %get-tuple-element.38.normed_hbm) | copy-start | bytes 4718596
  152.0 0.8 copy-start.8
  152.8 0.8 copy-start.10
  153.6 0.6 copy-start.13
  157.8 1.4 copy-start.2
  159.2 1.1 copy-start.11
  160.3 51.6 %copy-start.18 = (f32[2834]{0:T(1024)S(1)}, f32[2834]{0:T(1024)}, u32[]{:S(2)}) copy-start(f32[2834]{0:T(1024)} %param.15) | copy-start | bytes 34012
  160.3 51.7 %copy-start.19 = (f32[2834]{0:T(1024)S(1)}, f32[2834]{0:T(1024)}, u32[]{:S(2)}) copy-start(f32[2834]{0:T(1024)} %param.20) | copy-start | bytes 34012
  160.3 51.7 %copy-start.20 = (f32[2834]{0:T(1024)S(1)}, f32[2834]{0:T(1024)}, u32[]{:S(2)}) copy-start(f32[2834]{0:T(1024)} %param.21) | copy-start | bytes 34012
  209.7 1.1 copy-start.3
  210.8 1.1 copy-start.5
  212.7 8.4 %copy-start.9 = (bf16[384,768]{1,0:T(8,128)(2,1)S(1)}, bf16[384,768]{1,0:T(8,128)(2,1)}, u32[]{:S(2)}) copy-start(bf16[384,768]{1,0:T(8,128)(2,1)} %copy-done.8) | copy-start | bytes 1769476
  212.7 8.4 %copy-start.14 = (f32[384,768]{1,0:T(8,128)S(1)}, f32[384,768]{1,0:T(8,128)}, u32[]{:S(2)}) copy-start(f32[384,768]{1,0:T(8,128)} %wout_hbm.1) | copy-start | bytes 3538948
  212.7 8.4 %copy-start.16 = (f32[384,768]{1,0:T(8,128)S(1)}, f32[384,768]{1,0:T(8,128)}, u32[]{:S(2)}) copy-start(f32[384,768]{1,0:T(8,128)} %param.18) | copy-start | bytes 3538948
  212.7 8.4 %copy-start.17 = (f32[384,768]{1,0:T(8,128)S(1)}, f32[384,768]{1,0:T(8,128)}, u32[]{:S(2)}) copy-start(f32[384,768]{1,0:T(8,128)} %param.19) | copy-start | bytes 3538948
  221.1 2.4 %copy-start.4 = (bf16[1024,768]{1,0:T(8,128)(2,1)S(1)}, bf16[1024,768]{1,0:T(8,128)(2,1)}, u32[]{:S(2)}) copy-start(bf16[1024,768]{1,0:T(8,128)(2,1)} %copy-done.3) | copy-start | bytes 4718596
  223.5 2.5 %copy-start.15 = (f32[1024,768]{1,0:T(8,128)S(1)}, f32[1024,768]{1,0:T(8,128)}, u32[]{:S(2)}) copy-start(f32[1024,768]{1,0:T(8,128)} %get-tuple-element.59) | copy-start | bytes 9437188

commit v5 on v4

--- a/solution.py
+++ b/solution.py
@@ -65,22 +65,24 @@
     return jnp.where(n == head + offset(k), 1.0, 0.0).astype(bf16)
 
 
-PIECES_OUT = 3
-WIDE = 512
-EARLY = PIECES_OUT + INNER // WIDE
 SLIM = 256
+PIECES_OUT = 2 * (D // SLIM)
+EARLY = PIECES_OUT + INNER // SLIM
 LATE = (CHANNELS + 256) // SLIM
 TALL = 192
 HALF = TALL // 2
 NEAR = 4
 QUARTER = TALL // NEAR
 FIRST_TICK = 1
-STAGE_TICKS = (1, 3, 4, 5, 6, 7)
+STAGE_TICKS = (1, 3, 5, 7, 9, 11)
+TICKS = 3
+STAGE_ORDER = (0, 5, 4, 3, 2, 1)
 MESH = pl.DeviceIdType.MESH
+VMEM = 64 * 1024 * 1024 - 256 * 1024
 
 
 class Reducer:
-    def __init__(self, far, g, rc, ry, rx, rz, rf, f, cs, cr, ys, yr, xs, xr, zs, zr, fs, fr, gs, gr, hs, hr):
+    def __init__(self, far, mixed, g, rb, rc, ry, rx, rz, rf, f, cs, cr, ys, yr, xs, xr, zs, zr, fs, fr, gs, gr, hs, hr):
         dp = lax.axis_index("dp")
         shard = lax.axis_index("shard")
         xbit = dp % 2
@@ -151,20 +153,59 @@
         def pair_arrival(p):
             return remote(f.at[p, :, give], f.at[p, :, give], gs.at[p], gr.at[p], x_id)
 
-        def to_y(p):
+        def wide_x_copy(p):
+            return remote(g.at[p, core, :, :, give], rb.at[p], ys.at[p], yr.at[p], x_id)
+
+        def slim_y_copy(p):
+            return remote(g.at[p, core, 1 - ybit, :, keep], rx.at[p], xs.at[p], xr.at[p], y_id)
+
+        def either(p, y_first, x_first):
+            if not mixed:
+                y_first()
+                return
+
+            @pl.when(p % 2 == 0)
+            def _():
+                y_first()
+
+            @pl.when(p % 2 == 1)
+            def _():
+                x_first()
+
+        def to_first(p):
             core_copy(p).wait_recv()
-            other = 1 - ybit
-            g[p, core, other] = (g[p, core, other].astype(f32) + rc[p, other].astype(f32)).astype(bf16)
-            y_copy(p).start()
-
-        def to_x(p):
-            y_copy(p).wait_recv()
-            total = g[p, core, ybit].astype(f32) + rc[p, ybit].astype(f32) + ry[p].astype(f32)
-            g[p, core, ybit] = total.astype(bf16)
-            x_copy(p).start()
+
+            def y_first():
+                other = 1 - ybit
+                g[p, core, other] = (g[p, core, other].astype(f32) + rc[p, other].astype(f32)).astype(bf16)
+                y_copy(p).start()
+
+            def x_first():
+                for n in range(2):
+                    total = g[p, core, n, :, give].astype(f32) + rc[p, n, :, give].astype(f32)
+                    g[p, core, n, :, give] = total.astype(bf16)
+                wide_x_copy(p).start()
+
+            either(p, y_first, x_first)
+
+        def to_second(p):
+            def y_first():
+                y_copy(p).wait_recv()
+                total = g[p, core, ybit].astype(f32) + rc[p, ybit].astype(f32) + ry[p].astype(f32)
+                g[p, core, ybit] = total.astype(bf16)
+                x_copy(p).start()
+
+            def x_first():
+                wide_x_copy(p).wait_recv()
+                for n in range(2):
+                    total = g[p, core, n, :, keep].astype(f32) + rc[p, n, :, keep].astype(f32) + rb[p, n].astype(f32)
+                    g[p, core, n, :, keep] = total.astype(bf16)
+                slim_y_copy(p).start()
+
+            either(p, y_first, x_first)
 
         def to_z(p):
-            x_copy(p).wait_recv()
+            either(p, lambda: x_copy(p).wait_recv(), lambda: slim_y_copy(p).wait_recv())
             g[p, core, ybit, :, keep] = (g[p, core, ybit, :, keep].astype(f32) + rx[p].astype(f32)).astype(bf16)
             for k in range(1, NEAR):
                 z_copy(p, k).start()
@@ -204,8 +245,15 @@
         def drain(count):
             def one(p, _):
                 core_copy(p).wait_send()
-                y_copy(p).wait_send()
-                x_copy(p).wait_send()
+                def y_first():
+                    y_copy(p).wait_send()
+                    x_copy(p).wait_send()
+
+                def x_first():
+                    wide_x_copy(p).wait_send()
+                    slim_y_copy(p).wait_send()
+
+                either(p, y_first, x_first)
                 for k in range(1, NEAR):
                     z_copy(p, k).wait_send()
                     spread_copy(p, k).wait_send()
@@ -215,14 +263,16 @@
             lax.fori_loop(0, count, one, 0)
 
         self.g, self.f, self.greet, self.drain = g, f, greet, drain
+        self.core_id, self.y_id, self.x_id, self.near_id, self.far_id = core_id, y_id, x_id, near_id, far_id
         self.start = lambda p: core_copy(p).start()
-        self.stages = (to_y, to_x, to_z, to_spread, to_pair, finish)
-
-
-def reducer_scratch(far, count, wide):
+        self.stages = (to_first, to_second, to_z, to_spread, to_pair, finish)
+
+
+def reducer_scratch(far, mixed, count, wide):
     dma = pltpu.SemaphoreType.DMA
     return [
         pltpu.VMEM((count, 2, 2, TALL, wide), bf16),
+        pltpu.VMEM((count if mixed else 1, 2, TALL, wide // 2), bf16),
         pltpu.VMEM((count, 2, TALL, wide), bf16),
         pltpu.VMEM((count, TALL, wide), bf16),
         pltpu.VMEM((count, TALL, wide // 2), bf16),
@@ -344,7 +394,7 @@
     step = pl.program_id(0)
     blocks = pl.num_programs(0)
     chunk = blocks - 1 - step
-    red = Reducer(far, *rest)
+    red = Reducer(far, False, *rest)
     g, f = red.g, red.f
     copies = [
         pltpu.make_async_copy(mixer_hbm, mixer, in_sem.at[0]),
@@ -353,50 +403,48 @@
         pltpu.make_async_copy(dz_hbm, dz, in_sem.at[3]),
     ]
 
-    def result_out(p, h):
+    def result_out(p):
+        rows = pl.ds(pl.multiple_of(p % 2 * TALL, 64), TALL)
         return pltpu.make_async_copy(
-            f.at[p, :, 256 * h : 256 * h + 256],
-            gout_hbm.at[TALL * h : TALL * h + TALL, pl.ds(pl.multiple_of(p * 256, 256), 256)],
-            res_sem.at[p, h],
+            f.at[p], gout_hbm.at[rows, pl.ds(pl.multiple_of(p // 2 * SLIM, SLIM), SLIM)], res_sem.at[p]
         )
 
     def result_z(p):
         return pltpu.make_async_copy(
-            f.at[p], gz_hbm.at[:, pl.ds(pl.multiple_of((p - PIECES_OUT) * WIDE, WIDE), WIDE)], res_sem.at[p, 0]
+            f.at[p], gz_hbm.at[:, pl.ds(pl.multiple_of((p - PIECES_OUT) * SLIM, SLIM), SLIM)], res_sem.at[p]
         )
 
     def compute_out(p):
-        right = cot[:, pl.ds(pl.multiple_of(p * 256, 256), 256)]
+        right = cot[:, pl.ds(pl.multiple_of(p // 2 * SLIM, SLIM), SLIM)]
         for owner in range(4):
             left = mixer[:, 2 * TALL * owner : 2 * TALL * (owner + 1)]
             value = mm_rows(left, right).astype(bf16)
             for h in range(2):
-                g[p, owner % 2, owner // 2, :, 256 * h : 256 * h + 256] = value[TALL * h : TALL * h + TALL]
+                g[p + h, owner % 2, owner // 2] = value[TALL * h : TALL * h + TALL]
 
     def compute_z(p):
-        value = mm_rows(normed[...], dz[:, pl.ds(pl.multiple_of((p - PIECES_OUT) * WIDE, WIDE), WIDE)]).astype(bf16)
+        value = mm_rows(normed[...], dz[:, pl.ds(pl.multiple_of((p - PIECES_OUT) * SLIM, SLIM), SLIM)]).astype(bf16)
         for owner in range(4):
             g[p, owner % 2, owner // 2] = value[TALL * owner : TALL * (owner + 1)]
 
     def tick(t):
         def at(delay):
-            since = t - FIRST_TICK - delay
-            p = 2 * ((since + 24) // 3 - 8) + (since + 24) % 3
-            return p, (since >= 0) & ((since + 24) % 3 < 2) & (p < EARLY)
+            p = t - FIRST_TICK - delay
+            return p, (p >= 0) & (p < EARLY)
 
         @pl.when(t == FIRST_TICK)
         def _():
             copies[0].wait()
             copies[1].wait()
 
-        @pl.when(t == FIRST_TICK + PIECES_OUT // 2 * 3 + PIECES_OUT % 2)
+        @pl.when(t == FIRST_TICK + PIECES_OUT)
         def _():
             copies[2].wait()
             copies[3].wait()
 
         p0, on0 = at(0)
 
-        @pl.when(on0 & (p0 < PIECES_OUT))
+        @pl.when(on0 & (p0 < PIECES_OUT) & (p0 % 2 == 0))
         def _():
             compute_out(p0)
 
@@ -408,19 +456,18 @@
         def _():
             red.start(p0)
 
-        for stage, delay in zip(red.stages, STAGE_TICKS):
-            p, on = at(delay)
+        for n in STAGE_ORDER:
+            p, on = at(STAGE_TICKS[n])
 
             @pl.when(on)
-            def _(stage=stage, p=p):
-                stage(p)
+            def _(n=n, p=p):
+                red.stages[n](p)
 
         p, on = at(STAGE_TICKS[-1])
 
         @pl.when(on & (p < PIECES_OUT))
         def _():
-            for h in range(2):
-                result_out(p, h).start()
+            result_out(p).start()
 
         @pl.when(on & (p >= PIECES_OUT))
         def _():
@@ -438,7 +485,7 @@
             copy.start()
         red.greet()
 
-    tick(2 * step)
+    tick(TICKS * step)
 
     lane = lax.broadcasted_iota(jnp.int32, (Q, 128), 1)
     row = lax.broadcasted_iota(jnp.int32, (Q, 128), 0)
@@ -484,8 +531,8 @@
     sums = jnp.zeros((Q, 128), f32)
     carry = jnp.zeros((8, 128), f32)
     for j in range(PAIRS):
-        if j == PAIRS // 2:
-            tick(2 * step + 1)
+        if j and j % (PAIRS // TICKS) == 0:
+            tick(TICKS * step + j // (PAIRS // TICKS))
         col = slice(128 * j, 128 * j + 128)
         shifted = taps(128 * j)
         c = conv(shifted, 128 * j)
@@ -554,8 +601,7 @@
     def _():
         red.drain(EARLY)
         for p in range(PIECES_OUT):
-            for h in range(2):
-                result_out(p, h).wait()
+            result_out(p).wait()
         for p in range(PIECES_OUT, EARLY):
             result_z(p).wait()
 
@@ -604,7 +650,7 @@
             pltpu.VMEM((8, CHANNELS), f32),
             pltpu.VMEM((Q, INNER), f32),
         ],
-        compiler_params=pltpu.CompilerParams(vmem_limit_bytes=48 * 1024 * 1024),
+        compiler_params=pltpu.CompilerParams(vmem_limit_bytes=VMEM - 384 * 1024),
         name="mix_forward",
     )(proj, dmix, pm, es)
 
@@ -615,7 +661,7 @@
     far = mesh_dp // 2 // NEAR
     any_space = pl.BlockSpec(memory_space=pl.ANY)
     dma = pltpu.SemaphoreType.DMA
-    assert 2 * blocks > FIRST_TICK + (EARLY - 1) // 2 * 3 + (EARLY - 1) % 2 + STAGE_TICKS[-1]
+    assert TICKS * blocks >= FIRST_TICK + EARLY + STAGE_TICKS[-1]
 
     def rows(width):
         return pl.BlockSpec((Q, width), lambda i: (blocks - 1 - i, 0))
@@ -653,27 +699,28 @@
             pltpu.VMEM((length, D), bf16),
             pltpu.VMEM((length, D), bf16),
             pltpu.VMEM((length, INNER), bf16),
-            dma((4,)), dma((EARLY, 2)),
-        ] + reducer_scratch(far, EARLY, WIDE),
+            dma((4,)), dma((EARLY,)),
+        ] + reducer_scratch(far, False, EARLY, SLIM),
         compiler_params=pltpu.CompilerParams(
-            collective_id=3, has_side_effects=True, vmem_limit_bytes=48 * 1024 * 1024
+            collective_id=3, has_side_effects=True, vmem_limit_bytes=VMEM - 384 * 1024
         ),
         name="mix_backward",
     )(proj, proj, ds, st, dt, cum, ps, pm, es, mixer, cot, normed, dz)
 
 
-BACK_SLOT = 1
-OUT_SLOT = 7
+BACK_SLOT = LATE
+OUT_SLOT = BACK_SLOT + 8
+LATE_TICKS = (1, 5, 7, 9, 11, 12)
 
 
 def reduce_kernel(
     far,
     normed_hbm, cot_hbm, mixer_hbm, dz_hbm, du_hbm, x_hbm, w_hbm, wo_hbm, gz_hbm, pm_ref, vec_ref,
-    gin_hbm, dx_hbm, out_hbm,
+    gin_hbm, dx_hbm, out_hbm, gg_ref,
     normed, cot, mixer, dproj, x, w, wo, gz, dn, dgain, dx, out,
-    in_sem, out_sem, dx_sem, res_sem, gz_sem, *rest,
+    mine, theirs, in_sem, out_sem, dx_sem, res_sem, gz_sem, ss, sr, *rest,
 ):
-    red = Reducer(far, *rest)
+    red = Reducer(far, True, *rest)
     g, f = red.g, red.f
     copies = [
         pltpu.make_async_copy(normed_hbm, normed, in_sem.at[0]),
@@ -705,16 +752,43 @@
         return jnp.sum(dgain[:, 128 * k : 128 * k + 128], axis=0, keepdims=True)
 
     def compute_small():
-        pieces = [dgain_row(k) for k in range(D // 128)] + [jnp.zeros((16 - D // 128, 128), f32)]
-        block = jnp.concatenate(pieces, axis=0).astype(bf16)
         for owner in range(4):
             g[LATE - 1, owner % 2, owner // 2, :, SLIM - 128 :] = jnp.zeros((TALL, 128), bf16)
             g[LATE - 1, owner % 2, owner // 2, 0:32, SLIM - 128 :] = vec_ref[owner].astype(bf16)
-            g[LATE - 1, owner % 2, owner // 2, 32:48, SLIM - 128 :] = block
-
-    def cover_back(n):
+
+    rounds = [[red.core_id], [red.y_id], [red.x_id], [red.near_id(k) for k in range(1, NEAR)]]
+    if far > 1:
+        rounds.append([red.far_id(k) for k in range(1, far)])
+    width = max(NEAR, far) - 1
+
+    def sum_copy(r, k):
+        there = len(rounds[r]) - 1 - k
+        return pltpu.make_async_remote_copy(
+            src_ref=mine.at[r], dst_ref=theirs.at[r * width + there], send_sem=ss.at[r * width + k],
+            recv_sem=sr.at[r * width + there], device_id=rounds[r][k], device_id_type=MESH,
+        )
+
+    def sum_start(r):
+        for k in range(len(rounds[r])):
+            sum_copy(r, k).start()
+
+    def sum_finish(r):
+        total = mine[r]
+        for k in range(len(rounds[r])):
+            sum_copy(r, len(rounds[r]) - 1 - k).wait_recv()
+        if len(rounds[r]) == 3:
+            return (total + theirs[r * width + 1]) + (theirs[r * width] + theirs[r * width + 2])
+        for k in range(len(rounds[r])):
+            total = total + theirs[r * width + k]
+        return total
+
+    def back_left(n):
         rows = pl.ds(pl.multiple_of(n * 256, 256), 256)
-        dn[...] = mm_t(dproj[rows, :], w[...])
+        dn[:, 0 : D // 2] = mm_t(dproj[rows, :], w[0 : D // 2, :])
+
+    def back_right(n):
+        rows = pl.ds(pl.multiple_of(n * 256, 256), 256)
+        dn[:, D // 2 :] = mm_t(dproj[rows, :], w[D // 2 :, :])
 
         def part(k, _):
             sub = pl.ds(pl.multiple_of(k * 32, 32), 32)
@@ -746,15 +820,23 @@
 
     kept = pltpu.make_async_copy(gz, gin_hbm.at[:, 0:INNER], gz_sem.at[0])
     tiles = x.shape[0] // 256
-    per_slot = tiles // 4
+    assert tiles == 4
     dgain[...] = jnp.zeros_like(dgain)
+    mine[...] = jnp.zeros_like(mine)
     copies[0].wait()
     copies[1].wait()
 
     def slot(i, _):
-        @pl.when(i < LATE - 1)
+        @pl.when(i < LATE)
         def _():
             compute_in(i)
+
+        @pl.when(i == LATE - 1)
+        def _():
+            compute_small()
+
+        @pl.when(i < LATE)
+        def _():
             red.start(i)
 
         @pl.when(i == BACK_SLOT)
@@ -762,34 +844,47 @@
             for copy in copies[2:6]:
                 copy.wait()
 
-        @pl.when((i >= BACK_SLOT) & (i < BACK_SLOT + 4))
-        def _():
-            lax.fori_loop(0, per_slot, lambda k, c: (cover_back((i - BACK_SLOT) * per_slot + k), c)[1], 0)
-
-        @pl.when(i == LATE - 1)
-        def _():
-            compute_in(i)
-            compute_small()
-            red.start(i)
+        back = i - BACK_SLOT
+
+        @pl.when((back >= 0) & (back < 2 * tiles) & (back % 2 == 0))
+        def _():
+            back_left(back // 2)
+
+        @pl.when((back >= 0) & (back < 2 * tiles) & (back % 2 == 1))
+        def _():
+            back_right(back // 2)
 
         @pl.when(i == OUT_SLOT)
         def _():
             for copy in copies[6:]:
                 copy.wait()
             kept.start()
-
-        @pl.when((i >= OUT_SLOT) & (i < OUT_SLOT + 4))
-        def _():
-            lax.fori_loop(0, per_slot, lambda k, c: (cover_out((i - OUT_SLOT) * per_slot + k), c)[1], 0)
-
-        for n, stage in enumerate(red.stages):
-            p = i - n
+            for k in range(D // 128):
+                mine[0, k : k + 1, :] = dgain_row(k)
+            sum_start(0)
+
+        for r in range(1, len(rounds) + 1):
+            @pl.when(i == OUT_SLOT + r)
+            def _(r=r):
+                total = sum_finish(r - 1)
+                if r < len(rounds):
+                    mine[r] = total
+                    sum_start(r)
+                else:
+                    gg_ref[...] = total
+
+        @pl.when((i >= OUT_SLOT) & (i < OUT_SLOT + tiles))
+        def _():
+            cover_out(i - OUT_SLOT)
+
+        for n in STAGE_ORDER:
+            p = i - LATE_TICKS[n]
 
             @pl.when((p >= 0) & (p < LATE))
-            def _(stage=stage, p=p):
-                stage(p)
-
-        done = i - len(red.stages) + 1
+            def _(n=n, p=p):
+                red.stages[n](p)
+
+        done = i - LATE_TICKS[-1]
 
         @pl.when((done >= 0) & (done < LATE))
         def _():
@@ -797,7 +892,10 @@
 
         return 0
 
-    lax.fori_loop(0, LATE + 5, slot, 0)
+    lax.fori_loop(0, max(LATE + LATE_TICKS[-1], OUT_SLOT + len(rounds) + 1), slot, 0)
+    for r in range(len(rounds)):
+        for k in range(len(rounds[r])):
+            sum_copy(r, k).wait_send()
     red.drain(LATE)
     kept.wait()
     for p in range(LATE):
@@ -816,11 +914,12 @@
     return pl.pallas_call(
         functools.partial(reduce_kernel, far),
         in_specs=[any_space] * 9 + [vmem] * 2,
-        out_specs=[any_space] * 3,
+        out_specs=[any_space] * 3 + [vmem],
         out_shape=[
             jax.ShapeDtypeStruct((TALL, WIDTH), bf16),
             jax.ShapeDtypeStruct((length, D), f32),
             jax.ShapeDtypeStruct((length, D), bf16),
+            jax.ShapeDtypeStruct((8, 128), f32),
         ],
         scratch_shapes=[
             pltpu.VMEM((length, D), bf16),
@@ -835,10 +934,13 @@
             pltpu.VMEM((8, D), f32),
             pltpu.VMEM((length, D), f32),
             pltpu.VMEM((length, D), bf16),
+            pltpu.VMEM((5, 8, 128), f32),
+            pltpu.VMEM((5 * (max(NEAR, far) - 1), 8, 128), f32),
             dma((9,)), dma((length // 256,)), dma((length // 256,)), dma((LATE,)), dma((1,)),
-        ] + reducer_scratch(far, LATE, SLIM),
+            dma((5 * (max(NEAR, far) - 1),)), dma((5 * (max(NEAR, far) - 1),)),
+        ] + reducer_scratch(far, True, LATE, SLIM),
         compiler_params=pltpu.CompilerParams(
-            collective_id=1, has_side_effects=True, vmem_limit_bytes=44 * 1024 * 1024
+            collective_id=1, has_side_effects=True, vmem_limit_bytes=VMEM
         ),
         name="reduce_grads",
     )(normed, cot, mixer, dz, du, x, w, wo, gz, pm, vec)
@@ -1005,13 +1107,11 @@
     outs = [pltpu.make_async_copy(normed, normed_hbm, keep_sem.at[0])]
     outs[0].start()
 
-    def dmix_half(side, n):
-        def tile(t, _):
-            start = pl.multiple_of(side * (INNER // 2) + t * 256, 256)
-            dstage[n, :, pl.ds(pl.multiple_of(t * 256, 256), 256)] = mm_t(cot[...], wo[pl.ds(start, 256), :])
-            return 0
-
-        lax.fori_loop(0, INNER // 512, tile, 0)
+    def dmix_tile(side, n, t):
+        start = pl.multiple_of(side * (INNER // 2) + t * 256, 256)
+        dstage[n, :, 256 * t : 256 * t + 256] = mm_t(cot[...], wo[pl.ds(start, 256), :])
+
+    def dmix_out(side, n):
         target = dmix_hbm.at[:, pl.ds(pl.multiple_of(side * (INNER // 2), 256), INNER // 2)]
         copy = pltpu.make_async_copy(dstage.at[n], target, dmix_sem.at[n])
         copy.start()
@@ -1030,30 +1130,10 @@
         first_arrival(k).wait_recv()
         second_arrival(k).wait_recv()
 
-    loads[2].wait()
-    core_wo_in.wait_recv()
-    pass_on(0)
-    dmix_half(ybit, 0)
-    pass_on(1)
-    pass_second(0)
-    pass_on(2)
-    pass_second(1)
-    core_w_in.wait_recv()
     projected = []
-    for k in range(GROUPS_OUT, GROUPS + 1):
-        if k < GROUPS:
-            pass_on(k)
-        pass_second(k - 1)
-        if k == GROUPS_OUT:
-            for n in range(GROUPS_OUT):
-                arrived(n)
-            dmix_half(1 - ybit, 1)
-            copy = pltpu.make_async_copy(wo, wo_hbm, keep_sem.at[1])
-            copy.start()
-            outs.append(copy)
-            continue
-        n = k - 1 - GROUPS_OUT
-        arrived(k - 1)
+
+    def project(n):
+        arrived(n + GROUPS_OUT)
         columns = slice(512 * n, 512 * n + 512)
         if n >= 2:
             projected[n - 2].wait()
@@ -1064,6 +1144,32 @@
         copy = pltpu.make_async_copy(w.at[:, columns], w_hbm.at[:, columns], w_sem.at[n])
         copy.start()
         outs.append(copy)
+
+    loads[2].wait()
+    core_wo_in.wait_recv()
+    dmix_tile(ybit, 0, 0)
+    for k in range(GROUPS + 2):
+        if k < GROUPS:
+            pass_on(k)
+        if 1 <= k <= GROUPS:
+            pass_second(k - 1)
+        if k < 2:
+            dmix_tile(ybit, 0, k + 1)
+        if k == 1:
+            dmix_out(ybit, 0)
+        if k == GROUPS_OUT + 1:
+            for n in range(GROUPS_OUT):
+                arrived(n)
+            copy = pltpu.make_async_copy(wo, wo_hbm, keep_sem.at[1])
+            copy.start()
+            outs.append(copy)
+            core_w_in.wait_recv()
+        if GROUPS_OUT + 1 <= k < 2 * GROUPS_OUT + 1:
+            dmix_tile(1 - ybit, 1, k - GROUPS_OUT - 1)
+        if k == 2 * GROUPS_OUT:
+            dmix_out(1 - ybit, 1)
+        if k >= GROUPS_OUT + 2:
+            project(k - GROUPS_OUT - 2)
     for copy in projected[-2:] + outs:
         copy.wait()
     for copy in small + [core_wo, core_w]:
@@ -1109,7 +1215,7 @@
             dma((GROUPS,)), dma((GROUPS,)), dma((GROUPS,)), dma((GROUPS,)),
         ],
         compiler_params=pltpu.CompilerParams(
-            collective_id=2, has_side_effects=True, vmem_limit_bytes=56 * 1024 * 1024
+            collective_id=2, has_side_effects=True, vmem_limit_bytes=VMEM
         ),
         name="gather_project",
     )(inputs, cot, w_in, w_out, vec)
@@ -1157,13 +1263,13 @@
     dnw = dnw.sum(axis=0)
     small = jnp.concatenate([dcw.reshape(-1), dcb, dhp[0, :HEADS], dhp[1, :HEADS], dskip, dnw, jnp.zeros((D,), f32)])
     small = jnp.pad(small.reshape(owners, vec_len), ((0, 0), (0, VEC_ROWS * 128 - vec_len))).reshape(owners, VEC_ROWS, 128)
-    gin, input_grad, outputs = reduce_grads(
+    gin, input_grad, outputs, gain_sum = reduce_grads(
         lax.axis_size("dp"), normed_low, cot, mixer_low, dz, du, rows_low, w_all, w_out_all, gz, pm, small
     )
     outputs = outputs.reshape(inputs.shape)
     input_grad = input_grad.reshape(inputs.shape)
     tail = gin[:, WIDTH - 128 :].astype(f32)
-    gain_grad = jnp.pad(tail[32 : 32 + D // 128].reshape(D), (owners * vec_len - D, 0))
+    gain_grad = jnp.pad(gain_sum[: D // 128].reshape(D), (owners * vec_len - D, 0))
     start = lax.axis_index("shard") * vec_len
     grad_vec = tail[:32].reshape(32 * 128)[:vec_len] + lax.dynamic_slice(gain_grad, (start,), (vec_len,))
     grad_in = gin[:, :in_width].astype(f32)

time: 228 us -> 217 us (0.952)
  local copies, waits for them, and re-layouts: 14.9 us -> 7.75 us
  Pallas kernels: 197 us -> 191 us
    unnamed x46 -> x24, local copies, waits for them, and re-layouts: 12.6 us -> 4.8 us
    pallas_call x1, Pallas kernels: 74.4 us -> 67.2 us  [mix_backward(): pl.pallas_call(functools.partial(backward_kernel, far), grid=(blocks,), i...]
where the time goes in v5:
time: 217 us; the launch traced here: 216 us
  Pallas kernels  191 us (88%)
  other arithmetic  17.4 us (8%)
  local copies, waits for them, and re-layouts  7.75 us (4%)
    pallas_call x1, Pallas kernels, mix_backward(): pl.pallas_call(functools.partial(backward_kernel, far), grid=(blocks,), i...  67.2 us
    pallas_call x1, Pallas kernels, reduce_grads(): pl.pallas_call(functools.partial(reduce_kernel, far), in_specs=[any_space...  50 us
    pallas_call x1, Pallas kernels, gather_project(): pl.pallas_call(functools.partial(gather_kernel, vec_len), in_specs=[any_s...  44.6 us
    pallas_call x1, Pallas kernels, mix_forward(): pl.pallas_call(forward_kernel, grid=(blocks,), in_specs=[rows(WIDTH), row...  28.7 us
    sub x3, other arithmetic, adam(): return (param - rate * (update + decay * param), new_first, new_second)  11.5 us
    unnamed x24, local copies, waits for them, and re-layouts  4.8 us

profile of v5, /device:TPU:0, one launch (start us, length us, event | category | flops | bytes accessed | tf_op | source)
XLA Modules:
  0.0 216.5 jit_solution(8945284951800974395)
XLA Ops:
  0.6 1.3 pad_bitcast_fusion.1.vec_ref
  2.0 44.6 %gather_project.1 = (f32[1024,3584]{1,0:T(8,128)}, f32[1024,1536]{1,0:T(8,128)}, bf16[1024,768]{1,0:T(8,128)(2,1)}, bf16[768,3584]{1,0:T(8,128)(2,1)}, bf16[1536,768]{1,0:T(8,128)(2,1)}, /*index=5*/f32[16,1792]{1,0:T(8,128)}) custom-call(bf16[1024,768]{1,0:T(8,128)(2,1)} %bitcast.22, bf16[1024,768]{1,0:T(8,128)(2,1)} %bitcast.19, f32[192,3352]{1,0:T(8,128)} %win_hbm.1, ...), custom_call_target="tpu_custom_call" | custom-call | tf_op jit(solution)/shard_map/gather_project/pallas_call | solution.py:1189
  46.6 0.1 add_add_fusion
  46.6 2.3 %fusion.es_ref = bf16[12,512,128]{2,1,0:T(8,128)(2,1)} fusion(s32[12,512]{1,0:T(8,128)S(1)} %add_add_fusion), kind=kLoop, calls=%fused_computation.2 | loop fusion | flops 1572864 | bytes 1597440 | tf_op jit(solution)/shard_map/convert_element_type | solution.py:614
  49.0 28.7 %mix_forward.1 = (bf16[1024,1536]{1,0:T(8,128)(2,1)}, bf16[1024,1536]{1,0:T(8,128)(2,1)}, bf16[1024,1536]{1,0:T(8,128)(2,1)}, bf16[8,128,1536]{2,1,0:T(8,128)(2,...) custom-call(f32[1024,3584]{1,0:T(8,128)} %get-tuple-element.40.proj_ref.prev_ref, ...), custom_call_target="tpu_custom_call" | custom-call | tf_op jit(solution)/shard_map/mix_forward/pallas_call | solution.py:628
  77.7 0.0 copy-start.7
  77.7 67.2 %mix_backward.1 = (bf16[1024,2048]{1,0:T(8,128)(2,1)}, f32[4,8,1792]{2,1,0:T(8,128)}, f32[8,1792]{1,0:T(8,128)}, f32[2,8,128]{2,1,0:T(8,128)}, f32[8,1536]{1,0:T...) custom-call(f32[1024,3584]{1,0:T(8,128)} %get-tuple-element.40.proj_ref.prev_ref, ...), custom_call_target="tpu_custom_call" | custom-call | tf_op jit(solution)/shard_map/mix_backward/pallas_call | solution.py:669
  144.9 1.0 reduce_sum.54
  146.0 0.8 reduce_sum.57
  146.8 0.1 reshape.130
  146.8 0.1 reduce_sum.58
  147.0 0.8 reduce_sum.55
  147.8 0.7 reduce_sum.56
  148.5 0.0 copy-done.7
  148.6 0.1 concatenate.3
  148.6 0.1 reshape.131
  148.8 0.6 copy.27
  149.4 0.0 copy-start.6
  149.4 0.0 copy-start.8
  149.4 0.0 copy-start.9
  149.4 50.0 %reduce_grads.1 = (bf16[192,3584]{1,0:T(8,128)(2,1)}, f32[1024,768]{1,0:T(8,128)}, bf16[1024,768]{1,0:T(8,128)(2,1)}, f32[8,128]{1,0:T(8,128)}) custom-call(bf16[1024,768]{1,0:T(8,128)(2,1)} %get-tuple-element.39.normed_hbm, bf16[1024,768]{1,0:T(8,128)(2,1)} %bitcast.21, bf16[1024,1536]{1,0:T(8,128)(2,1)} %get-tuple-element.43.mixer_hbm, ...), custom_call_target="tpu_custom_call" | custom-call | tf_op jit(solution)/shard_map/reduce_grads/pallas_call | solution.py:914
  199.4 0.7 slice_bitcast_fusion
  200.1 0.7 slice_bitcast_fusion.1
  200.8 0.0 copy-done.6
  200.8 0.0 copy-done.8
  200.8 0.0 copy-done.9
  200.8 0.7 multiply_subtract_fusion.2
  201.5 0.0 copy-start
  201.5 0.0 copy-start.3
  201.5 0.0 copy-start.4
  201.5 0.0 copy-start.5
  201.5 8.4 %multiply_subtract_fusion = (f32[192,3352]{1,0:T(8,128)}, f32[192,3352]{1,0:T(8,128)}, f32[192,3352]{1,0:T(8,128)}, f32[192,3352]{1,0:T(8,128)}) fusion(f32[192,3352]{1,0:T(8,128)} %win_hbm.1, f32[192,3352]{1,0:T(8,128)} %param.16, f32[192,3352]{1,0:T(8,128)} %param.17, bf16[192,3584]{1,0:T(8,128)(2,1)} %get-tuple-element.61), kind=kLoop, calls=%fused_computation.4 | loop fusion | flops 10297344 | bytes 19307520 | tf_op jit(solution)/shard_map/sub | solution.py:1237
  209.9 0.0 copy-done
  209.9 0.0 copy-done.3
  209.9 0.0 copy-done.4
  209.9 0.0 copy-done.5
  209.9 0.0 copy-start.2
  209.9 2.4 %multiply_subtract_fusion.1 = (f32[384,768]{1,0:T(8,128)}, f32[384,768]{1,0:T(8,128)}, f32[384,768]{1,0:T(8,128)}, f32[384,768]{1,0:T(8,128)}) fusion(f32[384,768]{1,0:T(8,128)S(1)} %copy-done, f32[384,768]{1,0:T(8,128)S(1)} %copy-done.3, f32[384,768]{1,0:T(8,128)S(1)} %copy-done.4, bf16[384,768]{1,0:T(8,128)(2,1)S(1)} %copy-done.5), kind=kLoop, calls=%fused_computation.9 | loop fusion | flops 4718592 | bytes 8847360 | tf_op jit(solution)/shard_map/sub | solution.py:1237
  212.4 0.0 copy-start.1
  212.4 0.0 copy-done.2
  212.4 1.1 copy.30
  213.5 1.3 copy-done.1
  214.8 1.7 copy.31
  (7 shorter events, 0.1 us)
Async XLA Ops:
  77.7 70.8 %copy-start.7 = (f32[8,1536]{1,0:T(8,128)S(1)}, f32[8,1536]{1,0:T(8,128)}, u32[]{:S(2)}) copy-start(f32[8,1536]{1,0:T(8,128)} %get-tuple-element.58) | copy-start | bytes 147460
  149.4 51.4 %copy-start.6 = (f32[2834]{0:T(1024)S(1)}, f32[2834]{0:T(1024)}, u32[]{:S(2)}) copy-start(f32[2834]{0:T(1024)} %param.15) | copy-start | bytes 34012
  149.4 51.4 %copy-start.8 = (f32[2834]{0:T(1024)S(1)}, f32[2834]{0:T(1024)}, u32[]{:S(2)}) copy-start(f32[2834]{0:T(1024)} %param.20) | copy-start | bytes 34012
  149.4 51.4 %copy-start.9 = (f32[2834]{0:T(1024)S(1)}, f32[2834]{0:T(1024)}, u32[]{:S(2)}) copy-start(f32[2834]{0:T(1024)} %param.21) | copy-start | bytes 34012
  201.5 8.4 %copy-start = (f32[384,768]{1,0:T(8,128)S(1)}, f32[384,768]{1,0:T(8,128)}, u32[]{:S(2)}) copy-start(f32[384,768]{1,0:T(8,128)} %wout_hbm.1) | copy-start | bytes 3538948
  201.5 8.4 %copy-start.3 = (f32[384,768]{1,0:T(8,128)S(1)}, f32[384,768]{1,0:T(8,128)}, u32[]{:S(2)}) copy-start(f32[384,768]{1,0:T(8,128)} %param.18) | copy-start | bytes 3538948
  201.5 8.4 %copy-start.4 = (f32[384,768]{1,0:T(8,128)S(1)}, f32[384,768]{1,0:T(8,128)}, u32[]{:S(2)}) copy-start(f32[384,768]{1,0:T(8,128)} %param.19) | copy-start | bytes 3538948
  201.5 8.4 %copy-start.5 = (bf16[384,768]{1,0:T(8,128)(2,1)S(1)}, bf16[384,768]{1,0:T(8,128)(2,1)}, u32[]{:S(2)}) copy-start(bf16[384,768]{1,0:T(8,128)(2,1)} %get-tuple-element.62) | copy-start | bytes 1769476
  209.9 2.4 %copy-start.2 = (bf16[1024,768]{1,0:T(8,128)(2,1)S(1)}, bf16[1024,768]{1,0:T(8,128)(2,1)}, u32[]{:S(2)}) copy-start(bf16[1024,768]{1,0:T(8,128)(2,1)} %get-tuple-element.59) | copy-start | bytes 4718596
  212.4 2.5 %copy-start.1 = (f32[1024,768]{1,0:T(8,128)S(1)}, f32[1024,768]{1,0:T(8,128)}, u32[]{:S(2)}) copy-start(f32[1024,768]{1,0:T(8,128)} %get-tuple-element.60) | copy-start | bytes 9437188

commit v6 on v5

--- a/solution.py
+++ b/solution.py
@@ -713,12 +713,31 @@
 LATE_TICKS = (1, 5, 7, 9, 11, 12)
 
 
+def flat_tile(sources, start, end):
+    lane = lax.broadcasted_iota(jnp.int32, (1, 128), 1)
+    out = None
+    done = 0
+    while done < 128 and start + done < end:
+        begin, length, fetch = [v for v in sources if v[0] <= start + done < v[0] + v[1]][0]
+        local = start + done - begin
+        off = local % 128
+        count = min(128 - done, 128 - off, length - local)
+        piece = fetch(local // 128)
+        shift = (done - off) % 128
+        if shift:
+            piece = pltpu.roll(piece, shift, 1)
+        out = piece if out is None else jnp.where(lane >= done, piece, out)
+        done += count
+    return out
+
+
 def reduce_kernel(
-    far,
-    normed_hbm, cot_hbm, mixer_hbm, dz_hbm, du_hbm, x_hbm, w_hbm, wo_hbm, gz_hbm, pm_ref, vec_ref,
+    far, vec_len,
+    normed_hbm, cot_hbm, mixer_hbm, dz_hbm, du_hbm, x_hbm, w_hbm, wo_hbm, gz_hbm,
+    dcw_hbm, dcb_hbm, dhp_hbm, dsk_hbm, dnw_hbm, pm_ref,
     gin_hbm, dx_hbm, out_hbm, gg_ref,
     normed, cot, mixer, dproj, x, w, wo, gz, dn, dgain, dx, out,
-    mine, theirs, in_sem, out_sem, dx_sem, res_sem, gz_sem, ss, sr, *rest,
+    mine, theirs, dcw, dcb, dhp, dsk, dnw, vec, vec_sem, in_sem, out_sem, dx_sem, res_sem, gz_sem, ss, sr, *rest,
 ):
     red = Reducer(far, True, *rest)
     g, f = red.g, red.f
@@ -733,7 +752,14 @@
         pltpu.make_async_copy(wo_hbm, wo, in_sem.at[7]),
         pltpu.make_async_copy(gz_hbm, gz, in_sem.at[8]),
     ]
-    for copy in copies:
+    small = [
+        pltpu.make_async_copy(dcw_hbm, dcw, vec_sem.at[0]),
+        pltpu.make_async_copy(dcb_hbm, dcb, vec_sem.at[1]),
+        pltpu.make_async_copy(dhp_hbm, dhp, vec_sem.at[2]),
+        pltpu.make_async_copy(dsk_hbm, dsk, vec_sem.at[3]),
+        pltpu.make_async_copy(dnw_hbm, dnw, vec_sem.at[4]),
+    ]
+    for copy in copies[:2] + small + copies[2:]:
         copy.start()
     red.greet()
 
@@ -751,10 +777,41 @@
     def dgain_row(k):
         return jnp.sum(dgain[:, 128 * k : 128 * k + 128], axis=0, keepdims=True)
 
+    def tiles_of(ref):
+        return lambda t: jnp.sum(ref[:, 128 * t : 128 * t + 128], axis=0, keepdims=True)
+
+    def skip_tile(t):
+        lane = lax.broadcasted_iota(jnp.int32, (1, 128), 1)
+        out = jnp.zeros((1, 128), f32)
+        for j in range(PAIRS):
+            row = tiles_of(dsk)(j)
+            low = jnp.sum(jnp.where(lane < 64, row, 0.0), axis=1, keepdims=True)
+            high = jnp.sum(jnp.where(lane < 64, 0.0, row), axis=1, keepdims=True)
+            out = jnp.where(lane == 2 * j, low, jnp.where(lane == 2 * j + 1, high, out))
+        return out
+
+    def lay_flat():
+        sources, begin = [], 0
+        skip = skip_tile(0)
+        parts = [(CHANNELS, tiles_of(dcw.at[k])) for k in range(CONV)] + [
+            (CHANNELS, tiles_of(dcb)), (HEADS, tiles_of(dhp.at[0])), (HEADS, tiles_of(dhp.at[1])),
+            (HEADS, lambda t: skip), (INNER, tiles_of(dnw)), (D, lambda t: jnp.zeros((1, 128), f32)),
+        ]
+        for length, fetch in parts:
+            sources.append((begin, length, fetch))
+            begin += length
+        for owner in range(4):
+            end = (owner + 1) * vec_len
+            for r in range((vec_len + 127) // 128):
+                vec[owner, r : r + 1, :] = flat_tile(sources, owner * vec_len + 128 * r, end)
+
     def compute_small():
+        for copy in small:
+            copy.wait()
+        lay_flat()
         for owner in range(4):
             g[LATE - 1, owner % 2, owner // 2, :, SLIM - 128 :] = jnp.zeros((TALL, 128), bf16)
-            g[LATE - 1, owner % 2, owner // 2, 0:32, SLIM - 128 :] = vec_ref[owner].astype(bf16)
+            g[LATE - 1, owner % 2, owner // 2, 0:32, SLIM - 128 :] = vec[owner].astype(bf16)
 
     rounds = [[red.core_id], [red.y_id], [red.x_id], [red.near_id(k) for k in range(1, NEAR)]]
     if far > 1:
@@ -823,6 +880,7 @@
     assert tiles == 4
     dgain[...] = jnp.zeros_like(dgain)
     mine[...] = jnp.zeros_like(mine)
+    vec[...] = jnp.zeros_like(vec)
     copies[0].wait()
     copies[1].wait()
 
@@ -905,15 +963,15 @@
         result_rows(n).wait()
 
 
-def reduce_grads(mesh_dp, normed, cot, mixer, dz, du, x, w, wo, gz, pm, vec):
+def reduce_grads(mesh_dp, normed, cot, mixer, dz, du, x, w, wo, gz, small, pm, vec_len):
     length = x.shape[0]
     far = mesh_dp // 2 // NEAR
     any_space = pl.BlockSpec(memory_space=pl.ANY)
     vmem = pl.BlockSpec(memory_space=pltpu.VMEM)
     dma = pltpu.SemaphoreType.DMA
     return pl.pallas_call(
-        functools.partial(reduce_kernel, far),
-        in_specs=[any_space] * 9 + [vmem] * 2,
+        functools.partial(reduce_kernel, far, vec_len),
+        in_specs=[any_space] * 14 + [vmem],
         out_specs=[any_space] * 3 + [vmem],
         out_shape=[
             jax.ShapeDtypeStruct((TALL, WIDTH), bf16),
@@ -936,14 +994,20 @@
             pltpu.VMEM((length, D), bf16),
             pltpu.VMEM((5, 8, 128), f32),
             pltpu.VMEM((5 * (max(NEAR, far) - 1), 8, 128), f32),
-            dma((9,)), dma((length // 256,)), dma((length // 256,)), dma((LATE,)), dma((1,)),
+            pltpu.VMEM((CONV, 8, CHANNELS), f32),
+            pltpu.VMEM((8, CHANNELS), f32),
+            pltpu.VMEM((2, 8, 128), f32),
+            pltpu.VMEM((8, INNER), f32),
+            pltpu.VMEM((8, INNER), f32),
+            pltpu.VMEM((4, VEC_ROWS, 128), f32),
+            dma((5,)), dma((9,)), dma((length // 256,)), dma((length // 256,)), dma((LATE,)), dma((1,)),
             dma((5 * (max(NEAR, far) - 1),)), dma((5 * (max(NEAR, far) - 1),)),
         ] + reducer_scratch(far, True, LATE, SLIM),
         compiler_params=pltpu.CompilerParams(
             collective_id=1, has_side_effects=True, vmem_limit_bytes=VMEM
         ),
         name="reduce_grads",
-    )(normed, cot, mixer, dz, du, x, w, wo, gz, pm, vec)
+    )(normed, cot, mixer, dz, du, x, w, wo, gz, *small, pm)
 
 
 GROUPS_OUT = 3
@@ -1256,15 +1320,9 @@
     du, dcw, dcb, dhp, dskip, gout, gz = mix_backward(
         lax.axis_size("dp"), proj, ds, st, dt, cum, ps, pm, es, mixer_low, cot, normed_low, dz
     )
-    dcw = dcw.sum(axis=1)
-    dcb = dcb.sum(axis=0)
-    dhp = dhp.sum(axis=1)
-    dskip = dskip.sum(axis=0).reshape(HEADS, HEADDIM).sum(axis=1)
-    dnw = dnw.sum(axis=0)
-    small = jnp.concatenate([dcw.reshape(-1), dcb, dhp[0, :HEADS], dhp[1, :HEADS], dskip, dnw, jnp.zeros((D,), f32)])
-    small = jnp.pad(small.reshape(owners, vec_len), ((0, 0), (0, VEC_ROWS * 128 - vec_len))).reshape(owners, VEC_ROWS, 128)
     gin, input_grad, outputs, gain_sum = reduce_grads(
-        lax.axis_size("dp"), normed_low, cot, mixer_low, dz, du, rows_low, w_all, w_out_all, gz, pm, small
+        lax.axis_size("dp"), normed_low, cot, mixer_low, dz, du, rows_low, w_all, w_out_all, gz,
+        (dcw, dcb, dhp, dskip, dnw), pm, vec_len
     )
     outputs = outputs.reshape(inputs.shape)
     input_grad = input_grad.reshape(inputs.shape)

time: 217 us -> 212 us (0.977)
  other arithmetic: 17.4 us -> 13.9 us
    reduce_sum x6 -> x0, other arithmetic: 3.52 us -> none  [the longest x1 1.01 us: shards(): dcw = dcw.sum(axis=1)]
    unnamed x24 -> x20, local copies, waits for them, and re-layouts: 4.8 us -> 4.16 us
where the time goes in v6:
time: 212 us
  Pallas kernels  191 us (90%)
  other arithmetic  13.9 us (7%)
  local copies, waits for them, and re-layouts  6.85 us (3%)
    pallas_call x1, Pallas kernels, mix_backward(): pl.pallas_call(functools.partial(backward_kernel, far), grid=(blocks,), i...  67.2 us
    pallas_call x1, Pallas kernels, reduce_grads(): pl.pallas_call(functools.partial(reduce_kernel, far, vec_len), in_specs=[...  50 us
    pallas_call x1, Pallas kernels, gather_project(): pl.pallas_call(functools.partial(gather_kernel, vec_len), in_specs=[any_s...  44.6 us
    pallas_call x1, Pallas kernels, mix_forward(): pl.pallas_call(forward_kernel, grid=(blocks,), in_specs=[rows(WIDTH), row...  28.7 us
    sub x3, other arithmetic, adam(): return (param - rate * (update + decay * param), new_first, new_second)  11.5 us

profile of v6, /device:TPU:0, one launch (start us, length us, event | category | flops | bytes accessed | tf_op | source)
XLA Modules:
  0.0 212.0 jit_solution(3042758809363079066)
XLA Ops:
  0.6 1.3 pad_bitcast_fusion.vec_ref
  2.0 44.6 %gather_project.1 = (f32[1024,3584]{1,0:T(8,128)}, f32[1024,1536]{1,0:T(8,128)}, bf16[1024,768]{1,0:T(8,128)(2,1)}, bf16[768,3584]{1,0:T(8,128)(2,1)}, bf16[1536,768]{1,0:T(8,128)(2,1)}, /*index=5*/f32[16,1792]{1,0:T(8,128)}) custom-call(bf16[1024,768]{1,0:T(8,128)(2,1)} %bitcast.13, bf16[1024,768]{1,0:T(8,128)(2,1)} %bitcast.10, f32[192,3352]{1,0:T(8,128)} %win_hbm.1, ...), custom_call_target="tpu_custom_call" | custom-call | tf_op jit(solution)/shard_map/gather_project/pallas_call | solution.py:1253
  46.6 0.1 add_add_fusion
  46.7 2.3 %fusion.es_ref = bf16[12,512,128]{2,1,0:T(8,128)(2,1)} fusion(s32[12,512]{1,0:T(8,128)S(1)} %add_add_fusion), kind=kLoop, calls=%fused_computation.2 | loop fusion | flops 1572864 | bytes 1597440 | tf_op jit(solution)/shard_map/convert_element_type | solution.py:614
  49.0 28.7 %mix_forward.1 = (bf16[1024,1536]{1,0:T(8,128)(2,1)}, bf16[1024,1536]{1,0:T(8,128)(2,1)}, bf16[1024,1536]{1,0:T(8,128)(2,1)}, bf16[8,128,1536]{2,1,0:T(8,128)(2,...) custom-call(f32[1024,3584]{1,0:T(8,128)} %get-tuple-element.40.proj_ref.prev_ref, ...), custom_call_target="tpu_custom_call" | custom-call | tf_op jit(solution)/shard_map/mix_forward/pallas_call | solution.py:628
  77.7 67.2 %mix_backward.1 = (bf16[1024,2048]{1,0:T(8,128)(2,1)}, f32[4,8,1792]{2,1,0:T(8,128)}, f32[8,1792]{1,0:T(8,128)}, f32[2,8,128]{2,1,0:T(8,128)}, f32[8,1536]{1,0:T...) custom-call(f32[1024,3584]{1,0:T(8,128)} %get-tuple-element.40.proj_ref.prev_ref, ...), custom_call_target="tpu_custom_call" | custom-call | tf_op jit(solution)/shard_map/mix_backward/pallas_call | solution.py:669
  144.9 0.0 copy-start.6
  144.9 0.0 copy-start.7
  144.9 0.0 copy-start.8
  144.9 50.0 %reduce_grads.1 = (bf16[192,3584]{1,0:T(8,128)(2,1)}, f32[1024,768]{1,0:T(8,128)}, bf16[1024,768]{1,0:T(8,128)(2,1)}, f32[8,128]{1,0:T(8,128)}) custom-call(bf16[1024,768]{1,0:T(8,128)(2,1)} %get-tuple-element.39.normed_hbm, bf16[1024,768]{1,0:T(8,128)(2,1)} %bitcast.12, bf16[1024,1536]{1,0:T(8,128)(2,1)} %get-tuple-element.43.mixer_hbm, ...), custom_call_target="tpu_custom_call" | custom-call | tf_op jit(solution)/shard_map/reduce_grads/pallas_call | solution.py:972
  194.9 0.7 slice_bitcast_fusion
  195.6 0.7 slice_bitcast_fusion.1
  196.3 0.0 copy-done.6
  196.3 0.0 copy-done.7
  196.3 0.0 copy-done.8
  196.3 0.7 multiply_subtract_fusion.2
  197.0 0.0 copy-start
  197.1 0.0 copy-start.3
  197.1 0.0 copy-start.4
  197.1 0.0 copy-start.5
  197.1 8.4 %multiply_subtract_fusion = (f32[192,3352]{1,0:T(8,128)}, f32[192,3352]{1,0:T(8,128)}, f32[192,3352]{1,0:T(8,128)}, f32[192,3352]{1,0:T(8,128)}) fusion(f32[192,3352]{1,0:T(8,128)} %win_hbm.1, f32[192,3352]{1,0:T(8,128)} %param.16, f32[192,3352]{1,0:T(8,128)} %param.17, bf16[192,3584]{1,0:T(8,128)(2,1)} %get-tuple-element.61), kind=kLoop, calls=%fused_computation.4 | loop fusion | flops 10297344 | bytes 19307520 | tf_op jit(solution)/shard_map/sub | solution.py:1301
  205.4 0.0 copy-done
  205.4 0.0 copy-done.3
  205.4 0.0 copy-done.4
  205.4 0.0 copy-done.5
  205.5 0.0 copy-start.2
  205.5 2.4 %multiply_subtract_fusion.1 = (f32[384,768]{1,0:T(8,128)}, f32[384,768]{1,0:T(8,128)}, f32[384,768]{1,0:T(8,128)}, f32[384,768]{1,0:T(8,128)}) fusion(f32[384,768]{1,0:T(8,128)S(1)} %copy-done, f32[384,768]{1,0:T(8,128)S(1)} %copy-done.3, f32[384,768]{1,0:T(8,128)S(1)} %copy-done.4, bf16[384,768]{1,0:T(8,128)(2,1)S(1)} %copy-done.5), kind=kLoop, calls=%fused_computation.9 | loop fusion | flops 4718592 | bytes 8847360 | tf_op jit(solution)/shard_map/sub | solution.py:1301
  207.9 0.0 copy-start.1
  207.9 0.0 copy-done.2
  207.9 1.1 copy.27
  209.0 1.3 copy-done.1
  210.4 1.7 copy.28
  (2 shorter events, 0.0 us)
Async XLA Ops:
  144.9 51.5 %copy-start.6 = (f32[2834]{0:T(1024)S(1)}, f32[2834]{0:T(1024)}, u32[]{:S(2)}) copy-start(f32[2834]{0:T(1024)} %param.15) | copy-start | bytes 34012
  144.9 51.5 %copy-start.7 = (f32[2834]{0:T(1024)S(1)}, f32[2834]{0:T(1024)}, u32[]{:S(2)}) copy-start(f32[2834]{0:T(1024)} %param.20) | copy-start | bytes 34012
  144.9 51.4 %copy-start.8 = (f32[2834]{0:T(1024)S(1)}, f32[2834]{0:T(1024)}, u32[]{:S(2)}) copy-start(f32[2834]{0:T(1024)} %param.21) | copy-start | bytes 34012
  197.0 8.4 %copy-start = (f32[384,768]{1,0:T(8,128)S(1)}, f32[384,768]{1,0:T(8,128)}, u32[]{:S(2)}) copy-start(f32[384,768]{1,0:T(8,128)} %wout_hbm.1) | copy-start | bytes 3538948
  197.1 8.4 %copy-start.3 = (f32[384,768]{1,0:T(8,128)S(1)}, f32[384,768]{1,0:T(8,128)}, u32[]{:S(2)}) copy-start(f32[384,768]{1,0:T(8,128)} %param.18) | copy-start | bytes 3538948
  197.1 8.4 %copy-start.4 = (f32[384,768]{1,0:T(8,128)S(1)}, f32[384,768]{1,0:T(8,128)}, u32[]{:S(2)}) copy-start(f32[384,768]{1,0:T(8,128)} %param.19) | copy-start | bytes 3538948
  197.1 8.4 %copy-start.5 = (bf16[384,768]{1,0:T(8,128)(2,1)S(1)}, bf16[384,768]{1,0:T(8,128)(2,1)}, u32[]{:S(2)}) copy-start(bf16[384,768]{1,0:T(8,128)(2,1)} %get-tuple-element.62) | copy-start | bytes 1769476
  205.5 2.4 %copy-start.2 = (bf16[1024,768]{1,0:T(8,128)(2,1)S(1)}, bf16[1024,768]{1,0:T(8,128)(2,1)}, u32[]{:S(2)}) copy-start(bf16[1024,768]{1,0:T(8,128)(2,1)} %get-tuple-element.59) | copy-start | bytes 4718596
  207.9 2.5 %copy-start.1 = (f32[1024,768]{1,0:T(8,128)S(1)}, f32[1024,768]{1,0:T(8,128)}, u32[]{:S(2)}) copy-start(f32[1024,768]{1,0:T(8,128)} %get-tuple-element.60) | copy-start | bytes 9437188

commit v7 on v6

--- a/solution.py
+++ b/solution.py
@@ -935,7 +935,7 @@
         def _():
             cover_out(i - OUT_SLOT)
 
-        for n in STAGE_ORDER:
+        for n in (0, 1, 2, 3, 4, 5):
             p = i - LATE_TICKS[n]
 
             @pl.when((p >= 0) & (p < LATE))

time: 212 us -> 210 us (level)
  Pallas kernels: 191 us -> 188 us
    pallas_call x1, Pallas kernels: 50 us -> 47.9 us  [reduce_grads(): pl.pallas_call(functools.partial(reduce_kernel, far, vec_len), in_specs=[...]
where the time goes in v7:
time: 210 us
  Pallas kernels  188 us (90%)
  other arithmetic  13.9 us (7%)
  local copies, waits for them, and re-layouts  6.85 us (3%)
    pallas_call x1, Pallas kernels, mix_backward(): pl.pallas_call(functools.partial(backward_kernel, far), grid=(blocks,), i...  67.2 us
    pallas_call x1, Pallas kernels, reduce_grads(): pl.pallas_call(functools.partial(reduce_kernel, far, vec_len), in_specs=[...  47.9 us
    pallas_call x1, Pallas kernels, gather_project(): pl.pallas_call(functools.partial(gather_kernel, vec_len), in_specs=[any_s...  44.6 us
    pallas_call x1, Pallas kernels, mix_forward(): pl.pallas_call(forward_kernel, grid=(blocks,), in_specs=[rows(WIDTH), row...  28.7 us
    sub x3, other arithmetic, adam(): return (param - rate * (update + decay * param), new_first, new_second)  11.5 us

profile of v7, /device:TPU:0, one launch (start us, length us, event | category | flops | bytes accessed | tf_op | source)
XLA Modules:
  0.0 209.9 jit_solution(1073284214961528606)
XLA Ops:
  0.6 1.3 pad_bitcast_fusion.vec_ref
  2.0 44.6 %gather_project.1 = (f32[1024,3584]{1,0:T(8,128)}, f32[1024,1536]{1,0:T(8,128)}, bf16[1024,768]{1,0:T(8,128)(2,1)}, bf16[768,3584]{1,0:T(8,128)(2,1)}, bf16[1536,768]{1,0:T(8,128)(2,1)}, /*index=5*/f32[16,1792]{1,0:T(8,128)}) custom-call(bf16[1024,768]{1,0:T(8,128)(2,1)} %bitcast.13, bf16[1024,768]{1,0:T(8,128)(2,1)} %bitcast.10, f32[192,3352]{1,0:T(8,128)} %win_hbm.1, ...), custom_call_target="tpu_custom_call" | custom-call | tf_op jit(solution)/shard_map/gather_project/pallas_call | solution.py:1253
  46.6 0.1 add_add_fusion
  46.7 2.3 %fusion.es_ref = bf16[12,512,128]{2,1,0:T(8,128)(2,1)} fusion(s32[12,512]{1,0:T(8,128)S(1)} %add_add_fusion), kind=kLoop, calls=%fused_computation.2 | loop fusion | flops 1572864 | bytes 1597440 | tf_op jit(solution)/shard_map/convert_element_type | solution.py:614
  49.0 28.7 %mix_forward.1 = (bf16[1024,1536]{1,0:T(8,128)(2,1)}, bf16[1024,1536]{1,0:T(8,128)(2,1)}, bf16[1024,1536]{1,0:T(8,128)(2,1)}, bf16[8,128,1536]{2,1,0:T(8,128)(2,...) custom-call(f32[1024,3584]{1,0:T(8,128)} %get-tuple-element.40.proj_ref.prev_ref, ...), custom_call_target="tpu_custom_call" | custom-call | tf_op jit(solution)/shard_map/mix_forward/pallas_call | solution.py:628
  77.7 67.2 %mix_backward.1 = (bf16[1024,2048]{1,0:T(8,128)(2,1)}, f32[4,8,1792]{2,1,0:T(8,128)}, f32[8,1792]{1,0:T(8,128)}, f32[2,8,128]{2,1,0:T(8,128)}, f32[8,1536]{1,0:T...) custom-call(f32[1024,3584]{1,0:T(8,128)} %get-tuple-element.40.proj_ref.prev_ref, ...), custom_call_target="tpu_custom_call" | custom-call | tf_op jit(solution)/shard_map/mix_backward/pallas_call | solution.py:669
  144.9 0.0 copy-start.6
  144.9 0.0 copy-start.7
  144.9 0.0 copy-start.8
  144.9 47.9 %reduce_grads.1 = (bf16[192,3584]{1,0:T(8,128)(2,1)}, f32[1024,768]{1,0:T(8,128)}, bf16[1024,768]{1,0:T(8,128)(2,1)}, f32[8,128]{1,0:T(8,128)}) custom-call(bf16[1024,768]{1,0:T(8,128)(2,1)} %get-tuple-element.39.normed_hbm, bf16[1024,768]{1,0:T(8,128)(2,1)} %bitcast.12, bf16[1024,1536]{1,0:T(8,128)(2,1)} %get-tuple-element.43.mixer_hbm, ...), custom_call_target="tpu_custom_call" | custom-call | tf_op jit(solution)/shard_map/reduce_grads/pallas_call | solution.py:972
  192.8 0.7 slice_bitcast_fusion
  193.5 0.7 slice_bitcast_fusion.1
  194.2 0.0 copy-done.6
  194.2 0.0 copy-done.7
  194.2 0.0 copy-done.8
  194.2 0.7 multiply_subtract_fusion.2
  194.9 0.0 copy-start
  194.9 0.0 copy-start.3
  194.9 0.0 copy-start.4
  194.9 0.0 copy-start.5
  194.9 8.4 %multiply_subtract_fusion = (f32[192,3352]{1,0:T(8,128)}, f32[192,3352]{1,0:T(8,128)}, f32[192,3352]{1,0:T(8,128)}, f32[192,3352]{1,0:T(8,128)}) fusion(f32[192,3352]{1,0:T(8,128)} %win_hbm.1, f32[192,3352]{1,0:T(8,128)} %param.16, f32[192,3352]{1,0:T(8,128)} %param.17, bf16[192,3584]{1,0:T(8,128)(2,1)} %get-tuple-element.61), kind=kLoop, calls=%fused_computation.4 | loop fusion | flops 10297344 | bytes 19307520 | tf_op jit(solution)/shard_map/sub | solution.py:1301
  203.3 0.0 copy-done
  203.3 0.0 copy-done.3
  203.3 0.0 copy-done.4
  203.3 0.0 copy-done.5
  203.3 0.0 copy-start.2
  203.3 2.4 %multiply_subtract_fusion.1 = (f32[384,768]{1,0:T(8,128)}, f32[384,768]{1,0:T(8,128)}, f32[384,768]{1,0:T(8,128)}, f32[384,768]{1,0:T(8,128)}) fusion(f32[384,768]{1,0:T(8,128)S(1)} %copy-done, f32[384,768]{1,0:T(8,128)S(1)} %copy-done.3, f32[384,768]{1,0:T(8,128)S(1)} %copy-done.4, bf16[384,768]{1,0:T(8,128)(2,1)S(1)} %copy-done.5), kind=kLoop, calls=%fused_computation.9 | loop fusion | flops 4718592 | bytes 8847360 | tf_op jit(solution)/shard_map/sub | solution.py:1301
  205.7 0.0 copy-start.1
  205.7 0.0 copy-done.2
  205.7 1.1 copy.27
  206.9 1.3 copy-done.1
  208.2 1.7 copy.28
  (2 shorter events, 0.0 us)
Async XLA Ops:
  144.9 49.3 %copy-start.6 = (f32[2834]{0:T(1024)S(1)}, f32[2834]{0:T(1024)}, u32[]{:S(2)}) copy-start(f32[2834]{0:T(1024)} %param.15) | copy-start | bytes 34012
  144.9 49.3 %copy-start.7 = (f32[2834]{0:T(1024)S(1)}, f32[2834]{0:T(1024)}, u32[]{:S(2)}) copy-start(f32[2834]{0:T(1024)} %param.20) | copy-start | bytes 34012
  144.9 49.3 %copy-start.8 = (f32[2834]{0:T(1024)S(1)}, f32[2834]{0:T(1024)}, u32[]{:S(2)}) copy-start(f32[2834]{0:T(1024)} %param.21) | copy-start | bytes 34012
  194.9 8.4 %copy-start = (f32[384,768]{1,0:T(8,128)S(1)}, f32[384,768]{1,0:T(8,128)}, u32[]{:S(2)}) copy-start(f32[384,768]{1,0:T(8,128)} %wout_hbm.1) | copy-start | bytes 3538948
  194.9 8.4 %copy-start.3 = (f32[384,768]{1,0:T(8,128)S(1)}, f32[384,768]{1,0:T(8,128)}, u32[]{:S(2)}) copy-start(f32[384,768]{1,0:T(8,128)} %param.18) | copy-start | bytes 3538948
  194.9 8.4 %copy-start.4 = (f32[384,768]{1,0:T(8,128)S(1)}, f32[384,768]{1,0:T(8,128)}, u32[]{:S(2)}) copy-start(f32[384,768]{1,0:T(8,128)} %param.19) | copy-start | bytes 3538948
  194.9 8.4 %copy-start.5 = (bf16[384,768]{1,0:T(8,128)(2,1)S(1)}, bf16[384,768]{1,0:T(8,128)(2,1)}, u32[]{:S(2)}) copy-start(bf16[384,768]{1,0:T(8,128)(2,1)} %get-tuple-element.62) | copy-start | bytes 1769476
  203.3 2.4 %copy-start.2 = (bf16[1024,768]{1,0:T(8,128)(2,1)S(1)}, bf16[1024,768]{1,0:T(8,128)(2,1)}, u32[]{:S(2)}) copy-start(bf16[1024,768]{1,0:T(8,128)(2,1)} %get-tuple-element.59) | copy-start | bytes 4718596
  205.7 2.5 %copy-start.1 = (f32[1024,768]{1,0:T(8,128)S(1)}, f32[1024,768]{1,0:T(8,128)}, u32[]{:S(2)}) copy-start(f32[1024,768]{1,0:T(8,128)} %get-tuple-element.60) | copy-start | bytes 9437188
